TPU v7x, 32 devices: a whole 2x2x4 slice. The times are simulated.
32 devices in a mesh: fsdp: 8 (over z, x), dp: 4 (over y, core).
Axes of the slice: x: 2, y: 2, z: 4, core: 2. Of those that a mesh axis runs over, the one named last changes fastest.
Arguments:
- tokens: bfloat16 [4, 4096, 1024], P('dp', 'fsdp'), may hold values from -6 to 6
- cotangent: bfloat16 [4, 4096, 1024], P('dp', 'fsdp'), may hold values from -6 to 6
- lengths: int32 [4, 32], P('dp'), may hold values from 8 to 248, as said below
- dealing: int32 [4, 32], P('dp'), may hold values from 0 to 31, as said below
- gain_mix: bfloat16 [1024], P('fsdp'), may hold values from 0.099609375 to 1.8984375
- w_qkv: bfloat16 [1024, 4096], P('fsdp'), may hold values from -0.1875 to 0.1875
- w_gates: bfloat16 [1024, 16], P('fsdp'), may hold values from -0.1875 to 0.1875
- w_outgate: bfloat16 [1024, 2048], P('fsdp'), may hold values from -0.1875 to 0.1875
- conv_weight: bfloat16 [4096, 4], P('fsdp'), may hold values from -3 to 3
- a_log: float32 [8], replicated, may hold values from -6 to -2
- dt_bias: float32 [8], replicated, may hold values from -2 to 2
- out_norm_gain: float32 [256], replicated, may hold values from 0.1 to 1.9
- w_out: bfloat16 [2048, 1024], P('fsdp'), may hold values from -0.125 to 0.125
- gain_ffn: bfloat16 [1024], P('fsdp'), may hold values from 0.099609375 to 1.8984375
- w_gate: bfloat16 [1024, 2816], P('fsdp'), may hold values from -0.1875 to 0.1875
- w_up: bfloat16 [1024, 2816], P('fsdp'), may hold values from -0.1875 to 0.1875
- w_down: bfloat16 [2816, 1024], P('fsdp'), may hold values from -0.109375 to 0.109375
Outputs:
- output: bfloat16 [4, 4096, 1024], P('dp', 'fsdp')
- input_grad: bfloat16 [4, 4096, 1024], P('dp', 'fsdp')
- grad_gain_mix: float32 [1024], P('fsdp')
- grad_qkv: float32 [1024, 4096], P('fsdp')
- grad_gates: float32 [1024, 16], P('fsdp')
- grad_outgate: float32 [1024, 2048], P('fsdp')
- grad_conv: float32 [4096, 4], P('fsdp')
- grad_a_log: float32 [8], replicated
- grad_dt_bias: float32 [8], replicated
- grad_out_norm: float32 [256], replicated
- grad_out: float32 [2048, 1024], P('fsdp')
- grad_gain_ffn: float32 [1024], P('fsdp')
- grad_gate: float32 [1024, 2816], P('fsdp')
- grad_up: float32 [1024, 2816], P('fsdp')
- grad_down: float32 [2816, 1024], P('fsdp')
Inputs may be any that keep to these rules, and one draw needn't show every extreme that they name: Every length is a multiple of 8, and the 2 sequences dealt to one slot group (one device and micro-batch) have lengths that sum to 256. In each replica a permutation of 0 to 31: sequence k of the given order goes to slot p = dealing[k], that is to fsdp device p // 4, micro-batch (p // 2) % 2, place p % 2 there.
All inputs are finite; a program needn't handle non-finite values.
Results may differ from a plain program's by a relative error of at most 0.014.
Values may be sent and summed in bfloat16 or wider, within the bound.
No kernel may reach another device: no remote copies, remote signals or barrier semaphores. Data moves between devices by JAX's collectives and lax.ppermute only.
A program may use at most 384 MiB of HBM per device.

v0:
```python
from functools import partial

import jax
import jax.numpy as jnp
from jax import lax
from jax.sharding import PartitionSpec as P

H = 8
DK = 128
DV = 256
SPAN = 64
MB_TOK = 256
MICRO = 2
SEQ_MB = 2


norm_eps = 1e-05
unit_eps = 1e-06
highest = lax.Precision.HIGHEST


def for_sending(shard):

    def short(part):
        return part.astype(jnp.bfloat16) if part.dtype == jnp.float32 else part

    return jax.tree.map(short, shard)


def rms_scale(values, gain):
    return values * lax.rsqrt(jnp.mean(values * values, axis=-1, keepdims=True) + norm_eps) * gain


def causal_conv(signal, weight, position):
    taps = weight.shape[1]
    rows = signal.shape[0]
    padded = jnp.concatenate([jnp.zeros((taps - 1, signal.shape[1]), signal.dtype), signal], axis=0)
    total = jnp.zeros_like(signal)
    for offset in range(taps):
        delay = taps - 1 - offset
        shifted = padded[offset : offset + rows]
        total = total + jnp.where((position >= delay)[:, None], shifted, 0.0) * weight[:, offset]
    return total


def mixer_inputs(projected, gate_in, conv_weight, a_log, dt_bias, position):
    rows = projected.shape[0]
    mixed = jax.nn.silu(causal_conv(projected, conv_weight, position))
    queries = mixed[:, : H * DK].reshape(rows, H, DK)
    keys = mixed[:, H * DK : 2 * H * DK].reshape(rows, H, DK)
    values = mixed[:, 2 * H * DK :].reshape(rows, H, DV)
    queries = (
        queries
        * lax.rsqrt(jnp.sum(queries * queries, axis=-1, keepdims=True) + unit_eps)
        * DK ** (-0.5)
    )
    keys = keys * lax.rsqrt(jnp.sum(keys * keys, axis=-1, keepdims=True) + unit_eps)
    decay = -jnp.exp(a_log) * jax.nn.softplus(gate_in[:, :H] + dt_bias)
    strength = jax.nn.sigmoid(gate_in[:, H:])
    return (queries, keys, values, decay, strength)


def output_norm(heads_out, out_gate, out_gain):
    rows = heads_out.shape[0]
    scaled = (
        heads_out
        * lax.rsqrt(jnp.mean(heads_out * heads_out, axis=-1, keepdims=True) + norm_eps)
        * out_gain
    )
    return scaled.reshape(rows, H * DV) * jax.nn.silu(out_gate)


def delta_spans(queries, keys, values, decay, strength, segment):
    rows = queries.shape[0]
    count = rows // SPAN

    def heads_first(array):
        return jnp.swapaxes(array.reshape((count, SPAN) + array.shape[1:]), 1, 2)

    stacked = (
        heads_first(queries),
        heads_first(keys),
        heads_first(values),
        heads_first(decay),
        heads_first(strength),
        segment.reshape(count, SPAN),
    )
    index = jnp.arange(SPAN)
    lower = index[:, None] >= index[None, :]
    strict = index[:, None] > index[None, :]
    identity = jnp.eye(SPAN, dtype=jnp.float32)

    def one_span(carry, inputs):
        state, before = carry
        query, key, value, rate, beta, label = inputs
        same = label[:, None] == label[None, :]
        total = jnp.cumsum(rate, axis=1)
        spread = jnp.where(lower, total[:, :, None] - total[:, None, :], 0.0)
        within = jnp.where(lower & same, jnp.exp(spread), 0.0)
        carried = jnp.where(label[None, :] == before, jnp.exp(total), 0.0)
        key_key = jnp.einsum("hid,hjd->hij", key, key, precision=highest)
        system = identity + jnp.where(strict, within * key_key * beta[:, None, :], 0.0)
        target = value - carried[:, :, None] * jnp.einsum(
            "hid,hde->hie", key, state, precision=highest
        )
        pseudo = jax.scipy.linalg.solve_triangular(system, target, lower=True, unit_diagonal=True)
        query_key = jnp.einsum("hid,hjd->hij", query, key, precision=highest)
        output = carried[:, :, None] * jnp.einsum("hid,hde->hie", query, state, precision=highest)
        output = output + jnp.einsum(
            "hij,hje->hie", within * query_key * beta[:, None, :], pseudo, precision=highest
        )
        last = label[SPAN - 1]
        tail = jnp.where(label[None, :] == last, jnp.exp(total[:, SPAN - 1 :] - total), 0.0) * beta
        keep = jnp.where(last == before, jnp.exp(total[:, SPAN - 1]), 0.0)
        state = keep[:, None, None] * state + jnp.einsum(
            "hj,hjd,hje->hde", tail, key, pseudo, precision=highest
        )
        return ((state, last), output)

    start = (jnp.zeros((H, DK, DV), jnp.float32), jnp.array(-1, jnp.int32))
    final, outputs = lax.scan(one_span, start, stacked)
    return jnp.swapaxes(outputs, 1, 2).reshape(rows, H, DV)


def mixer_local(
    position, segment, projected, gate_in, out_gate, conv_weight, a_log, dt_bias, out_gain
):
    queries, keys, values, decay, strength = mixer_inputs(
        projected, gate_in, conv_weight, a_log, dt_bias, position
    )
    return output_norm(
        delta_spans(queries, keys, values, decay, strength, segment), out_gate, out_gain
    )


def swiglu(gate_act, up_act):
    return jax.nn.silu(gate_act) * up_act


def gram_rows(left, right):
    return lax.dot_general(
        left, right, (((0,), (0,)), ((), ())), preferred_element_type=jnp.float32
    )


def times_transposed(left, right):
    return lax.dot_general(
        left, right, (((1,), (1,)), ((), ())), preferred_element_type=jnp.float32
    )


def local(
    tokens,
    cotangent,
    lengths,
    dealing,
    gain_mix,
    w_qkv,
    w_gates,
    w_outgate,
    conv_weight,
    a_log,
    dt_bias,
    out_norm_gain,
    w_out,
    gain_ffn,
    w_gate,
    w_up,
    w_down,
):
    parts = lax.axis_size("fsdp")
    own_index = lax.axis_index("fsdp")
    share = MB_TOK // parts
    width = tokens.shape[2]
    given_x = tokens[0]
    given_cot = cotangent[0]
    seq_len = lengths[0]
    dealt_slot = dealing[0]
    count = seq_len.shape[0]
    order = jnp.arange(count, dtype=jnp.int32)
    holder = jnp.sum(jnp.where(dealt_slot[None, :] == order[:, None], order[None, :], 0), axis=1)
    piece = seq_len // parts
    begin_given = jnp.cumsum(piece) - piece
    slot_len = seq_len[holder].reshape(parts, MICRO, SEQ_MB)
    slot_piece = slot_len // parts
    slot_given = begin_given[holder].reshape(parts, MICRO, SEQ_MB)
    slot_row = jnp.arange(share, dtype=jnp.int32)
    source = jnp.arange(parts, dtype=jnp.int32)
    place = jnp.arange(MB_TOK, dtype=jnp.int32)
    labels = jnp.arange(SEQ_MB, dtype=jnp.int32)
    shards = (
        gain_mix,
        w_qkv,
        w_gates,
        w_outgate,
        conv_weight,
        w_out,
        gain_ffn,
        w_gate,
        w_up,
        w_down,
    )
    back_shards = (gain_mix, w_qkv, w_gates, w_outgate, w_out, gain_ffn, w_gate, w_up, w_down)
    totals = tuple(
        (jnp.zeros((item.shape[0] * parts,) + item.shape[1:], jnp.float32) for item in shards)
    )
    small_totals = (jnp.zeros_like(a_log), jnp.zeros_like(dt_bias), jnp.zeros_like(out_norm_gain))
    sent_rows = []
    outs_back = []
    grads_back = []
    for micro in range(MICRO):
        pieces_now = slot_piece[:, micro, :]
        first = jnp.cumsum(pieces_now, axis=1) - pieces_now
        inside = (slot_row[None, :, None] >= first[:, None, :]) & (
            slot_row[None, :, None] < (first + pieces_now)[:, None, :]
        )
        rows_send = jnp.sum(
            jnp.where(
                inside,
                slot_given[:, micro, None, :] + slot_row[None, :, None] - first[:, None, :],
                0,
            ),
            axis=2,
        )
        own_len = lax.dynamic_index_in_dim(slot_len[:, micro, :], own_index, 0, keepdims=False)
        own_piece = own_len // parts
        own_first = jnp.cumsum(own_piece) - own_piece
        own_start = jnp.cumsum(own_len) - own_len
        offset = place[:, None] - own_start[None, :]
        covered = (offset >= 0) & (offset < own_len[None, :])
        flat_row = (
            offset // own_piece[None, :] * share + own_first[None, :] + offset % own_piece[None, :]
        )
        arrange = jnp.sum(jnp.where(covered, flat_row, 0), axis=1)
        position = jnp.sum(jnp.where(covered, offset, 0), axis=1)
        segment = jnp.sum(jnp.where(covered, labels[None, :], 0), axis=1)
        within_share = (slot_row[:, None] >= own_first[None, :]) & (
            slot_row[:, None] < (own_first + own_piece)[None, :]
        )
        back_rows = jnp.sum(
            jnp.where(
                within_share[None],
                own_start[None, None, :]
                + source[:, None, None] * own_piece[None, None, :]
                + slot_row[None, :, None]
                - own_first[None, None, :],
                0,
            ),
            axis=2,
        )
        sent_rows.append(rows_send.reshape(-1))
        recv_x, recv_cot = (
            lax.all_to_all(given_x[rows_send], "fsdp", split_axis=0, concat_axis=0, tiled=True),
            lax.all_to_all(given_cot[rows_send], "fsdp", split_axis=0, concat_axis=0, tiled=True),
        )
        local_x = recv_x.reshape(parts * share, width)[arrange]
        local_cot = recv_cot.reshape(parts * share, width)[arrange]
        weights = (
            lax.all_gather(shards[0], "fsdp", axis=0, tiled=True),
            lax.all_gather(shards[1], "fsdp", axis=0, tiled=True),
            lax.all_gather(shards[2], "fsdp", axis=0, tiled=True),
            lax.all_gather(shards[3], "fsdp", axis=0, tiled=True),
            lax.all_gather(shards[4], "fsdp", axis=0, tiled=True),
            lax.all_gather(shards[5], "fsdp", axis=0, tiled=True),
            lax.all_gather(shards[6], "fsdp", axis=0, tiled=True),
            lax.all_gather(shards[7], "fsdp", axis=0, tiled=True),
            lax.all_gather(shards[8], "fsdp", axis=0, tiled=True),
            lax.all_gather(shards[9], "fsdp", axis=0, tiled=True),
        )
        inputs_f = local_x.astype(jnp.float32)
        normed_low = rms_scale(inputs_f, weights[0].astype(jnp.float32)).astype(jnp.bfloat16)
        projected = jnp.dot(normed_low, weights[1], preferred_element_type=jnp.float32)
        gate_in = jnp.dot(normed_low, weights[2], preferred_element_type=jnp.float32)
        out_gate = jnp.dot(normed_low, weights[3], preferred_element_type=jnp.float32)
        gated, mixer_back = jax.vjp(
            partial(mixer_local, position, segment),
            projected,
            gate_in,
            out_gate,
            weights[4].astype(jnp.float32),
            a_log,
            dt_bias,
            out_norm_gain,
        )
        gated_low = gated.astype(jnp.bfloat16)
        residual = inputs_f + jnp.dot(gated_low, weights[5], preferred_element_type=jnp.float32)
        ffn_low = rms_scale(residual, weights[6].astype(jnp.float32)).astype(jnp.bfloat16)
        gate_act = jnp.dot(ffn_low, weights[7], preferred_element_type=jnp.float32)
        up_act = jnp.dot(ffn_low, weights[8], preferred_element_type=jnp.float32)
        hidden, act_back = jax.vjp(swiglu, gate_act, up_act)
        hidden_low = hidden.astype(jnp.bfloat16)
        result = (
            residual + jnp.dot(hidden_low, weights[9], preferred_element_type=jnp.float32)
        ).astype(jnp.bfloat16)
        result_send = result[back_rows]
        outs_back.append(
            lax.all_to_all(result_send, "fsdp", split_axis=0, concat_axis=0, tiled=True)
        )
        back_weights = (
            lax.all_gather(back_shards[0], "fsdp", axis=0, tiled=True),
            lax.all_gather(back_shards[1], "fsdp", axis=0, tiled=True),
            lax.all_gather(back_shards[2], "fsdp", axis=0, tiled=True),
            lax.all_gather(back_shards[3], "fsdp", axis=0, tiled=True),
            lax.all_gather(back_shards[4], "fsdp", axis=0, tiled=True),
            lax.all_gather(back_shards[5], "fsdp", axis=0, tiled=True),
            lax.all_gather(back_shards[6], "fsdp", axis=0, tiled=True),
            lax.all_gather(back_shards[7], "fsdp", axis=0, tiled=True),
            lax.all_gather(back_shards[8], "fsdp", axis=0, tiled=True),
        )
        grad_down = gram_rows(hidden_low, local_cot)
        grad_hidden = times_transposed(local_cot, back_weights[8])
        grad_gate_act, grad_up_act = act_back(grad_hidden)
        gate_low = grad_gate_act.astype(jnp.bfloat16)
        up_low = grad_up_act.astype(jnp.bfloat16)
        grad_gate = gram_rows(ffn_low, gate_low)
        grad_up = gram_rows(ffn_low, up_low)
        grad_ffn_normed = times_transposed(gate_low, back_weights[6]) + times_transposed(
            up_low, back_weights[7]
        )
        ffn_back = jax.vjp(rms_scale, residual, back_weights[5].astype(jnp.float32))[1]
        grad_residual_part, grad_gain_ffn = ffn_back(grad_ffn_normed)
        grad_residual = local_cot.astype(jnp.float32) + grad_residual_part
        mix_low = grad_residual.astype(jnp.bfloat16)
        grad_out = gram_rows(gated_low, mix_low)
        grad_gated = times_transposed(mix_low, back_weights[4])
        (
            grad_projected,
            grad_gate_in,
            grad_out_gate,
            grad_conv,
            grad_a_log,
            grad_dt_bias,
            grad_out_gain,
        ) = mixer_back(grad_gated)
        projected_low = grad_projected.astype(jnp.bfloat16)
        gate_in_low = grad_gate_in.astype(jnp.bfloat16)
        out_gate_low = grad_out_gate.astype(jnp.bfloat16)
        grad_qkv = gram_rows(normed_low, projected_low)
        grad_gates = gram_rows(normed_low, gate_in_low)
        grad_outgate = gram_rows(normed_low, out_gate_low)
        grad_normed = (
            times_transposed(projected_low, back_weights[1])
            + times_transposed(gate_in_low, back_weights[2])
            + times_transposed(out_gate_low, back_weights[3])
        )
        mix_back = jax.vjp(rms_scale, inputs_f, back_weights[0].astype(jnp.float32))[1]
        grad_inputs_part, grad_gain_mix = mix_back(grad_normed)
        grad_inputs = (grad_residual + grad_inputs_part).astype(jnp.bfloat16)
        grad_send = grad_inputs[back_rows]
        grads_back.append(
            lax.all_to_all(grad_send, "fsdp", split_axis=0, concat_axis=0, tiled=True)
        )
        updates = (
            grad_gain_mix,
            grad_qkv,
            grad_gates,
            grad_outgate,
            grad_conv,
            grad_out,
            grad_gain_ffn,
            grad_gate,
            grad_up,
            grad_down,
        )
        totals = tuple((total + update for total, update in zip(totals, updates)))
        small_totals = (
            small_totals[0] + grad_a_log,
            small_totals[1] + grad_dt_bias,
            small_totals[2] + grad_out_gain,
        )
    summed = lax.psum_scatter(totals, "fsdp", scatter_dimension=0, tiled=True)
    summed = jax.tree.map(
        lambda part: part.astype(jnp.float32), lax.psum(for_sending(summed), "dp")
    )
    small = lax.psum((small_totals[0], small_totals[1], small_totals[2]), ("fsdp", "dp"))
    rows_all = jnp.concatenate(sent_rows)
    inverse = (
        jnp.zeros((MICRO * MB_TOK,), jnp.int32)
        .at[rows_all]
        .set(jnp.arange(MICRO * MB_TOK, dtype=jnp.int32))
    )
    output = jnp.concatenate([item.reshape(-1, width) for item in outs_back], axis=0)[inverse][None]
    input_grad = jnp.concatenate([item.reshape(-1, width) for item in grads_back], axis=0)[inverse][
        None
    ]
    return (
        output,
        input_grad,
        summed[0],
        summed[1],
        summed[2],
        summed[3],
        summed[4],
        small[0],
        small[1],
        small[2],
        summed[5],
        summed[6],
        summed[7],
        summed[8],
        summed[9],
    )


def solution(mesh):
    in_specs = (
        P("dp", "fsdp", None),
        P("dp", "fsdp", None),
        P("dp", None),
        P("dp", None),
        P("fsdp"),
        P("fsdp", None),
        P("fsdp", None),
        P("fsdp", None),
        P("fsdp", None),
        P(),
        P(),
        P(),
        P("fsdp", None),
        P("fsdp"),
        P("fsdp", None),
        P("fsdp", None),
        P("fsdp", None),
    )
    out_specs = (
        P("dp", "fsdp", None),
        P("dp", "fsdp", None),
        P("fsdp"),
        P("fsdp", None),
        P("fsdp", None),
        P("fsdp", None),
        P("fsdp", None),
        P(),
        P(),
        P(),
        P("fsdp", None),
        P("fsdp"),
        P("fsdp", None),
        P("fsdp", None),
        P("fsdp", None),
    )
    return jax.shard_map(local, mesh=mesh, in_specs=in_specs, out_specs=out_specs, check_vma=False)
```

profile of v0, /device:TPU:0, one launch (start us, length us, event | category | flops | bytes accessed | tf_op | source)
XLA Modules:
  0.0 2384.0 jit_solution(9279947183439470576)
XLA Ops:
  16.5 7.3 all-to-all-start.2
  28.6 23.4 all-to-all-done.2
  56.3 48.6 %all_gather.23 = bf16[4096,4]{0,1:T(4,128)(2,1)S(1)} all-gather(bf16[512,4]{0,1:T(4,128)(2,1)S(1)} %copy-done.194), channel_id=1, replica_groups=mesh['fsdp'=8,'dp'=4] {'fsdp'}, dimensions={0}, use_global_device_ids=true | all-gather | bytes 36864 | tf_op jit(solution)/shard_map/all_gather | solution.py:263
  108.8 19.0 all-gather
  129.0 16.5 all-gather.1
  146.2 26.2 %all_gather.21 = bf16[1024,16]{0,1:T(8,128)(2,1)S(1)} all-gather(bf16[128,16]{0,1:T(8,128)(2,1)S(1)} %copy-done.195), channel_id=1, replica_groups=mesh['fsdp'=8,'dp'=4] {'fsdp'}, dimensions={0}, use_global_device_ids=true | all-gather | bytes 36864 | tf_op jit(solution)/shard_map/all_gather | solution.py:261
  180.6 20.1 all-to-all-done.6
  200.7 7.7 all-to-all-start.4
  214.4 18.4 all-to-all-done.4
  239.8 11.7 all-gather.9.cloned.1.call-done
  251.5 8.0 fusion.463
  263.9 22.3 fusion.351
  325.3 264.4 %while.197 = (s32[]{:T(128)}, f32[8,128,256]{2,1,0:T(8,128)S(1)}, s32[]{:T(128)}, f32[4,8,64,256]{3,2,1,0:T(8,128)}, f32[4,8,64,64]{3,2,1,0:T(8,128)}, /*index=5...) while((s32[]{:T(128)}, f32[8,128,256]{2,1,0:T(8,128)S(1)}, ...), condition=%wide.region_30.35_spmd.clone.clone, body=%wide.region_28.34_spmd.clone.clone.sunk | while | flops 909119168 | bytes 18458524 | solution.py:121
  333.8 40.7 %custom-call.59 = f32[8,1,64,64]{2,3,1,0:T(8,128)} custom-call(f32[8,1,64,64]{3,2,1,0:T(8,128)} %add_bitcast_fusion.5), custom_call_target="InvertDiagBlocksLowerTriangular" | custom-call | tf_op jit(solution)/shard_map/jvp()/while/body/eval_jaxpr/jit(_solve_triangular)/vmap()/triangular_solve | solution.py:106
  399.7 40.7 %custom-call.59 = f32[8,1,64,64]{2,3,1,0:T(8,128)} custom-call(f32[8,1,64,64]{3,2,1,0:T(8,128)} %add_bitcast_fusion.5), custom_call_target="InvertDiagBlocksLowerTriangular" | custom-call | tf_op jit(solution)/shard_map/jvp()/while/body/eval_jaxpr/jit(_solve_triangular)/vmap()/triangular_solve | solution.py:106
  465.7 40.7 %custom-call.59 = f32[8,1,64,64]{2,3,1,0:T(8,128)} custom-call(f32[8,1,64,64]{3,2,1,0:T(8,128)} %add_bitcast_fusion.5), custom_call_target="InvertDiagBlocksLowerTriangular" | custom-call | tf_op jit(solution)/shard_map/jvp()/while/body/eval_jaxpr/jit(_solve_triangular)/vmap()/triangular_solve | solution.py:106
  531.7 40.7 %custom-call.59 = f32[8,1,64,64]{2,3,1,0:T(8,128)} custom-call(f32[8,1,64,64]{3,2,1,0:T(8,128)} %add_bitcast_fusion.5), custom_call_target="InvertDiagBlocksLowerTriangular" | custom-call | tf_op jit(solution)/shard_map/jvp()/while/body/eval_jaxpr/jit(_solve_triangular)/vmap()/triangular_solve | solution.py:106
  620.9 9.3 multiply_convert_fusion
  668.6 241.6 %while.196 = (s32[]{:T(128)}, f32[8,128,256]{2,1,0:T(8,128)S(1)}, s32[]{:T(128)}, f32[4,8,64,256]{3,2,1,0:T(8,128)}, f32[4,8,64,64]{3,2,1,0:T(8,128)}, /*index=5...) while((s32[]{:T(128)}, f32[8,128,256]{2,1,0:T(8,128)S(1)}, ...), condition=%wide.region_14.19_spmd.clone.clone, body=%wide.region_12.18_spmd.clone.clone.sunk | while | flops 909119168 | bytes 18330588 | solution.py:121
  676.2 40.0 %custom-call.58 = f32[8,1,64,64]{2,3,1,0:T(8,128)S(1)} custom-call(f32[8,1,64,64]{3,2,1,0:T(8,128)} %add_bitcast_fusion.4), custom_call_target="InvertDiagBlocksLowerTriangular" | custom-call | tf_op jit(solution)/shard_map/jvp()/while/body/eval_jaxpr/jit(_solve_triangular)/vmap()/triangular_solve | solution.py:106
  736.5 40.0 %custom-call.58 = f32[8,1,64,64]{2,3,1,0:T(8,128)S(1)} custom-call(f32[8,1,64,64]{3,2,1,0:T(8,128)} %add_bitcast_fusion.4), custom_call_target="InvertDiagBlocksLowerTriangular" | custom-call | tf_op jit(solution)/shard_map/jvp()/while/body/eval_jaxpr/jit(_solve_triangular)/vmap()/triangular_solve | solution.py:106
  796.8 40.0 %custom-call.58 = f32[8,1,64,64]{2,3,1,0:T(8,128)S(1)} custom-call(f32[8,1,64,64]{3,2,1,0:T(8,128)} %add_bitcast_fusion.4), custom_call_target="InvertDiagBlocksLowerTriangular" | custom-call | tf_op jit(solution)/shard_map/jvp()/while/body/eval_jaxpr/jit(_solve_triangular)/vmap()/triangular_solve | solution.py:106
  857.1 40.0 %custom-call.58 = f32[8,1,64,64]{2,3,1,0:T(8,128)S(1)} custom-call(f32[8,1,64,64]{3,2,1,0:T(8,128)} %add_bitcast_fusion.4), custom_call_target="InvertDiagBlocksLowerTriangular" | custom-call | tf_op jit(solution)/shard_map/jvp()/while/body/eval_jaxpr/jit(_solve_triangular)/vmap()/triangular_solve | solution.py:106
  953.2 7.5 multiply_reduce_fusion.9
  999.9 309.6 %while.194 = (s32[]{:T(128)}, f32[8,128,256]{2,1,0:T(8,128)S(1)}, f32[4,8,64,128]{3,1,2,0:T(8,128)}, f32[4,8,64,128]{3,1,2,0:T(8,128)}, f32[4,8,64,256]{3,2,1,0:...) while((s32[]{:T(128)}, f32[8,128,256]{2,1,0:T(8,128)S(1)}, ...), condition=%wide.region_47.53_spmd.clone, body=%wide.region_37.52_spmd.clone.sunk | while | flops 1842496000 | bytes 53597836 | solution.py:121
  1004.6 39.3 %custom-call.56 = f32[8,1,64,64]{2,3,1,0:T(8,128)S(1)} custom-call(f32[8,1,64,64]{3,2,1,0:T(8,128)S(1)} %fusion.703), custom_call_target="InvertDiagBlocksLowerTriangular" | custom-call | tf_op jit(solution)/shard_map/transpose(jvp())/while/body/eval_jaxpr/jit(_solve_triangular)/vmap()/triangular_solve | solution.py:106
  1082.0 39.3 %custom-call.56 = f32[8,1,64,64]{2,3,1,0:T(8,128)S(1)} custom-call(f32[8,1,64,64]{3,2,1,0:T(8,128)S(1)} %fusion.703), custom_call_target="InvertDiagBlocksLowerTriangular" | custom-call | tf_op jit(solution)/shard_map/transpose(jvp())/while/body/eval_jaxpr/jit(_solve_triangular)/vmap()/triangular_solve | solution.py:106
  1159.4 39.3 %custom-call.56 = f32[8,1,64,64]{2,3,1,0:T(8,128)S(1)} custom-call(f32[8,1,64,64]{3,2,1,0:T(8,128)S(1)} %fusion.703), custom_call_target="InvertDiagBlocksLowerTriangular" | custom-call | tf_op jit(solution)/shard_map/transpose(jvp())/while/body/eval_jaxpr/jit(_solve_triangular)/vmap()/triangular_solve | solution.py:106
  1236.8 39.3 %custom-call.56 = f32[8,1,64,64]{2,3,1,0:T(8,128)S(1)} custom-call(f32[8,1,64,64]{3,2,1,0:T(8,128)S(1)} %fusion.703), custom_call_target="InvertDiagBlocksLowerTriangular" | custom-call | tf_op jit(solution)/shard_map/transpose(jvp())/while/body/eval_jaxpr/jit(_solve_triangular)/vmap()/triangular_solve | solution.py:106
  1332.2 298.5 %while.195 = (s32[]{:T(128)}, f32[8,128,256]{2,1,0:T(8,128)S(1)}, f32[4,8,64,128]{3,1,2,0:T(8,128)}, f32[4,8,64,128]{3,1,2,0:T(8,128)}, f32[4,8,64,256]{3,2,1,0:...) while((s32[]{:T(128)}, f32[8,128,256]{2,1,0:T(8,128)S(1)}, ...), condition=%wide.region_63.69_spmd.clone, body=%wide.region_53.68_spmd.clone.sunk | while | flops 1842496000 | bytes 51500676 | solution.py:121
  1337.2 39.3 %custom-call.57 = f32[8,1,64,64]{2,3,1,0:T(8,128)S(1)} custom-call(f32[8,1,64,64]{3,2,1,0:T(8,128)S(1)} %fusion.743), custom_call_target="InvertDiagBlocksLowerTriangular" | custom-call | tf_op jit(solution)/shard_map/transpose(jvp())/while/body/eval_jaxpr/jit(_solve_triangular)/vmap()/triangular_solve | solution.py:106
  1411.6 39.3 %custom-call.57 = f32[8,1,64,64]{2,3,1,0:T(8,128)S(1)} custom-call(f32[8,1,64,64]{3,2,1,0:T(8,128)S(1)} %fusion.743), custom_call_target="InvertDiagBlocksLowerTriangular" | custom-call | tf_op jit(solution)/shard_map/transpose(jvp())/while/body/eval_jaxpr/jit(_solve_triangular)/vmap()/triangular_solve | solution.py:106
  1486.2 39.3 %custom-call.57 = f32[8,1,64,64]{2,3,1,0:T(8,128)S(1)} custom-call(f32[8,1,64,64]{3,2,1,0:T(8,128)S(1)} %fusion.743), custom_call_target="InvertDiagBlocksLowerTriangular" | custom-call | tf_op jit(solution)/shard_map/transpose(jvp())/while/body/eval_jaxpr/jit(_solve_triangular)/vmap()/triangular_solve | solution.py:106
  1560.7 39.3 %custom-call.57 = f32[8,1,64,64]{2,3,1,0:T(8,128)S(1)} custom-call(f32[8,1,64,64]{3,2,1,0:T(8,128)S(1)} %fusion.743), custom_call_target="InvertDiagBlocksLowerTriangular" | custom-call | tf_op jit(solution)/shard_map/transpose(jvp())/while/body/eval_jaxpr/jit(_solve_triangular)/vmap()/triangular_solve | solution.py:106
  1651.9 7.5 multiply_reduce_fusion.7
  1659.5 6.3 multiply_reduce_fusion.3
  1665.8 11.8 multiply_select_fusion.3
  1677.6 9.6 fusion.349
  1687.2 6.8 fusion.348
  1698.3 10.1 convolution_add_fusion.20
  1738.3 23.0 all-to-all-done.5
  1775.3 79.8 %reduce-scatter.23.cloned.1.call-done = f32[352,1024]{1,0:T(8,128)} async-done(((f32[2816,1024]{1,0:T(8,128)}), f32[352,1024]{1,0:T(8,128)}) %reduce-scatter.23.cloned.1.call-update) | async-done | bytes 1441808 | tf_op jit(solution)/shard_map/reduce_scatter | solution.py:371
  1857.4 283.1 %reduce-scatter.11.cloned.1.call-done = f32[128,4096]{1,0:T(8,128)} async-done(((f32[1024,4096]{1,0:T(8,128)}), f32[128,4096]{1,0:T(8,128)}) %reduce-scatter.11.cloned.1.call-update) | async-done | bytes 2097168 | tf_op jit(solution)/shard_map/reduce_scatter | solution.py:371
  2162.9 18.7 all-to-all-done.1
  2188.5 41.7 %all-reduce.34 = (f32[8]{0:T(128)}, f32[8]{0:T(128)}, f32[256]{0:T(256)}) all-reduce(f32[8]{0:T(128)S(1)} %add_multiply_fusion, f32[8]{0:T(128)S(1)} %add.871, f32[256]{0:T(256)S(1)} %add.872), channel_id=1, replica_groups=mesh['fsdp'=8,'dp'=4] {'fsdp','dp'}, use_global_device_ids=true, to_apply=%region_89.95 | all-reduce | flops 272 | bytes 2176 | tf_op jit(solution)/shard_map/psum | solution.py:375
  2230.2 21.1 all-reduce.35
  2252.5 25.5 %reduce-scatter.13.cloned.1.call-done = f32[128,16]{0,1:T(8,128)} async-done(((f32[1024,16]{0,1:T(8,128)}), f32[128,16]{0,1:T(8,128)}) %reduce-scatter.13.cloned.1.call-update) | async-done | bytes 8208 | tf_op jit(solution)/shard_map/reduce_scatter | solution.py:371
  2293.6 74.9 %all-reduce.40.cloned.1.call-done = (bf16[128,4096]{1,0:T(8,128)(2,1)}, bf16[128,2048]{1,0:T(8,128)(2,1)}, bf16[256,1024]{1,0:T(8,128)(2,1)}, bf16[128,2816]{1,0...) async-done(((bf16[128,4096]{1,0:T(8,128)(2,1)}, bf16[128,2048]{1,0:T(8,128)(2,1)}, bf16[256,1024]{1,0:T(8,128)(2,1)}, bf16[128,2816]{1,0:T(8,128)(2,1)}, ...) | async-done | bytes 4259856 | tf_op jit(solution)/shard_map/psum | solution.py:373
  (1501 shorter events, 849.4 us)
Async XLA Ops:
  7.2 227.6 %all-gather.11.cloned.1.call-start = ((), (), s32[]{:S(2)}) async-start(), calls=%async_computation.17 | async-start | bytes 4718592 | tf_op jit(solution)/shard_map/all_gather | solution.py:262
  8.0 243.6 %all-gather.9.cloned.1.call-start = ((), (), s32[]{:S(2)}) async-start(), calls=%async_computation.16 | async-start | bytes 9437184 | tf_op jit(solution)/shard_map/all_gather | solution.py:260
  8.7 593.7 %all-gather.13.cloned.1.call-start = ((), (), s32[]{:S(2)}) async-start(), calls=%async_computation.18 | async-start | bytes 4718592 | tf_op jit(solution)/shard_map/all_gather | solution.py:264
  9.4 599.6 %all-gather.15.cloned.1.call-start = ((), (), s32[]{:S(2)}) async-start(), calls=%async_computation.19 | async-start | bytes 6488064 | tf_op jit(solution)/shard_map/all_gather | solution.py:266
  10.0 605.0 %all-gather.17.cloned.1.call-start = ((), (), s32[]{:S(2)}) async-start(), calls=%async_computation.20 | async-start | bytes 6488064 | tf_op jit(solution)/shard_map/all_gather | solution.py:267
  16.5 35.5 %all-to-all-start.2 = ((bf16[8,32,1024]{2,1,0:T(8,128)(2,1)}), bf16[8,32,1024]{2,1,0:T(8,128)(2,1)S(1)}, u32[]{:S(2)}, u32[]{:S(2)}) async-start(bf16[8,32,1024]{2,1,0:T(8,128)(2,1)} %bitcast.53), calls=%async_computation.2 | async-start | bytes 1048576 | tf_op jit(solution)/shard_map/all_to_all | solution.py:253
  23.8 597.1 %all-gather.19.cloned.1.call-start = ((), (), s32[]{:S(2)}) async-start(), calls=%async_computation.21 | async-start | bytes 6488064 | tf_op jit(solution)/shard_map/all_gather | solution.py:268
  26.6 78.3 %copy-start.9 = (bf16[1,512,1024]{2,1,0:T(8,128)(2,1)S(1)}, bf16[1,512,1024]{2,1,0:T(8,128)(2,1)}, u32[]{:S(2)}) copy-start(bf16[1,512,1024]{2,1,0:T(8,128)(2,1)} %param.37) | copy-start | bytes 3145732
  28.5 185.6 %copy-start.192 = (f32[8]{0:T(128)}, f32[8]{0:T(128)S(1)}, u32[]{:S(2)}) copy-start(f32[8]{0:T(128)S(1)} %exponential_negate_fusion) | copy-start | bytes 100
  28.6 235.3 %copy-start.174 = (pred[256]{0:T(512)(128)(4,1)}, pred[256]{0:T(512)(128)(4,1)S(1)}, u32[]{:S(2)}) copy-start(pred[256]{0:T(512)(128)(4,1)S(1)} %get-tuple-element.4785) | copy-start | bytes 772
  28.6 235.3 %copy-start.176 = (pred[256]{0:T(512)(128)(4,1)}, pred[256]{0:T(512)(128)(4,1)S(1)}, u32[]{:S(2)}) copy-start(pred[256]{0:T(512)(128)(4,1)S(1)} %get-tuple-element.4786) | copy-start | bytes 772
  28.6 235.3 %copy-start.178 = (pred[256]{0:T(512)(128)(4,1)}, pred[256]{0:T(512)(128)(4,1)S(1)}, u32[]{:S(2)}) copy-start(pred[256]{0:T(512)(128)(4,1)S(1)} %get-tuple-element.4787) | copy-start | bytes 772
  28.6 235.3 %copy-start.180 = (pred[256]{0:T(512)(128)(4,1)}, pred[256]{0:T(512)(128)(4,1)S(1)}, u32[]{:S(2)}) copy-start(pred[256]{0:T(512)(128)(4,1)S(1)} %get-tuple-element.4788) | copy-start | bytes 772
  52.1 120.4 %all-to-all-start = ((bf16[8,32,1024]{2,1,0:T(8,128)(2,1)}), bf16[8,32,1024]{2,1,0:T(8,128)(2,1)}, u32[]{:S(2)}, u32[]{:S(2)}) async-start(bf16[8,32,1024]{2,1,0:T(8,128)(2,1)} %bitcast.11), calls=%async_computation | async-start | bytes 1048576 | tf_op jit(solution)/shard_map/all_to_all | solution.py:253
  108.8 67.3 %copy-start.17 = (bf16[8,32,1024]{2,1,0:T(8,128)(2,1)S(1)}, bf16[8,32,1024]{2,1,0:T(8,128)(2,1)}, u32[]{:S(2)}) copy-start(bf16[8,32,1024]{2,1,0:T(8,128)(2,1)} %copy-done.16) | copy-start | bytes 1572868
  127.8 834.3 %copy-start.88 = (f32[8,1,128]{2,1,0:T(1,128)}, f32[8,1,128]{2,1,0:T(1,128)S(1)}, u32[]{:S(2)}) copy-start(f32[8,1,128]{2,1,0:T(1,128)S(1)} %convert_element_type.219) | copy-start | bytes 12292
  172.4 41.5 %copy-start.107 = (bf16[1024,16]{0,1:T(8,128)(2,1)}, bf16[1024,16]{0,1:T(8,128)(2,1)S(1)}, u32[]{:S(2)}) copy-start(bf16[1024,16]{0,1:T(8,128)(2,1)S(1)} %all_gather.21) | copy-start | bytes 98308
  172.4 91.5 %copy-start.113 = (f32[4096,1]{0,1:T(1,128)}, f32[4096,1]{0,1:T(1,128)S(1)}, u32[]{:S(2)}) copy-start(f32[4096,1]{0,1:T(1,128)S(1)} %get-tuple-element.4751) | copy-start | bytes 49156
  172.4 91.5 %copy-start.115 = (f32[4096,1]{0,1:T(1,128)}, f32[4096,1]{0,1:T(1,128)S(1)}, u32[]{:S(2)}) copy-start(f32[4096,1]{0,1:T(1,128)S(1)} %get-tuple-element.4752) | copy-start | bytes 49156
  172.4 91.5 %copy-start.117 = (f32[4096,1]{0,1:T(1,128)}, f32[4096,1]{0,1:T(1,128)S(1)}, u32[]{:S(2)}) copy-start(f32[4096,1]{0,1:T(1,128)S(1)} %get-tuple-element.4753) | copy-start | bytes 49156
  172.4 91.5 %copy-start.119 = (f32[4096,1]{0,1:T(1,128)}, f32[4096,1]{0,1:T(1,128)S(1)}, u32[]{:S(2)}) copy-start(f32[4096,1]{0,1:T(1,128)S(1)} %get-tuple-element.4754) | copy-start | bytes 49156
  172.5 28.2 %all-to-all-start.6 = ((bf16[8,32,1024]{2,1,0:T(8,128)(2,1)}), bf16[8,32,1024]{2,1,0:T(8,128)(2,1)S(1)}, u32[]{:S(2)}, u32[]{:S(2)}) async-start(bf16[8,32,1024]{2,1,0:T(8,128)(2,1)} %bitcast.1391), calls=%async_computation.6 | async-start | bytes 1048576 | tf_op jit(solution)/shard_map/all_to_all | solution.py:254
  176.0 87.9 %copy-start.182 = (pred[256]{0:T(512)(128)(4,1)}, pred[256]{0:T(512)(128)(4,1)S(1)}, u32[]{:S(2)}) copy-start(pred[256]{0:T(512)(128)(4,1)S(1)} %get-tuple-element.4789) | copy-start | bytes 772
  176.0 87.9 %copy-start.184 = (pred[256]{0:T(512)(128)(4,1)}, pred[256]{0:T(512)(128)(4,1)S(1)}, u32[]{:S(2)}) copy-start(pred[256]{0:T(512)(128)(4,1)S(1)} %get-tuple-element.4790) | copy-start | bytes 772
  176.0 87.9 %copy-start.186 = (pred[256]{0:T(512)(128)(4,1)}, pred[256]{0:T(512)(128)(4,1)S(1)}, u32[]{:S(2)}) copy-start(pred[256]{0:T(512)(128)(4,1)S(1)} %get-tuple-element.4791) | copy-start | bytes 772
  176.0 87.9 %copy-start.188 = (pred[256]{0:T(512)(128)(4,1)}, pred[256]{0:T(512)(128)(4,1)S(1)}, u32[]{:S(2)}) copy-start(pred[256]{0:T(512)(128)(4,1)S(1)} %get-tuple-element.4792) | copy-start | bytes 772
  179.3 72.2 %copy-start.150 = (f32[256]{0:T(256)}, f32[256]{0:T(256)S(1)}, u32[]{:S(2)}) copy-start(f32[256]{0:T(256)S(1)} %fusion.442) | copy-start | bytes 3076
  200.7 32.2 %all-to-all-start.4 = ((bf16[8,32,1024]{2,1,0:T(8,128)(2,1)}), bf16[8,32,1024]{2,1,0:T(8,128)(2,1)S(1)}, u32[]{:S(2)}, u32[]{:S(2)}) async-start(bf16[8,32,1024]{2,1,0:T(8,128)(2,1)} %bitcast.1390), calls=%async_computation.4 | async-start | bytes 1048576 | tf_op jit(solution)/shard_map/all_to_all | solution.py:254
  208.4 1558.1 %reduce-scatter.17.cloned.1.call-start = ((), (), s32[]{:S(2)}) async-start(), calls=%async_computation.25 | async-start | bytes 9437184 | tf_op jit(solution)/shard_map/reduce_scatter | solution.py:371
  213.6 45.9 %copy-start.27 = (bf16[256,1024]{1,0:T(8,128)(2,1)}, bf16[256,1024]{1,0:T(8,128)(2,1)S(1)}, u32[]{:S(2)}) copy-start(bf16[256,1024]{1,0:T(8,128)(2,1)S(1)} %gather_fusion.3) | copy-start | bytes 1572868
  213.8 45.6 %copy-start.141 = (f32[256]{0:T(256)}, f32[256]{0:T(256)S(1)}, u32[]{:S(2)}) copy-start(f32[256]{0:T(256)S(1)} %fusion.440) | copy-start | bytes 3076
  953.1 815.5 %reduce-scatter.15.cloned.1.call-start = ((), (), s32[]{:S(2)}) async-start(), calls=%async_computation.24 | async-start | bytes 9437184 | tf_op jit(solution)/shard_map/reduce_scatter | solution.py:371
  967.1 803.6 %reduce-scatter.21.cloned.1.call-start = ((), (), s32[]{:S(2)}) async-start(), calls=%async_computation.27 | async-start | bytes 12976128 | tf_op jit(solution)/shard_map/reduce_scatter | solution.py:371
  977.2 795.8 %reduce-scatter.19.cloned.1.call-start = ((), (), s32[]{:S(2)}) async-start(), calls=%async_computation.26 | async-start | bytes 12976128 | tf_op jit(solution)/shard_map/reduce_scatter | solution.py:371
  996.2 858.9 %reduce-scatter.23.cloned.1.call-start = ((), (), s32[]{:S(2)}) async-start(), calls=%async_computation.28 | async-start | bytes 12976128 | tf_op jit(solution)/shard_map/reduce_scatter | solution.py:371
  1328.5 812.0 %reduce-scatter.11.cloned.1.call-start = ((), (), s32[]{:S(2)}) async-start(), calls=%async_computation.22 | async-start | bytes 18874368 | tf_op jit(solution)/shard_map/reduce_scatter | solution.py:371
  1730.2 31.0 %all-to-all-start.5 = ((bf16[8,32,1024]{2,1,0:T(8,128)(2,1)}), bf16[8,32,1024]{2,1,0:T(8,128)(2,1)S(1)}, u32[]{:S(2)}, u32[]{:S(2)}) async-start(bf16[8,32,1024]{2,1,0:T(8,128)(2,1)} %bitcast.95), calls=%async_computation.5 | async-start | bytes 1048576 | tf_op jit(solution)/shard_map/all_to_all | solution.py:351
  1733.7 517.7 %reduce-scatter.25.cloned.1.call-start = ((), (), s32[]{:S(2)}) async-start(), calls=%async_computation.29 | async-start | bytes 2359296
  1761.2 390.0 %all-to-all-start.7 = ((bf16[8,32,1024]{2,1,0:T(8,128)(2,1)}), bf16[8,32,1024]{2,1,0:T(8,128)(2,1)}, u32[]{:S(2)}, u32[]{:S(2)}) async-start(bf16[8,32,1024]{2,1,0:T(8,128)(2,1)} %bitcast.107), calls=%async_computation.7 | async-start | bytes 1048576 | tf_op jit(solution)/shard_map/all_to_all | solution.py:351
  1765.4 512.6 %reduce-scatter.13.cloned.1.call-start = ((), (), s32[]{:S(2)}) async-start(), calls=%async_computation.23 | async-start | bytes 73728 | tf_op jit(solution)/shard_map/reduce_scatter | solution.py:371
  1766.4 602.1 %all-reduce.40.cloned.1.call-start = ((), (), s32[]{:S(2)}) async-start(), calls=%async_computation.30 | async-start | bytes 8519680 | tf_op jit(solution)/shard_map/psum | solution.py:373
  2151.2 30.5 %all-to-all-start.1 = ((bf16[8,32,1024]{2,1,0:T(8,128)(2,1)}), bf16[8,32,1024]{2,1,0:T(8,128)(2,1)S(1)}, u32[]{:S(2)}, u32[]{:S(2)}) async-start(bf16[8,32,1024]{2,1,0:T(8,128)(2,1)} %bitcast.1392), calls=%async_computation.1 | async-start | bytes 1048576 | tf_op jit(solution)/shard_map/all_to_all | solution.py:297
  2160.9 69.2 %copy-start.196 = (f32[1024]{0:T(1024)S(1)}, f32[1024]{0:T(1024)}, u32[]{:S(2)}) copy-start(f32[1024]{0:T(1024)} %get-tuple-element.4266) | copy-start | bytes 12292
  2160.9 69.2 %copy-start.197 = (f32[1024]{0:T(1024)S(1)}, f32[1024]{0:T(1024)}, u32[]{:S(2)}) copy-start(f32[1024]{0:T(1024)} %get-tuple-element.4268) | copy-start | bytes 12292
  2161.0 69.2 %copy-start.156 = (f32[1024]{0:T(1024)S(1)}, f32[1024]{0:T(1024)}, u32[]{:S(2)}) copy-start(f32[1024]{0:T(1024)} %get-tuple-element.4778) | copy-start | bytes 12292
  2161.0 125.8 %copy-start.76 = (bf16[8,32,1024]{2,1,0:T(8,128)(2,1)S(1)}, bf16[8,32,1024]{2,1,0:T(8,128)(2,1)}, u32[]{:S(2)}) copy-start(bf16[8,32,1024]{2,1,0:T(8,128)(2,1)} %copy-done.75) | copy-start | bytes 1572868
  2181.7 105.1 %copy-start.77 = (bf16[8,32,1024]{2,1,0:T(8,128)(2,1)}, bf16[8,32,1024]{2,1,0:T(8,128)(2,1)S(1)}, u32[]{:S(2)}) copy-start(bf16[8,32,1024]{2,1,0:T(8,128)(2,1)S(1)} %all-to-all-done.1) | copy-start | bytes 1572868
  2181.7 109.1 %all-to-all-start.3 = ((bf16[8,32,1024]{2,1,0:T(8,128)(2,1)}), bf16[8,32,1024]{2,1,0:T(8,128)(2,1)S(1)}, u32[]{:S(2)}, u32[]{:S(2)}) async-start(bf16[8,32,1024]{2,1,0:T(8,128)(2,1)} %bitcast.80), calls=%async_computation.3 | async-start | bytes 1048576 | tf_op jit(solution)/shard_map/all_to_all | solution.py:297
  (243 other events, 1539.0 us)
Sparse Core Ops, SparseCore 0:
  10.2 94.9 all-gather.10
  107.3 144.2 all-gather.8
  253.6 72.5 all-gather.12
  328.3 92.0 all-gather.14
  422.4 91.4 all-gather.16
  516.0 91.7 all-gather.18
  953.2 148.4 reduce-scatter.16
  1105.8 147.7 reduce-scatter.14
  1257.2 191.8 reduce-scatter.20
  1452.6 191.9 reduce-scatter.18
  1648.2 206.8 reduce-scatter.22
  1858.7 281.7 reduce-scatter.10
  2145.0 76.7 reduce-scatter.24
  2225.1 52.8 reduce-scatter.12
  2282.0 86.5 all-reduce.39
where the time goes:
time: 2400 us; the launch traced here: 2380 us
  other arithmetic  869 us (36%)
  waiting for transfers between devices  582 us (24%)
  matrix products  458 us (19%)
  local copies, waits for them, and re-layouts  225 us (9%)
  blocking collectives  179 us (7%)
  starting transfers between devices  39 us (2%)
    another operation x80, other arithmetic, one_span(): jax.scipy.linalg.solve_triangular(system, target, lower=True, unit_diagon...  654 us
    reduce_scatter x7, waiting for transfers between devices, local(): summed = lax.psum_scatter(totals, 'fsdp', scatter_dimension=0, tiled=True)  388 us
    psum x1, waiting for transfers between devices, local(): lax.psum(for_sending(summed), 'dp')  74.9 us
    dot_general x14, matrix products, times_transposed(): lax.dot_general(left, right, (((1,), (1,)), ((), ())), preferred_element_...  58.2 us
    dot_general x24, matrix products, one_span(): jnp.einsum('hid,hde->hie', query, state, precision=highest)  57.6 us
    dot_general x14, matrix products, gram_rows(): lax.dot_general(left, right, (((0,), (0,)), ((), ())), preferred_element_...  52.2 us
    another operation x62, local copies, waits for them, and re-layouts  52.2 us
    all_gather x1, blocking collectives, local(): lax.all_gather(shards[4], 'fsdp', axis=0, tiled=True)  48.6 us
  transfers between devices with their start and end apart: 23, of which 10 were waited for; matrix products, arithmetic and copies ran while one was open for 50% of the time, Pallas kernels for 0%

commit v1 on v0

v1 whole, which is shorter than its diff:
```python
from functools import partial

import jax
import jax.numpy as jnp
from jax import lax
from jax.experimental import pallas as pl
from jax.experimental.pallas import tpu as pltpu
from jax.sharding import PartitionSpec as P

H = 8
DK = 128
DV = 256
TAPS = 4
MB_TOK = 256
MICRO = 2
SEQ_MB = 2
ROWS = MB_TOK * MICRO

norm_eps = 1e-05
unit_eps = 1e-06
f32 = jnp.float32
bf16 = jnp.bfloat16
NN = (((1,), (0,)), ((), ()))
NT = (((1,), (1,)), ((), ()))
TN = (((0,), (0,)), ((), ()))


def mm(left, right, dims=NN):
    return lax.dot_general(
        left.astype(bf16), right.astype(bf16), dims, preferred_element_type=f32
    )


def halves(value):
    high = value.astype(bf16)
    return high, (value - high.astype(f32)).astype(bf16)


def mm_split(left, right, dims=NN):
    return mm(left[0], right[0], dims) + (mm(left[0], right[1], dims) + mm(left[1], right[0], dims))


def conv_taps(signal, weight, position):
    total = signal * weight[TAPS - 1 : TAPS]
    shifted = []
    for delay in range(1, TAPS):
        moved = jnp.where(position >= delay, pltpu.roll(signal, delay, 0), 0.0)
        shifted.append(moved)
        total = total + moved * weight[TAPS - 1 - delay : TAPS - delay]
    return total, shifted


def unit_rows(value):
    return lax.rsqrt(jnp.sum(value * value, axis=1, keepdims=True) + unit_eps)


def chain_masks(label_col, label_row):
    size = MB_TOK
    row = lax.broadcasted_iota(jnp.int32, (size, size), 0)
    col = lax.broadcasted_iota(jnp.int32, (size, size), 1)
    same = label_col == label_row
    return row, col, (row >= col) & same, (row > col) & same


def unit_lower_inverses(systems):
    row = lax.broadcasted_iota(jnp.int32, (MB_TOK, MB_TOK), 0)
    col = lax.broadcasted_iota(jnp.int32, (MB_TOK, MB_TOK), 1)
    apart = row ^ col
    eye = jnp.where(row == col, 1.0, 0.0)
    inverses = [eye - jnp.where(apart == 1, system, 0.0) for system in systems]
    lows = [system.astype(bf16) for system in systems]
    level = 1
    while (1 << level) < MB_TOK:
        now = (apart >> level) == 1
        pairs = [inverse.astype(bf16) for inverse in inverses]
        halfway = [mm(pair, jnp.where(now, low, 0)) for pair, low in zip(pairs, lows)]
        inverses = [
            inverse - mm(half, pair) for inverse, half, pair in zip(inverses, halfway, pairs)
        ]
        level += 1
    pairs = [halves(inverse) for inverse in inverses]
    rests = [
        eye - inverse - mm_split(halves(system), pair)
        for inverse, system, pair in zip(inverses, systems, pairs)
    ]
    return [inverse + mm(pair[0], rest) for inverse, pair, rest in zip(inverses, pairs, rests)]


def mixer_forward_kernel(
    pq, pk, pv, og, col, row, wq, wk, wv, gain, gated_ref, inverse_ref, pseudo_ref
):
    position = col[0, :, 3:4]
    query, key, value = (
        pre * jax.nn.sigmoid(pre)
        for pre in (
            conv_taps(pq[...], wq[...], position)[0],
            conv_taps(pk[...], wk[...], position)[0],
            conv_taps(pv[...], wv[...], position)[0],
        )
    )
    query = (query * (unit_rows(query) * DK ** (-0.5))).astype(bf16)
    key = (key * unit_rows(key)).astype(bf16)
    chains = [slice(chain * MB_TOK, (chain + 1) * MB_TOK) for chain in range(MICRO)]
    systems, attends = [], []
    for rows in chains:
        _, _, lower, strict = chain_masks(col[0, rows, 2:3], row[0, 2:3, rows])
        spread = jnp.where(lower, col[0, rows, 0:1] - row[0, 0:1, rows], 0.0)
        weight = jnp.exp(spread) * row[0, 1:2, rows]
        systems.append(jnp.where(strict, weight * mm(key[rows], key[rows], NT), 0.0))
        attends.append(jnp.where(lower, weight * mm(query[rows], key[rows], NT), 0.0).astype(bf16))
    inverses = unit_lower_inverses(systems)
    for rows, inverse, attend in zip(chains, inverses, attends):
        low = inverse.astype(bf16)
        inverse_ref[0, rows] = low
        pseudo = mm(low, value[rows]).astype(bf16)
        pseudo_ref[0, rows] = pseudo
        heads_out = mm(attend, pseudo)
        scale = lax.rsqrt(jnp.mean(heads_out * heads_out, axis=1, keepdims=True) + norm_eps)
        gate = og[rows]
        gated_ref[rows] = (
            heads_out * scale * gain[...] * (gate * jax.nn.sigmoid(gate))
        ).astype(bf16)


def silu_back(pre, sig):
    return sig * (1.0 + pre * (1.0 - sig))


def conv_back(grad, shifted, signal, weight, position):
    out = grad * weight[TAPS - 1 : TAPS]
    taps = [jnp.sum(grad * signal, axis=0, keepdims=True)]
    for delay in range(1, TAPS):
        taps.append(jnp.sum(grad * shifted[delay - 1], axis=0, keepdims=True))
        kept = jnp.where(position >= delay, grad, 0.0)
        out = out + pltpu.roll(kept, ROWS - delay, 0) * weight[TAPS - 1 - delay : TAPS - delay]
    return out, jnp.concatenate(taps[::-1], axis=0)


def mixer_backward_kernel(
    pq, pk, pv, og, gg, col, row, wq, wk, wv, gain, inverse_ref, pseudo_ref,
    dq_ref, dk_ref, dv_ref, dog_ref, dwq_ref, dwk_ref, dwv_ref, dgain_ref, dcol_ref, drow_ref,
    gq_s, gk_s, gv_s,
):
    position = col[0, :, 3:4]
    pres = []
    for signal, weight in ((pq, wq), (pk, wk), (pv, wv)):
        pre, shifted = conv_taps(signal[...], weight[...], position)
        pres.append((pre, jax.nn.sigmoid(pre), shifted))
    mixed_q, mixed_k, value = (pre * sig for pre, sig, _ in pres)
    unit_q, unit_k = unit_rows(mixed_q), unit_rows(mixed_k)
    query = mixed_q * (unit_q * DK ** (-0.5))
    key = mixed_k * unit_k
    gain_total = jnp.zeros((1, DV), f32)
    for chain in range(MICRO):
        rows = slice(chain * MB_TOK, (chain + 1) * MB_TOK)
        at, to, lower, strict = chain_masks(col[0, rows, 2:3], row[0, 2:3, rows])
        spread = jnp.where(lower, col[0, rows, 0:1] - row[0, 0:1, rows], 0.0)
        fade = jnp.where(lower, jnp.exp(spread), 0.0)
        beta = row[0, 1:2, rows]
        q, k = query[rows].astype(bf16), key[rows].astype(bf16)
        system = jnp.where(strict, fade, 0.0) * mm(k, k, NT)
        attend = fade * mm(q, k, NT)
        spread_attend = (attend * beta).astype(bf16)
        pseudo_low = pseudo_ref[0, rows]
        heads_out = mm(spread_attend, pseudo_low)
        scale = lax.rsqrt(jnp.mean(heads_out * heads_out, axis=1, keepdims=True) + norm_eps)
        gate = og[rows]
        sig = jax.nn.sigmoid(gate)
        grad = gg[rows]
        unit = heads_out * scale
        dog_ref[rows] = (grad * unit * gain[...] * silu_back(gate, sig)).astype(bf16)
        grad = grad * (gate * sig)
        gain_total = gain_total + jnp.sum(grad * unit, axis=0, keepdims=True)
        grad = grad * gain[...]
        grad_out = scale * (grad - unit * jnp.mean(grad * unit, axis=1, keepdims=True))
        out_low = grad_out.astype(bf16)
        grad_attend = mm(out_low, pseudo_low, NT)
        grad_value = mm(inverse_ref[0, rows], mm(spread_attend, out_low, TN), TN)
        grad_system = -mm(grad_value, pseudo_low, NT)
        both = grad_attend * attend + grad_system * system
        drow_ref[0, 0:1, rows] = jnp.sum(both, axis=0, keepdims=True)
        dcol_ref[0, rows] = jnp.broadcast_to(
            jnp.sum(both * beta, axis=1, keepdims=True), (MB_TOK, 8)
        )
        weight = fade * beta
        from_attend = (grad_attend * weight).astype(bf16)
        from_system = (jnp.where(strict, grad_system, 0.0) * weight).astype(bf16)
        gq_s[rows] = mm(from_attend, k)
        gk_s[rows] = mm(from_attend, q, TN) + (mm(from_system, k) + mm(from_system, k, TN))
        gv_s[rows] = grad_value
    drow_ref[0, 1:8] = jnp.zeros((7, ROWS), f32)
    dgain_ref[0] = jnp.broadcast_to(gain_total, (8, DV))
    grad_q = gq_s[...] * DK ** (-0.5)
    unit = mixed_q * unit_q
    grad_q = unit_q * (grad_q - unit * jnp.sum(grad_q * unit, axis=1, keepdims=True))
    grad_k = gk_s[...]
    grad_k = unit_k * (grad_k - key * jnp.sum(grad_k * key, axis=1, keepdims=True))
    for grad, (pre, sig, shifted), signal, weight, out, dw in (
        (grad_q, pres[0], pq, wq, dq_ref, dwq_ref),
        (grad_k, pres[1], pk, wk, dk_ref, dwk_ref),
        (gv_s[...], pres[2], pv, wv, dv_ref, dwv_ref),
    ):
        back, taps = conv_back(
            grad * silu_back(pre, sig), shifted, signal[...], weight[...], position
        )
        out[...] = back.astype(bf16)
        dw[...] = taps


def columns(width, start):
    return pl.BlockSpec((ROWS, width), lambda head: (0, head + start))


def tap_columns(width, start):
    return pl.BlockSpec((TAPS, width), lambda head: (0, head + start))


def per_head(*shape, start=0):
    return pl.BlockSpec((1,) + shape, lambda head: (head + start,) + (0,) * len(shape))


def mixer_inputs(first):
    return (
        [columns(DK, first), columns(DK, H + first), columns(DV, H + first)]
        + [columns(DV, 2 * H + first)],
        [per_head(ROWS, 8, start=first), per_head(8, ROWS, start=first)]
        + [tap_columns(DK, first), tap_columns(DK, H + first), tap_columns(DV, H + first)]
        + [pl.BlockSpec((1, DV), lambda head: (0, 0))],
    )


def mixer_forward(projected, col, row, taps, gain, first, count):
    start, rest = mixer_inputs(first)
    return pl.pallas_call(
        mixer_forward_kernel,
        grid=(count,),
        in_specs=start + rest,
        out_specs=[columns(DV, 0), per_head(ROWS, MB_TOK), per_head(ROWS, DV)],
        out_shape=[
            jax.ShapeDtypeStruct((ROWS, count * DV), bf16),
            jax.ShapeDtypeStruct((count, ROWS, MB_TOK), bf16),
            jax.ShapeDtypeStruct((count, ROWS, DV), bf16),
        ],
        name="mixer_forward",
        cost_estimate=cost(4.4 * count),
    )(projected, projected, projected, projected, col, row, taps, taps, taps, gain)


def mixer_backward(projected, grad_gated, col, row, taps, gain, inverse, pseudo, first):
    start, rest = mixer_inputs(first)
    count = inverse.shape[0]
    return pl.pallas_call(
        mixer_backward_kernel,
        grid=(count,),
        in_specs=start
        + [columns(DV, first)]
        + rest
        + [per_head(ROWS, MB_TOK), per_head(ROWS, DV)],
        out_specs=[columns(DK, 0), columns(DK, 0), columns(DV, 0), columns(DV, 0)]
        + [tap_columns(DK, 0), tap_columns(DK, 0), tap_columns(DV, 0)]
        + [per_head(8, DV), per_head(ROWS, 8), per_head(8, ROWS)],
        out_shape=[
            jax.ShapeDtypeStruct((ROWS, count * DK), bf16),
            jax.ShapeDtypeStruct((ROWS, count * DK), bf16),
            jax.ShapeDtypeStruct((ROWS, count * DV), bf16),
            jax.ShapeDtypeStruct((ROWS, count * DV), bf16),
            jax.ShapeDtypeStruct((TAPS, count * DK), f32),
            jax.ShapeDtypeStruct((TAPS, count * DK), f32),
            jax.ShapeDtypeStruct((TAPS, count * DV), f32),
            jax.ShapeDtypeStruct((count, 8, DV), f32),
            jax.ShapeDtypeStruct((count, ROWS, 8), f32),
            jax.ShapeDtypeStruct((count, 8, ROWS), f32),
        ],
        scratch_shapes=[
            pltpu.VMEM((ROWS, DK), f32),
            pltpu.VMEM((ROWS, DK), f32),
            pltpu.VMEM((ROWS, DV), f32),
        ],
        name="mixer_backward",
        cost_estimate=cost(4.6 * count),
    )(
        projected, projected, projected, projected, grad_gated, col, row,
        taps, taps, taps, gain, inverse, pseudo,
    )


BLOCKS = tuple((dz, dx) for dx in (1, 0) for dz in (1, 3, 0, 2))


class Plane:
    def __init__(self):
        fsdp, dp = lax.axis_index("fsdp"), lax.axis_index("dp")
        self.z, self.x = fsdp // 2, fsdp % 2
        self.y, self.core = dp // 2, dp % 2

    @staticmethod
    def move(value, dz=0, dx=0, dy=0, dc=0):
        flip = (dz * 2 + dx) * 4 + dy * 2 + dc
        return lax.ppermute(value, ("fsdp", "dp"), [(here, here ^ flip) for here in range(32)])

    def units(self):
        own, other = [], []
        for dz, dx in BLOCKS:
            base = ((self.z ^ dz) * 2 + (self.x ^ dx)) * 2
            own.append(base + self.core)
            other.append(base + 1 - self.core)
        return jnp.stack(own + other).astype(jnp.int32)

    def half(self, shard):
        rows = shard.shape[0] // 2
        return lax.dynamic_slice_in_dim(shard, self.core * rows, rows, 0)

    def gather_small(self, row):
        fsdp = self.z * 2 + self.x
        rows = [row]
        for step in range(1, 8):
            pairs = [(i, (i // 4 ^ step) * 4 + i % 4) for i in range(32)]
            rows.append(lax.ppermute(row, ("fsdp", "dp"), pairs))
        place = jnp.arange(8, dtype=jnp.int32)
        picks = (place[:, None] ^ place[None, :]) == fsdp
        return exact(picks.astype(bf16), jnp.stack(rows).reshape(8, -1)).astype(bf16)

    def sum_small(self, value):
        for step in (1, 2, 4, 8, 16):
            value = value + lax.ppermute(value, ("fsdp", "dp"), [(i, i ^ step) for i in range(32)])
        return value


def after(value, *others):
    return lax.optimization_barrier((value,) + others)[0]


def summed(*terms):
    return sum(term.astype(f32) for term in terms).astype(bf16)


def gather_blocks(plane, half):
    got = {(0, 0): half, (1, 0): plane.move(half, dz=1), (2, 0): plane.move(half, dz=2)}
    got[3, 0] = plane.move(got[2, 0], dz=1)
    for dz in range(4):
        got[dz, 1] = plane.move(got[dz, 0], dx=1)
    return [got[at] for at in BLOCKS] + [plane.move(got[at], dc=1) for at in BLOCKS]


class Reduce:
    def __init__(self, plane, sums, split=False):
        self.plane, self.split = plane, split
        self.keep, self.send = sums
        self.back = plane.move(self.send, dc=1)

    def start(self, *others):
        back = after(self.back, *others)
        if not self.split:
            self.part = summed(self.keep[4:], back[4:])
            return self._beside(summed(self.keep[:4], back[:4]))

        def take(array, at):
            return lax.dynamic_slice_in_dim(array, at * 32, 32, 1)

        y = self.plane.y
        self.mine = summed(take(self.keep, y), take(back, y))
        sent = summed(take(self.keep, 1 - y), take(back, 1 - y))
        self.from_y = self.plane.move(sent, dy=1)
        return sent

    def _beside(self, sent):
        self.from_x = self.plane.move(sent, dx=1)
        return sent

    def beside(self, *others):
        from_y = after(self.from_y, *others)
        self.part = summed(self.mine[4:], from_y[4:])
        return self._beside(summed(self.mine[:4], from_y[:4]))

    def turn(self, *others):
        from_x = after(self.from_x, *others)
        sent = summed(self.part[:2], from_x[:2])
        self.rest = summed(self.part[2:], from_x[2:])
        self.from_z = self.plane.move(sent, dz=1)
        return sent

    def along(self, *others):
        self.near = after(self.from_z, *others)
        sent = summed(self.rest[1], self.near[1])
        self.far = self.plane.move(sent, dz=2)
        return sent

    def across(self, *others):
        self.total = summed(self.rest[0], self.near[0], after(self.far, *others))
        self.other = self.plane.move(self.total, dy=1)
        return self.total

    def close(self, *others):
        other = after(self.other, *others)
        if self.split:
            first = self.plane.y == 0
            total = jnp.concatenate(
                [jnp.where(first, self.total, other), jnp.where(first, other, self.total)], axis=0
            )
        else:
            total = summed(self.total, other)
        self.total, self.other = total, self.plane.move(total, dc=1)
        return total

    def halves(self):
        first = self.plane.core == 0
        return (
            jnp.where(first, self.total, self.other),
            jnp.where(first, self.other, self.total),
        )


def cost(us):
    return pl.CostEstimate(
        flops=int(us * 1.0e9), transcendentals=0, bytes_accessed=int(us * 3.0e6)
    )


def place(weight, units, blocks, rows, parts=1):
    width = weight.shape[1]
    for i, block in enumerate(blocks):
        for part in range(parts):
            count = min(rows - 64 * part, 64)
            start = pl.multiple_of(units[i] * rows + 64 * part, 16)
            weight[pl.ds(start, count), :] = block[:count, part * width : (part + 1) * width]


def project_kernel(units, x_ref, *refs):
    blocks, y_ref, weight = refs[:16], refs[16], refs[17]
    place(weight, units, blocks, 64)
    y_ref[...] = jnp.dot(x_ref[...], weight[...], preferred_element_type=f32)


def project(units, value, blocks, tile):
    width = blocks[0].shape[1]
    rows, depth = value.shape
    return pl.pallas_call(
        project_kernel,
        grid_spec=pltpu.PrefetchScalarGridSpec(
            num_scalar_prefetch=1,
            grid=(width // tile,),
            in_specs=[pl.BlockSpec((rows, depth), lambda n, s: (0, 0))]
            + [pl.BlockSpec((64, tile), lambda n, s: (0, n))] * 16,
            out_specs=pl.BlockSpec((rows, tile), lambda n, s: (0, n)),
            scratch_shapes=[pltpu.VMEM((depth, tile), bf16)],
        ),
        out_shape=jax.ShapeDtypeStruct((rows, width), f32),
        name="project",
        cost_estimate=cost(17),
    )(units, value, *blocks)


def tiles_of(arrays, tile):
    specs, firsts, first = [], [], 0
    for array in arrays:
        count = array.shape[1] // tile

        def index(n, s, first=first, count=count):
            return (0, jnp.clip(n - first, 0, count - 1))

        specs.append(pl.BlockSpec((array.shape[0], tile), index))
        firsts.append(first)
        first += count
    return specs, firsts, first


def pick(step, firsts, refs, chosen):
    for i, ref in enumerate(refs):
        here = step >= firsts[i]
        if i + 1 < len(refs):
            here = here & (step < firsts[i + 1])

        @pl.when(here)
        def _():
            chosen[...] = ref[...]


def back_project_kernel(firsts, units, *refs):
    rights, blocks = refs[: len(firsts)], refs[len(firsts) : len(firsts) + 16]
    out_ref, chosen, weight = refs[len(firsts) + 16 :]
    step = pl.program_id(0)
    pick(step, firsts, rights, chosen)
    place(weight, units, blocks, 64)
    part = lax.dot_general(chosen[...], weight[...], NT, preferred_element_type=f32)

    @pl.when(step == 0)
    def _():
        out_ref[...] = part

    @pl.when(step > 0)
    def _():
        out_ref[...] += part


def back_project(units, rights, blocks, depth, tile):
    specs, firsts, steps = tiles_of(rights, tile)
    rows = rights[0].shape[0]
    return pl.pallas_call(
        partial(back_project_kernel, tuple(firsts)),
        grid_spec=pltpu.PrefetchScalarGridSpec(
            num_scalar_prefetch=1,
            grid=(steps,),
            in_specs=specs + [pl.BlockSpec((64, tile), lambda n, s: (0, n))] * 16,
            out_specs=pl.BlockSpec((rows, depth), lambda n, s: (0, 0)),
            scratch_shapes=[pltpu.VMEM((rows, tile), bf16), pltpu.VMEM((depth, tile), bf16)],
        ),
        out_shape=jax.ShapeDtypeStruct((rows, depth), f32),
        name="back_project",
        cost_estimate=cost(18),
    )(units, *rights, *blocks)


def gram_kernel(firsts, rows, units, left_ref, *refs):
    rights = refs[: len(firsts)]
    keep, send, chosen, total = refs[-4:]
    step, part = pl.program_id(0), pl.program_id(1)

    @pl.when(part == 0)
    def _():
        pick(step, firsts, rights, chosen)
        total[0 : left_ref.shape[0], :] = jnp.dot(
            left_ref[...], chosen[...], preferred_element_type=f32
        )

    def block(i):
        value = total[pl.ds(pl.multiple_of(units[i] * rows + part * 64, 16), 64), :]
        if rows % 64:
            inside = lax.broadcasted_iota(jnp.int32, value.shape, 0) < rows - part * 64
            value = jnp.where(inside, value, 0.0)
        return value.astype(bf16)

    for i in range(8):
        keep[i] = block(i)
        send[i] = block(8 + i)


def gram_blocks(units, left, rights, tile, width, base=0, into=()):
    depth, inner = left.shape
    rows = depth // 16
    parts = -(-rows // 64)
    specs, firsts, steps = tiles_of(rights, tile)
    specs = [
        pl.BlockSpec(spec.block_shape, lambda n, p, s, index=spec.index_map: index(n, s))
        for spec in specs
    ]
    first = base // tile

    def column(n, p, s):
        return (0, first + p * steps + n)

    whole = pl.BlockSpec(memory_space=pl.ANY)
    out = pl.pallas_call(
        partial(gram_kernel, tuple(firsts), rows),
        grid_spec=pltpu.PrefetchScalarGridSpec(
            num_scalar_prefetch=1,
            grid=(steps, parts),
            in_specs=[pl.BlockSpec((depth, inner), lambda n, p, s: (0, 0))]
            + specs
            + [whole] * len(into),
            out_specs=[pl.BlockSpec((8, 64, tile), lambda n, p, s: (0,) + column(n, p, s))] * 2,
            scratch_shapes=[
                pltpu.VMEM((inner, tile), bf16),
                pltpu.VMEM((depth + 64, tile), f32),
            ],
        ),
        out_shape=[jax.ShapeDtypeStruct((8, 64, width), bf16)] * 2,
        input_output_aliases={2 + len(rights) + i: i for i in range(len(into))},
        name="gram_blocks",
        cost_estimate=cost(steps * tile * depth / 2.9e5),
    )(units, left, *rights, *into)
    return list(out)


FTILE = 256


PART = 32
DOWN_AT = (0, 96, 176, 256)


def late_quarter(w_down, w_out, w_gate, w_up):
    dp = lax.axis_index("dp")

    def parts(shard, start, rows):
        piece = lax.dynamic_slice_in_dim(shard, start, rows, 0)
        return [piece[i : i + PART] for i in range(0, rows, PART)]

    start = jnp.asarray(DOWN_AT, jnp.int32)[dp]
    return jnp.concatenate(
        parts(w_down, start, 96)
        + parts(w_out, dp * 64, 64)
        + parts(w_gate, dp * PART, PART)
        + parts(w_up, dp * PART, PART),
        axis=1,
    )


def late_specs(depth, wide):
    fixed = dict(pipeline_mode=pl.Buffered(1))
    gate = 5 * depth // FTILE
    return [
        pl.BlockSpec((32 * PART, 3 * depth), lambda n: (0, 0), **fixed),
        pl.BlockSpec((32 * PART, depth), lambda n: (0, 3), **fixed),
        pl.BlockSpec((32 * PART, depth), lambda n: (0, 4), **fixed),
        pl.BlockSpec((32 * PART, FTILE), lambda n: (0, gate + n)),
        pl.BlockSpec((32 * PART, FTILE), lambda n: (0, gate + wide // FTILE + n)),
    ]


def place_late(down, first, second, w_out, w_down):
    depth = w_down.shape[1]
    for group in range(32):
        given = slice(group * PART, (group + 1) * PART)
        w_out[group * 64 : group * 64 + PART] = first[given]
        w_out[group * 64 + PART : (group + 1) * 64] = second[given]
        start = group // 4 * 352 + DOWN_AT[group % 4]
        for i in range(3):
            at = start + i * PART
            w_down[at : at + PART] = down[given, i * depth : (i + 1) * depth]


def ffn_forward_kernel(
    gated, more, x, gain, down, out_first, out_second, w_gate, w_up,
    residual, ffn_low, gate_act, up_act, hidden, result, w_out, w_down, total,
):
    step = pl.program_id(0)

    @pl.when(step == 0)
    def _():
        place_late(down, out_first, out_second, w_out, w_down)
        inner = gated.shape[1]
        value = x[...].astype(f32)
        value += jnp.dot(gated[...], w_out[:inner], preferred_element_type=f32)
        value += jnp.dot(more[...], w_out[inner:], preferred_element_type=f32)
        residual[...] = value
        total[...] = value
        scale = lax.rsqrt(jnp.mean(value * value, axis=1, keepdims=True) + norm_eps)
        ffn_low[...] = (value * scale * gain[...]).astype(bf16)

    gate = jnp.dot(ffn_low[...], w_gate[...], preferred_element_type=f32)
    up = jnp.dot(ffn_low[...], w_up[...], preferred_element_type=f32)
    gate_act[...] = gate.astype(bf16)
    up_act[...] = up.astype(bf16)
    low = (gate * jax.nn.sigmoid(gate) * up).astype(bf16)
    hidden[...] = low
    total[...] += jnp.dot(
        low, w_down[pl.ds(pl.multiple_of(step * FTILE, FTILE), FTILE), :],
        preferred_element_type=f32,
    )

    @pl.when(step == pl.num_programs(0) - 1)
    def _():
        result[...] = total[...].astype(bf16)


def ffn_forward(gated, more, x, gain, late):
    rows, depth = x.shape
    wide = (late.shape[1] - 5 * depth) // 2
    tall = gated.shape[1] + more.shape[1]
    still = lambda array: pl.BlockSpec(array.shape, lambda n: (0, 0))
    tile = pl.BlockSpec((rows, FTILE), lambda n: (0, n))
    whole = pl.BlockSpec((rows, depth), lambda n: (0, 0))
    return pl.pallas_call(
        ffn_forward_kernel,
        grid_spec=pltpu.PrefetchScalarGridSpec(
            num_scalar_prefetch=0,
            grid=(wide // FTILE,),
            in_specs=[still(gated), still(more), still(x), still(gain)] + late_specs(depth, wide),
            out_specs=[whole, whole, tile, tile, tile, whole],
            scratch_shapes=[
                pltpu.VMEM((tall, depth), bf16),
                pltpu.VMEM((wide, depth), bf16),
                pltpu.VMEM((rows, depth), f32),
            ],
        ),
        out_shape=[
            jax.ShapeDtypeStruct((rows, depth), f32),
            jax.ShapeDtypeStruct((rows, depth), bf16),
            jax.ShapeDtypeStruct((rows, wide), bf16),
            jax.ShapeDtypeStruct((rows, wide), bf16),
            jax.ShapeDtypeStruct((rows, wide), bf16),
            jax.ShapeDtypeStruct((rows, depth), bf16),
        ],
        name="ffn_forward",
        cost_estimate=cost(27),
    )(gated, more, x, gain, *[late] * 5)


def ffn_backward_kernel(
    cot, residual, gain, gate_act, up_act, down, out_first, out_second, w_gate, w_up,
    gate_low, up_low, grad_residual, mix_low, grad_gated, grad_gain, w_out, w_down, total,
):
    step = pl.program_id(0)

    @pl.when(step == 0)
    def _():
        place_late(down, out_first, out_second, w_out, w_down)
        total[...] = jnp.zeros_like(total)

    grad = lax.dot_general(
        cot[...], w_down[pl.ds(pl.multiple_of(step * FTILE, FTILE), FTILE), :], NT,
        preferred_element_type=f32,
    )
    gate, up = gate_act[...].astype(f32), up_act[...].astype(f32)
    sig = jax.nn.sigmoid(gate)
    low = (grad * up * silu_back(gate, sig)).astype(bf16)
    gate_low[...] = low
    part = lax.dot_general(low, w_gate[...], NT, preferred_element_type=f32)
    low = (grad * (gate * sig)).astype(bf16)
    up_low[...] = low
    total[...] += part + lax.dot_general(low, w_up[...], NT, preferred_element_type=f32)

    @pl.when(step == pl.num_programs(0) - 1)
    def _():
        value, grad = residual[...], total[...]
        scale = lax.rsqrt(jnp.mean(value * value, axis=1, keepdims=True) + norm_eps)
        unit = value * scale
        grad_gain[...] = jnp.sum(grad * unit, axis=0, keepdims=True)
        grad = grad * gain[...]
        grad = scale * (grad - unit * jnp.mean(grad * unit, axis=1, keepdims=True))
        grad = cot[...].astype(f32) + grad
        grad_residual[...] = grad
        low = grad.astype(bf16)
        mix_low[...] = low
        grad_gated[...] = lax.dot_general(low, w_out[...], NT, preferred_element_type=f32)


def ffn_backward(cot, residual, gain, gate_act, up_act, late):
    rows, depth = cot.shape
    wide = gate_act.shape[1]
    tall = 2 * depth
    still = lambda array: pl.BlockSpec(array.shape, lambda n: (0, 0))
    tile = pl.BlockSpec((rows, FTILE), lambda n: (0, n))
    whole = pl.BlockSpec((rows, depth), lambda n: (0, 0))
    return pl.pallas_call(
        ffn_backward_kernel,
        grid_spec=pltpu.PrefetchScalarGridSpec(
            num_scalar_prefetch=0,
            grid=(wide // FTILE,),
            in_specs=[still(cot), still(residual), still(gain), tile, tile] + late_specs(depth, wide),
            out_specs=[
                tile, tile, whole, whole,
                pl.BlockSpec((rows, tall), lambda n: (0, 0)),
                pl.BlockSpec((1, depth), lambda n: (0, 0)),
            ],
            scratch_shapes=[
                pltpu.VMEM((tall, depth), bf16),
                pltpu.VMEM((wide, depth), bf16),
                pltpu.VMEM((rows, depth), f32),
            ],
        ),
        out_shape=[
            jax.ShapeDtypeStruct((rows, wide), bf16),
            jax.ShapeDtypeStruct((rows, wide), bf16),
            jax.ShapeDtypeStruct((rows, depth), f32),
            jax.ShapeDtypeStruct((rows, depth), bf16),
            jax.ShapeDtypeStruct((rows, tall), f32),
            jax.ShapeDtypeStruct((1, depth), f32),
        ],
        name="ffn_backward",
        cost_estimate=cost(35),
    )(cot, residual, gain, gate_act, up_act, *[late] * 5)


def rows_of(array, rows, width):
    count = array.shape[1] // width
    parts = [array[:, i * width : (i + 1) * width] for i in range(count)]
    parts[-1] = parts[-1][: rows - 64 * (count - 1)]
    return jnp.concatenate(parts, axis=0)


def rms_scale(values, gain):
    return values * lax.rsqrt(jnp.mean(values * values, axis=-1, keepdims=True) + norm_eps) * gain


def swiglu(gate_act, up_act):
    return jax.nn.silu(gate_act) * up_act


def exact(left, right, dims=NN):
    return lax.dot_general(left, right, dims, preferred_element_type=f32)


def select_rows(rows, array, dims=NN):
    picks = rows[:, None] == jnp.arange(array.shape[0], dtype=jnp.int32)[None, :]
    return exact(picks.astype(bf16), array, dims).astype(bf16)


def routing(seq_len, dealt_slot, parts, own_index):
    share = MB_TOK // parts
    count = seq_len.shape[0]
    order = jnp.arange(count, dtype=jnp.int32)
    holder = jnp.sum(jnp.where(dealt_slot[None, :] == order[:, None], order[None, :], 0), axis=1)
    piece = seq_len // parts
    begin = jnp.sum(jnp.where(order[None, :] < order[:, None], piece[None, :], 0), axis=1)
    holds = holder[:, None] == order[None, :]
    slot_len = jnp.sum(jnp.where(holds, seq_len[None, :], 0), axis=1)
    slot_len = slot_len.reshape(parts, MICRO, SEQ_MB)
    slot_given = jnp.sum(jnp.where(holds, begin[None, :], 0), axis=1)
    slot_given = slot_given.reshape(parts, MICRO, SEQ_MB)
    slot_piece = slot_len // parts
    slot_row = jnp.arange(share, dtype=jnp.int32)
    place = jnp.arange(MB_TOK, dtype=jnp.int32)
    source = jnp.arange(parts, dtype=jnp.int32)
    micro = jnp.arange(MICRO, dtype=jnp.int32)
    first = jnp.cumsum(slot_piece, axis=2) - slot_piece
    row = slot_row[None, None, :, None]
    inside = (row >= first[:, :, None, :]) & (row < (first + slot_piece)[:, :, None, :])
    send = jnp.sum(
        jnp.where(inside, slot_given[:, :, None, :] + row - first[:, :, None, :], 0), axis=3
    )
    own_len = lax.dynamic_index_in_dim(slot_len, own_index, 0, keepdims=False)
    own_piece = own_len // parts
    own_first = jnp.cumsum(own_piece, axis=1) - own_piece
    own_start = jnp.cumsum(own_len, axis=1) - own_len
    offset = place[None, :, None] - own_start[:, None, :]
    covered = (offset >= 0) & (offset < own_len[:, None, :])
    per = own_piece[:, None, :]
    flat = (
        offset // per * (MICRO * share)
        + micro[:, None, None] * share
        + own_first[:, None, :]
        + offset % per
    )
    arrange = jnp.sum(jnp.where(covered, flat, 0), axis=2).reshape(-1)
    position = jnp.sum(jnp.where(covered, offset, 0), axis=2).reshape(-1)
    label = jnp.sum(
        jnp.where(covered, jnp.arange(SEQ_MB, dtype=jnp.int32)[None, None, :], 0), axis=2
    ).reshape(-1)
    return send.reshape(-1), arrange, position, label


def gate_tables(gate_in, a_log, dt_bias):
    rate = -jnp.exp(a_log) * jax.nn.softplus(gate_in[:, :H] + dt_bias)
    place = jnp.arange(MB_TOK, dtype=jnp.int32)
    lower = (place[:, None] >= place[None, :]).astype(f32)
    total = jnp.einsum(
        "ij,cjh->cih", lower, rate.reshape(MICRO, MB_TOK, H), precision=lax.Precision.HIGHEST
    ).reshape(ROWS, H)
    return total, jax.nn.sigmoid(gate_in[:, H:])


def gather_full(shard):
    reps = lax.axis_size("dp")
    if shard.shape[0] % (8 * reps) == 0:
        rows = shard.shape[0] // reps
        part = lax.dynamic_slice_in_dim(shard, lax.axis_index("dp") * rows, rows, 0)
        return lax.all_gather(part, ("fsdp", "dp"), axis=0, tiled=True)
    return lax.all_gather(shard, "fsdp", axis=0, tiled=True)


def reduce_grad(grad):
    parts, reps = lax.axis_size("fsdp"), lax.axis_size("dp")
    if grad.shape[0] % (8 * parts * reps) == 0:
        part = lax.psum_scatter(grad, ("fsdp", "dp"), scatter_dimension=0, tiled=True)
        return lax.all_gather(part, "dp", axis=0, tiled=True).astype(f32)
    part = lax.psum_scatter(grad, "fsdp", scatter_dimension=0, tiled=True)
    return lax.psum(part, "dp").astype(f32)


def local(
    tokens,
    cotangent,
    lengths,
    dealing,
    gain_mix,
    w_qkv,
    w_gates,
    w_outgate,
    conv_weight,
    a_log,
    dt_bias,
    out_norm_gain,
    w_out,
    gain_ffn,
    w_gate,
    w_up,
    w_down,
):
    parts = lax.axis_size("fsdp")
    own = lax.axis_index("fsdp")
    width = tokens.shape[2]
    share = MB_TOK // parts
    plane = Plane() if (parts, lax.axis_size("dp")) == (8, 4) else None
    send, arrange, position, label = routing(lengths[0], dealing[0], parts, own)

    def exchange(rows):
        return lax.all_to_all(
            rows.reshape(parts, MICRO * share, width),
            "fsdp",
            split_axis=0,
            concat_axis=0,
            tiled=True,
        ).reshape(ROWS, width)

    def give_back(rows):
        return select_rows(send, exchange(select_rows(arrange, rows, TN)), TN)[None]

    def gram(left, right):
        return exact(left, right, TN).astype(bf16)

    small = (gain_mix, gain_ffn, w_gates, conv_weight)
    packed = jnp.concatenate([item.reshape(-1) for item in small])
    if plane:
        packed = plane.gather_small(packed.reshape(-1, 128))
    else:
        packed = lax.all_gather(packed, "fsdp", axis=0, tiled=False)
    packed = packed.reshape(parts, -1)
    full, start = [], 0
    for item in small:
        piece = packed[:, start : start + item.size]
        full.append(piece.reshape((parts * item.shape[0],) + item.shape[1:]))
        start += item.size
    full_gain_mix, full_gain_ffn = full[0].astype(f32), full[1].astype(f32)
    full_gates, taps = full[2], full[3].astype(f32).T

    local_x = select_rows(arrange, exchange(select_rows(send, tokens[0])))

    w_mix = jnp.concatenate([w_qkv, w_outgate], axis=1)
    late = (w_down, w_out, w_gate, w_up)
    if plane:
        units = plane.units()
        late_full = lax.all_gather(late_quarter(*late), ("fsdp", "dp"), axis=0, tiled=True)
        mix_blocks = gather_blocks(plane, plane.half(w_mix))
        widths = (3 * width, 2 * width, w_gate.shape[1], w_up.shape[1])
    else:
        full_mix = gather_full(w_mix)
        full_down, full_out, full_gate, full_up = (gather_full(item) for item in late)

    inputs_f = local_x.astype(f32)
    normed, mix_back = jax.vjp(rms_scale, inputs_f, full_gain_mix)
    normed_low = normed.astype(bf16)
    gate_in = exact(normed_low, full_gates)
    (total, strength), gates_back = jax.vjp(gate_tables, gate_in, a_log, dt_bias)
    spread = lambda item: jnp.broadcast_to(item.astype(f32)[:, None], (ROWS, H))
    table = jnp.stack(
        [total, strength, spread(label), spread(position)] + [jnp.zeros((ROWS, H), f32)] * 4
    )
    col = jnp.transpose(table, (2, 1, 0))
    row = jnp.transpose(table, (2, 0, 1))
    gain = out_norm_gain[None, :]
    if plane:
        projected = project(units, normed_low, mix_blocks, 512)
    else:
        projected = exact(normed_low, full_mix)
    count = H // 2
    firsts = (0, count)
    mixed = [mixer_forward(projected, col, row, taps, gain, firsts[0], count)]
    mixed.append(mixer_forward(projected, col, row, taps, gain, firsts[1], count))
    given_cot = after(cotangent[0], mixed[0][0])
    local_cot = select_rows(arrange, exchange(select_rows(send, given_cot)))
    if plane:
        residual, ffn_low, gate_act, up_act, hidden_low, result = ffn_forward(
            mixed[0][0], mixed[1][0], local_x, full_gain_ffn[None, :], late_full
        )
        down = Reduce(
            plane, gram_blocks(units, hidden_low.T, [local_cot], 1024, widths[0])
        )
        rows_out = select_rows(arrange, after(result, down.send), TN)
        recv_out = exchange(rows_out)
        sent = down.start(rows_out)
        gate_low, up_low, grad_residual, mix_low, grad_gated, grad_gain_ffn = ffn_backward(
            after(local_cot, sent), residual, full_gain_ffn[None, :], gate_act, up_act, late_full
        )
        sent = down.turn(grad_gated)
        gated_t = jnp.concatenate([part[0].T for part in mixed], axis=0)
        wide = widths[1] + widths[2]
        sums = gram_blocks(units, gated_t, [after(mix_low, sent)], 1024, wide)
        sums = gram_blocks(units, ffn_low.T, [gate_low], FTILE, wide, widths[1], sums)
        out_gate_sums = Reduce(plane, sums)
        up = Reduce(
            plane,
            gram_blocks(
                units, ffn_low.T, [after(up_low, out_gate_sums.send)], FTILE, widths[3]
            ),
            split=True,
        )
        sent = down.along(up.send)
        sent = out_gate_sums.start(sent)
    else:
        gated_low = jnp.concatenate([part[0] for part in mixed], axis=1)
        residual = inputs_f + exact(gated_low, full_out)
        ffn_normed, ffn_back = jax.vjp(rms_scale, residual, full_gain_ffn)
        ffn_low = ffn_normed.astype(bf16)
        gate_act = exact(ffn_low, full_gate)
        up_act = exact(ffn_low, full_up)
        hidden, act_back = jax.vjp(swiglu, gate_act, up_act)
        hidden_low = hidden.astype(bf16)
        result = (residual + exact(hidden_low, full_down)).astype(bf16)
        output = give_back(result)
        grad_gate_act, grad_up_act = act_back(exact(local_cot, full_down, NT))
        gate_low, up_low = grad_gate_act.astype(bf16), grad_up_act.astype(bf16)
        grad_part, grad_gain_ffn = ffn_back(
            exact(gate_low, full_gate, NT) + exact(up_low, full_up, NT)
        )
        grad_residual = local_cot.astype(f32) + grad_part
        mix_low = grad_residual.astype(bf16)
        grad_gated = exact(mix_low, full_out, NT)
        late_grads = [
            reduce_grad(gram(left, right))
            for left, right in (
                (hidden_low, local_cot), (gated_low, mix_low), (ffn_low, gate_low),
                (ffn_low, up_low),
            )
        ]
    backs = []
    for part, first in zip(mixed, firsts):
        grad = after(grad_gated, sent) if plane else grad_gated
        backs.append(
            mixer_backward(projected, grad, col, row, taps, gain, part[1], part[2], first)
        )
        if plane and not first:
            sent = up.start(backs[0][0])
            sent = down.across(sent)
    rights = [back[i] for i in range(4) for back in backs]
    dtap_q, dtap_k, dtap_v = (
        jnp.concatenate([back[i] for back in backs], axis=1) for i in (4, 5, 6)
    )
    dgain, dcol, drow = (jnp.concatenate([back[i] for back in backs]) for i in (7, 8, 9))
    if plane:
        left = normed_low.T
        qk = Reduce(plane, gram_blocks(units, left, rights[:4], 512, 2 * H * DK))
        rights[4] = after(rights[4], qk.send)
        vo = Reduce(plane, gram_blocks(units, left, rights[4:], 512, 2 * H * DV), split=True)
        sent = out_gate_sums.turn(vo.send)
        sent = qk.start(sent)
        rights[0] = after(rights[0], sent)
        grad_normed = back_project(units, rights, mix_blocks, width, 512)
        sent = up.beside(grad_normed)
        sent = out_gate_sums.along(sent)
        sent = vo.start(sent)
        sent = down.close(sent)
    else:
        low = jnp.concatenate(rights, axis=1)
        grad_mix = reduce_grad(gram(normed_low, low))
        grad_normed = exact(low, full_mix, NT)
    grad_conv = jnp.concatenate([dtap_q, dtap_k, dtap_v], axis=1).T
    grad_out_gain = jnp.sum(dgain[:, 0], axis=0)
    grad_strength = drow[:, 0].T
    grad_total = dcol[:, :, 0].T - strength * grad_strength
    grad_gate_in, grad_a_log, grad_dt_bias = gates_back((grad_total, grad_strength))
    gate_in_low = grad_gate_in.astype(bf16)
    grad_gates = exact(normed_low, gate_in_low, TN)
    grad_normed = grad_normed + exact(gate_in_low, full_gates, NT)
    grad_part, grad_gain_mix = mix_back(grad_normed)
    grad_inputs = (grad_residual + grad_part).astype(bf16)
    if plane:
        rows_in = select_rows(arrange, after(grad_inputs, sent), TN)
        recv_in = exchange(rows_in)
        sent = qk.turn(rows_in)
        sent = up.turn(sent)
        sent = out_gate_sums.across(sent)
        output = select_rows(send, after(recv_out, sent), TN)[None]
    else:
        input_grad = give_back(grad_inputs)

    small_grads = (grad_gain_mix, grad_gain_ffn, grad_gates, grad_conv)
    alone = (grad_a_log, grad_dt_bias, grad_out_gain)
    sums = jnp.concatenate(
        [item.reshape(parts, -1) for item in small_grads]
        + [jnp.broadcast_to(jnp.concatenate(alone)[None], (parts, 2 * H + DV))],
        axis=1,
    )
    if plane:
        sums = plane.sum_small(after(sums, sent))
        sent = qk.along(sums)
        sent = vo.beside(sent)
        sent = up.along(sent)
        sent = out_gate_sums.close(sent)
        input_grad = select_rows(send, after(recv_in, sent), TN)[None]
        sent = qk.across(input_grad)
        sent = vo.turn(sent)
        sent = up.across(sent)
        sent = qk.close(sent)
        sent = vo.along(sent)
        sent = up.close(sent)
        sent = vo.across(sent)
        vo.close(sent)
        out_gate_halves = out_gate_sums.halves()
        cut = widths[1]

        def whole(halves, rows, columns):
            return jnp.concatenate(
                [rows_of(part, rows // 2, columns) for part in halves], axis=0
            ).astype(f32)

        late_grads = (
            whole(down.halves(), w_down.shape[0], width),
            whole([part[:, :cut] for part in out_gate_halves], w_out.shape[0], width),
            jnp.concatenate([part[:, cut:] for part in out_gate_halves], axis=0).astype(f32),
            jnp.concatenate(up.halves(), axis=0).astype(f32),
        )
        qk_grad, vo_grad = (
            jnp.concatenate(item.halves(), axis=0).astype(f32) for item in (qk, vo)
        )
        grad_qkv = jnp.concatenate([qk_grad, vo_grad[:, : H * DV]], axis=1)
        grad_outgate = vo_grad[:, H * DV :]
    else:
        sums = lax.psum(sums, ("fsdp", "dp"))
        grad_qkv, grad_outgate = grad_mix[:, : w_qkv.shape[1]], grad_mix[:, w_qkv.shape[1] :]
    sums = lax.dynamic_index_in_dim(sums, own, 0, keepdims=False)
    ready, start = [], 0
    for item in (gain_mix, gain_ffn, w_gates, conv_weight) + alone:
        ready.append(sums[start : start + item.size].reshape(item.shape))
        start += item.size
    return (
        output,
        input_grad,
        ready[0],
        grad_qkv,
        ready[2],
        grad_outgate,
        ready[3],
        ready[4],
        ready[5],
        ready[6],
        late_grads[1],
        ready[1],
        late_grads[2],
        late_grads[3],
        late_grads[0],
    )


def solution(mesh):
    in_specs = (
        P("dp", "fsdp", None),
        P("dp", "fsdp", None),
        P("dp", None),
        P("dp", None),
        P("fsdp"),
        P("fsdp", None),
        P("fsdp", None),
        P("fsdp", None),
        P("fsdp", None),
        P(),
        P(),
        P(),
        P("fsdp", None),
        P("fsdp"),
        P("fsdp", None),
        P("fsdp", None),
        P("fsdp", None),
    )
    out_specs = (
        P("dp", "fsdp", None),
        P("dp", "fsdp", None),
        P("fsdp"),
        P("fsdp", None),
        P("fsdp", None),
        P("fsdp", None),
        P("fsdp", None),
        P(),
        P(),
        P(),
        P("fsdp", None),
        P("fsdp"),
        P("fsdp", None),
        P("fsdp", None),
        P("fsdp", None),
    )
    return jax.shard_map(local, mesh=mesh, in_specs=in_specs, out_specs=out_specs, check_vma=False)
```

time: 2400 us -> 773 us (0.32)
  other arithmetic: 869 us -> 76.7 us
  matrix products: 458 us -> 22.5 us
  waiting for transfers between devices: 582 us -> 288 us
  Pallas kernels: 0 us -> 228 us
  blocking collectives: 179 us -> 0 us
  local copies, waits for them, and re-layouts: 225 us -> 56.8 us
  starting transfers between devices: 39 us -> 76 us
    another operation x114 -> x3, other arithmetic: 682 us -> 1.73 us  [the longest x1 1.38 us: routing(): first = jnp.cumsum(slot_piece, axis=2) - slot_piece]
    dot_general x194 -> x14, matrix products: 422 us -> 22.5 us  [the longest x12 22.1 us: exact(): return lax.dot_general(left, right, dims, preferred_element_type=f32)]
    reduce_scatter x7 -> x0, waiting for transfers between devices: 388 us -> none  [local(): summed = lax.psum_scatter(totals, 'fsdp', scatter_dimension=0, tiled=True)]
    ppermute x0 -> x59, waiting for transfers between devices: none -> 280 us  [the longest x47 190 us: move(): lax.ppermute(value, ('fsdp', 'dp'), [(here, here ^ flip) for here in rang...]
    pallas_call x0 -> x14, Pallas kernels: none -> 228 us  [the longest x6 59.2 us: gram_blocks(): pl.pallas_call(partial(gram_kernel, tuple(firsts), rows), grid_spec=pltpu...]
    all_gather x4 -> x0, blocking collectives: 110 us -> none  [the longest x1 48.6 us: local(): lax.all_gather(shards[4], 'fsdp', axis=0, tiled=True)]
    all_to_all x8 -> x4, waiting for transfers between devices: 104 us -> 7.65 us  [exchange(): lax.all_to_all(rows.reshape(parts, MICRO * share, width), 'fsdp', split_a...]
    psum x1 -> x0, waiting for transfers between devices: 74.9 us -> none  [local(): lax.psum(for_sending(summed), 'dp')]
  transfers between devices with their start and end apart: 23 -> 64, of which waited for: 10 -> 19; matrix products, arithmetic and copies ran while one was open for 50% -> 17% of each run, Pallas kernels for 0% -> 23%
where the time goes in v1:
time: 773 us; the launch traced here: 766 us
  waiting for transfers between devices  288 us (37%)
  Pallas kernels  228 us (29%)
  other arithmetic  76.7 us (10%)
  starting transfers between devices  76 us (10%)
  local copies, waits for them, and re-layouts  56.8 us (7%)
  matrix products  22.5 us (3%)
  between operations  17.6 us (2%)
    ppermute x47, waiting for transfers between devices, move(): lax.ppermute(value, ('fsdp', 'dp'), [(here, here ^ flip) for here in rang...  190 us
    pallas_call x6, Pallas kernels, gram_blocks(): pl.pallas_call(partial(gram_kernel, tuple(firsts), rows), grid_spec=pltpu...  59.2 us
    convert_element_type x25, other arithmetic, summed(): return sum((term.astype(f32) for term in terms)).astype(bf16)  56.4 us
    ppermute x7, waiting for transfers between devices, gather_small(): rows.append(lax.ppermute(row, ('fsdp', 'dp'), pairs))  45.9 us
    ppermute x5, waiting for transfers between devices, sum_small(): lax.ppermute(value, ('fsdp', 'dp'), [(i, i ^ step) for i in range(32)])  44.2 us
    pallas_call x2, Pallas kernels, mixer_backward(): pl.pallas_call(mixer_backward_kernel, grid=(count,), in_specs=start + [co...  39 us
    pallas_call x2, Pallas kernels, mixer_forward(): pl.pallas_call(mixer_forward_kernel, grid=(count,), in_specs=start + rest...  37.4 us
    ppermute x47, starting transfers between devices, move(): lax.ppermute(value, ('fsdp', 'dp'), [(here, here ^ flip) for here in rang...  36.5 us
  transfers between devices with their start and end apart: 64, of which 19 were waited for; matrix products, arithmetic and copies ran while one was open for 17% of the time, Pallas kernels for 23%

profile of v1, /device:TPU:0, one launch (start us, length us, event | category | flops | bytes accessed | tf_op | source)
XLA Modules:
  0.0 765.8 jit_solution(8149892579566508011)
XLA Ops:
  29.6 3.0 convolution_convert_fusion.8
  32.6 6.5 all-to-all-start
  39.5 3.9 collective-permute-start.4
  45.4 49.8 %collective-permute-done.9.refs_7_.refs_15_ = bf16[64,6144]{1,0:T(8,128)(2,1)} collective-permute-done((bf16[64,6144]{1,0:T(8,128)(2,1)S(1)}, bf16[64,6144]{1,0:T(8,128)(2,1)}, u32[]{:S(2)}, u32[]{:S(2)}) %collective-permute-start.9) | collective-permute-done | bytes 786464 | tf_op jit(solution)/shard_map/ppermute | solution.py:299
  95.7 26.1 %collective-permute-done.4 = bf16[34,128]{1,0:T(8,128)(2,1)S(1)} collective-permute-done((bf16[34,128]{1,0:T(8,128)(2,1)S(1)}, bf16[34,128]{1,0:T(8,128)(2,1)S(1)}, u32[]{:S(2)}, u32[]{:S(2)}) %collective-permute-start.4) | collective-permute-done | bytes 8736 | tf_op jit(solution)/shard_map/ppermute | solution.py:318
  123.9 15.6 %collective-permute-done.5 = bf16[34,128]{1,0:T(8,128)(2,1)S(1)} collective-permute-done((bf16[34,128]{1,0:T(8,128)(2,1)S(1)}, bf16[34,128]{1,0:T(8,128)(2,1)S(1)}, u32[]{:S(2)}, u32[]{:S(2)}) %collective-permute-start.5) | collective-permute-done | bytes 8736 | tf_op jit(solution)/shard_map/ppermute | solution.py:318
  142.0 4.1 collective-permute-done.6
  157.0 60.6 %collective-permute-done.8.refs_0_.refs_8_ = bf16[64,6144]{1,0:T(8,128)(2,1)} collective-permute-done((bf16[64,6144]{1,0:T(8,128)(2,1)}, bf16[64,6144]{1,0:T(8,128)(2,1)}, u32[]{:S(2)}, u32[]{:S(2)}) %collective-permute-start.8) | collective-permute-done | bytes 786464 | tf_op jit(solution)/shard_map/ppermute | solution.py:299
  218.6 12.5 %collective-permute-done.11.refs_1_.refs_9_ = bf16[64,6144]{1,0:T(8,128)(2,1)} collective-permute-done((bf16[64,6144]{1,0:T(8,128)(2,1)}, bf16[64,6144]{1,0:T(8,128)(2,1)}, u32[]{:S(2)}, u32[]{:S(2)}) %collective-permute-start.11) | collective-permute-done | bytes 786464 | tf_op jit(solution)/shard_map/ppermute | solution.py:299
  235.1 17.6 %project.1.pq.pk.pv.og = f32[512,6144]{1,0:T(8,128)} custom-call(s32[16]{0:T(128)} %stack.102.units, bf16[512,1024]{1,0:T(8,128)(2,1)} %copy-done.4, bf16[64,6144]{1,0:T(8,128)(2,1)} %collective-permute-done.8.refs_0_.refs_8_, bf16[64,6144]{1,0:T(8,128)(2,1)} %collective-permute-done.11.refs_1_.refs_9_, ...), custom_call_target="tpu_custom_call" | custom-call | flops 16999999488 | bytes 51000000 | tf_op jit(solution)/shard_map/project/pallas_call | solution.py:437
  252.7 18.7 %mixer_forward.2 = (bf16[512,1024]{1,0:T(8,128)(2,1)}, bf16[4,512,256]{2,1,0:T(8,128)(2,1)}, bf16[4,512,256]{2,1,0:T(8,128)(2,1)}) custom-call(f32[512,6144]{1,0:T(8,128)} %project.1.pq.pk.pv.og, f32[512,6144]{1,0:T(8,128)} %project.1.pq.pk.pv.og, f32[512,6144]{1,0:T(8,128)} %project.1.pq.pk.pv.og, f32[512,6144]{1,0:T(8,128)} %project.1.pq.pk.pv.og, ...), custom_call_target="tpu_custom_call" | custom-call | flops 17600000000 | bytes 52800000 | tf_op jit(solution)/shard_map/mixer_forward/pallas_call | solution.py:234
  273.2 4.1 all-to-all-start.1
  277.3 18.7 %mixer_forward.3 = (bf16[512,1024]{1,0:T(8,128)(2,1)}, bf16[4,512,256]{2,1,0:T(8,128)(2,1)}, bf16[4,512,256]{2,1,0:T(8,128)(2,1)}) custom-call(f32[512,6144]{1,0:T(8,128)} %project.1.pq.pk.pv.og, f32[512,6144]{1,0:T(8,128)} %project.1.pq.pk.pv.og, f32[512,6144]{1,0:T(8,128)} %project.1.pq.pk.pv.og, f32[512,6144]{1,0:T(8,128)} %project.1.pq.pk.pv.og, ...), custom_call_target="tpu_custom_call" | custom-call | flops 17600000000 | bytes 52800000 | tf_op jit(solution)/shard_map/mixer_forward/pallas_call | solution.py:234
  296.0 7.6 all-to-all-done.1
  305.4 24.3 %ffn_forward.1 = (f32[512,1024]{1,0:T(8,128)}, bf16[512,1024]{1,0:T(8,128)(2,1)}, bf16[512,2816]{1,0:T(8,128)(2,1)}, bf16[512,2816]{1,0:T(8,128)(2,1)}, bf16[512...) custom-call(bf16[512,1024]{1,0:T(8,128)(2,1)} %get-tuple-element.105.gated, bf16[512,1024]{1,0:T(8,128)(2,1)} %get-tuple-element.106.more, ...), custom_call_target="tpu_custom_call" | custom-call | flops 27000000512 | bytes 81000000 | tf_op jit(solution)/shard_map/ffn_forward/pallas_call | solution.py:663
  329.7 4.6 copy.107
  334.3 9.3 %gram_blocks.6 = (bf16[8,64,3072]{2,1,0:T(8,128)(2,1)}, bf16[8,64,3072]{2,1,0:T(8,128)(2,1)}) custom-call(s32[16]{0:T(128)} %stack.102.units, bf16[2816,512]{1,0:T(8,128)(2,1)} %bitcast.188, bf16[512,1024]{1,0:T(8,128)(2,1)} %convolution_convert_fusion.5.refs_0_.cot), custom_call_target="tpu_custom_call" | custom-call | flops 9943393280 | bytes 29830180 | tf_op jit(solution)/shard_map/gram_blocks/pallas_call | solution.py:552
  350.3 5.2 add_convert_fusion.4
  356.9 31.2 %ffn_backward.1 = (bf16[512,2816]{1,0:T(8,128)(2,1)}, bf16[512,2816]{1,0:T(8,128)(2,1)}, f32[512,1024]{1,0:T(8,128)}, bf16[512,1024]{1,0:T(8,128)(2,1)}, f32[512,2048]{1,0:T(8,128)}, /*index=5*/f32[1,1024]{1,0:T(1,128)}) custom-call(bf16[512,1024]{1,0:T(8,128)(2,1)} %convolution_convert_fusion.5.refs_0_.cot, f32[512,1024]{1,0:T(8,128)} %get-tuple-element.116.residual, ...), custom_call_target="tpu_custom_call" | custom-call | flops 35000000512 | bytes 105000000 | tf_op jit(solution)/shard_map/ffn_backward/pallas_call | solution.py:735
  388.1 3.8 collective-permute-done.23
  394.8 7.2 gram_blocks.7
  402.0 11.7 %gram_blocks.8 = (bf16[8,64,4864]{2,1,0:T(8,128)(2,1)}, bf16[8,64,4864]{2,1,0:T(8,128)(2,1)}) custom-call(s32[16]{0:T(128)} %stack.102.units, bf16[1024,512]{1,0:T(8,128)(2,1)} %bitcast.190, bf16[512,2816]{1,0:T(8,128)(2,1)} %get-tuple-element.119.refs_0_, ...), custom_call_target="tpu_custom_call", output_to_operand_aliasing={{0}: (3, {}), {1}: (4, {})} | custom-call | flops 9943393280 | bytes 29830180 | tf_op jit(solution)/shard_map/gram_blocks/pallas_call | solution.py:552
  415.4 4.6 all-to-all-start.2
  422.0 11.6 %gram_blocks.9 = (bf16[8,64,2816]{2,1,0:T(8,128)(2,1)}, bf16[8,64,2816]{2,1,0:T(8,128)(2,1)}) custom-call(s32[16]{0:T(128)} %stack.102.units, bf16[1024,512]{1,0:T(8,128)(2,1)} %bitcast.191, bf16[512,2816]{1,0:T(8,128)(2,1)} %get-tuple-element.129.refs_0_), custom_call_target="tpu_custom_call" | custom-call | flops 9943393280 | bytes 29830180 | tf_op jit(solution)/shard_map/gram_blocks/pallas_call | solution.py:552
  433.6 23.3 %collective-permute-done.25 = bf16[2,64,3072]{2,1,0:T(8,128)(2,1)S(1)} collective-permute-done((bf16[2,64,3072]{2,1,0:T(8,128)(2,1)S(1)}, bf16[2,64,3072]{2,1,0:T(8,128)(2,1)S(1)}, u32[]{:S(2)}, u32[]{:S(2)}) %collective-permute-start.25) | collective-permute-done | bytes 786464 | tf_op jit(solution)/shard_map/ppermute | solution.py:299
  460.3 5.5 add_convert_fusion
  467.2 19.6 %mixer_backward.2 = (bf16[512,512]{1,0:T(8,128)(2,1)}, bf16[512,512]{1,0:T(8,128)(2,1)}, bf16[512,1024]{1,0:T(8,128)(2,1)}, bf16[512,1024]{1,0:T(8,128)(2,1)}, f...) custom-call(f32[512,6144]{1,0:T(8,128)} %project.1.pq.pk.pv.og, ...), custom_call_target="tpu_custom_call" | custom-call | flops 18400000000 | bytes 55200000 | tf_op jit(solution)/shard_map/mixer_backward/pallas_call | solution.py:252
  486.9 5.1 add_convert_fusion.6
  495.9 19.4 %mixer_backward.3 = (bf16[512,512]{1,0:T(8,128)(2,1)}, bf16[512,512]{1,0:T(8,128)(2,1)}, bf16[512,1024]{1,0:T(8,128)(2,1)}, bf16[512,1024]{1,0:T(8,128)(2,1)}, f...) custom-call(f32[512,6144]{1,0:T(8,128)} %project.1.pq.pk.pv.og, ...), custom_call_target="tpu_custom_call" | custom-call | flops 18400000000 | bytes 55200000 | tf_op jit(solution)/shard_map/mixer_backward/pallas_call | solution.py:252
  515.3 7.1 gram_blocks.10
  522.4 12.3 %gram_blocks.11 = (bf16[8,64,4096]{2,1,0:T(8,128)(2,1)}, bf16[8,64,4096]{2,1,0:T(8,128)(2,1)}) custom-call(s32[16]{0:T(128)} %stack.102.units, bf16[1024,512]{1,0:T(8,128)(2,1)} %copy.114.left_ref, bf16[512,1024]{1,0:T(8,128)(2,1)} %get-tuple-element.148.refs_0_.refs_4_, bf16[512,1024]{1,0:T(8,128)(2,1)} %get-tuple-element.149.refs_1_.refs_5_, ...), custom_call_target="tpu_custom_call" | custom-call | flops 14463117312 | bytes 43389352 | tf_op jit(solution)/shard_map/gram_blocks/pallas_call | solution.py:552
  559.6 3.9 reshape.399
  566.3 3.8 add_convert_fusion.8
  570.6 3.7 add_convert_fusion.12
  574.5 19.8 %back_project.1 = f32[512,1024]{1,0:T(8,128)} custom-call(s32[16]{0:T(128)} %stack.102.units, bf16[512,512]{1,0:T(8,128)(2,1)} %get-tuple-element.156.refs_0_, bf16[512,512]{1,0:T(8,128)(2,1)} %get-tuple-element.144.refs_1_, bf16[512,512]{1,0:T(8,128)(2,1)} %get-tuple-element.145.refs_2_, bf16[512,512]{1,0:T(8,128)(2,1)} %get-tuple-element.146.refs_3_, ...), custom_call_target="tpu_custom_call" | custom-call | flops 17999998976 | bytes 54000000 | tf_op jit(solution)/shard_map/back_project/pallas_call | solution.py:498
  603.8 5.2 add_convert_fusion.2
  619.1 13.0 %collective-permute-done.32 = bf16[64,4864]{1,0:T(8,128)(2,1)S(1)} collective-permute-done((bf16[64,4864]{1,0:T(8,128)(2,1)S(1)}, bf16[64,4864]{1,0:T(8,128)(2,1)S(1)}, u32[]{:S(2)}, u32[]{:S(2)}) %collective-permute-start.32) | collective-permute-done | bytes 622624 | tf_op jit(solution)/shard_map/ppermute | solution.py:299
  634.2 4.4 all-to-all-start.3
  638.7 3.0 fusion.8
  645.0 27.3 %collective-permute-done.42 = f32[8,4624]{1,0:T(8,128)S(1)} collective-permute-done((f32[8,4624]{1,0:T(8,128)S(1)}, f32[8,4624]{1,0:T(8,128)S(1)}, u32[]{:S(2)}, u32[]{:S(2)}) %collective-permute-start.42) | collective-permute-done | bytes 148000 | tf_op jit(solution)/shard_map/ppermute | solution.py:325
  673.3 4.2 collective-permute-done.43
  678.4 5.2 collective-permute-done.44
  687.4 7.5 collective-permute-done.45
  700.4 3.3 add_convert_fusion.10
  710.3 3.0 fusion.9
  726.5 7.5 collective-permute-done.51
  735.7 10.5 %collective-permute-done.52 = bf16[32,4096]{1,0:T(8,128)(2,1)S(1)} collective-permute-done((bf16[32,4096]{1,0:T(8,128)(2,1)S(1)}, bf16[32,4096]{1,0:T(8,128)(2,1)S(1)}, u32[]{:S(2)}, u32[]{:S(2)}) %collective-permute-start.52) | collective-permute-done | bytes 262176 | tf_op jit(solution)/shard_map/ppermute | solution.py:299
  746.6 6.9 collective-permute-done.54
  (405 shorter events, 161.4 us)
Async XLA Ops:
  7.3 298.1 %all-gather.2.cloned.1.call-start = ((), (), s32[]{:S(2)}) async-start(), calls=%async_computation.4 | async-start | bytes 22708224 | tf_op jit(solution)/shard_map/all_gather | solution.py:923
  19.3 20.2 %collective-permute-start = (bf16[34,128]{1,0:T(8,128)(2,1)S(1)}, bf16[34,128]{1,0:T(8,128)(2,1)S(1)}, u32[]{:S(2)}, u32[]{:S(2)}) collective-permute-start(bf16[34,128]{1,0:T(8,128)(2,1)S(1)} %bitcast.229), channel_id=1, source_target_pairs={{0,4},{1,5},{2,6},{3,7},{4,0},{5,1},{6,2},{7,3},{8,12},{9,13},{10,... | collective-permute-start | bytes 26120 | tf_op jit(solution)/shard_map/ppermute | solution.py:318
  22.3 21.1 %collective-permute-start.1 = (bf16[34,128]{1,0:T(8,128)(2,1)S(1)}, bf16[34,128]{1,0:T(8,128)(2,1)S(1)}, u32[]{:S(2)}, u32[]{:S(2)}) collective-permute-start(bf16[34,128]{1,0:T(8,128)(2,1)S(1)} %bitcast.230), channel_id=1, source_target_pairs={{0,8},{1,9},{2,10},{3,11},{4,12},{5,13},{6,14},{7,15},{8,0},{9,1},... | collective-permute-start | bytes 26120 | tf_op jit(solution)/shard_map/ppermute | solution.py:318
  23.8 21.0 %collective-permute-start.2 = (bf16[34,128]{1,0:T(8,128)(2,1)S(1)}, bf16[34,128]{1,0:T(8,128)(2,1)S(1)}, u32[]{:S(2)}, u32[]{:S(2)}) collective-permute-start(bf16[34,128]{1,0:T(8,128)(2,1)S(1)} %bitcast.231), channel_id=1, source_target_pairs={{0,12},{1,13},{2,14},{3,15},{4,8},{5,9},{6,10},{7,11},{8,4},{9,5},... | collective-permute-start | bytes 26120 | tf_op jit(solution)/shard_map/ppermute | solution.py:318
  23.8 21.6 %collective-permute-start.3 = (bf16[34,128]{1,0:T(8,128)(2,1)S(1)}, bf16[34,128]{1,0:T(8,128)(2,1)S(1)}, u32[]{:S(2)}, u32[]{:S(2)}) collective-permute-start(bf16[34,128]{1,0:T(8,128)(2,1)S(1)} %bitcast.232), channel_id=1, source_target_pairs={{0,16},{1,17},{2,18},{3,19},{4,20},{5,21},{6,22},{7,23},{8,24},{9,... | collective-permute-start | bytes 26120 | tf_op jit(solution)/shard_map/ppermute | solution.py:318
  26.9 68.3 %collective-permute-start.9 = (bf16[64,6144]{1,0:T(8,128)(2,1)S(1)}, bf16[64,6144]{1,0:T(8,128)(2,1)}, u32[]{:S(2)}, u32[]{:S(2)}) collective-permute-start(bf16[64,6144]{1,0:T(8,128)(2,1)S(1)} %fusion.12.refs_6_.refs_14_), channel_id=1, source_target_pairs={{0,16},{1,17},{2,18},{3,19},{4,20},{5,21},{6,22},{7,23},{8,24},{9,... | collective-permute-start | bytes 2359304 | tf_op jit(solution)/shard_map/ppermute | solution.py:299
  32.6 122.3 %all-to-all-start = ((bf16[8,64,1024]{2,1,0:T(8,128)(2,1)}), bf16[8,64,1024]{2,1,0:T(8,128)(2,1)}, u32[]{:S(2)}, u32[]{:S(2)}) async-start(bf16[8,64,1024]{2,1,0:T(8,128)(2,1)} %bitcast.21), calls=%async_computation | async-start | bytes 2097152 | tf_op jit(solution)/shard_map/all_to_all | solution.py:888
  39.5 82.3 %collective-permute-start.4 = (bf16[34,128]{1,0:T(8,128)(2,1)S(1)}, bf16[34,128]{1,0:T(8,128)(2,1)S(1)}, u32[]{:S(2)}, u32[]{:S(2)}) collective-permute-start(bf16[34,128]{1,0:T(8,128)(2,1)S(1)} %bitcast.233), channel_id=1, source_target_pairs={{0,20},{1,21},{2,22},{3,23},{4,16},{5,17},{6,18},{7,19},{8,28},{9,... | collective-permute-start | bytes 26120 | tf_op jit(solution)/shard_map/ppermute | solution.py:318
  43.4 104.6 %collective-permute-start.7 = (bf16[64,6144]{1,0:T(8,128)(2,1)S(1)}, bf16[64,6144]{1,0:T(8,128)(2,1)}, u32[]{:S(2)}, u32[]{:S(2)}) collective-permute-start(bf16[64,6144]{1,0:T(8,128)(2,1)S(1)} %fusion.12.refs_6_.refs_14_), channel_id=1, source_target_pairs={{0,8},{1,9},{2,10},{3,11},{4,12},{5,13},{6,14},{7,15},{8,0},{9,1},... | collective-permute-start | bytes 2359304 | tf_op jit(solution)/shard_map/ppermute | solution.py:299
  44.9 103.7 %collective-permute-start.12 = (bf16[64,6144]{1,0:T(8,128)(2,1)S(1)}, bf16[64,6144]{1,0:T(8,128)(2,1)}, u32[]{:S(2)}, u32[]{:S(2)}) collective-permute-start(bf16[64,6144]{1,0:T(8,128)(2,1)S(1)} %fusion.12.refs_6_.refs_14_), channel_id=1, source_target_pairs={{0,4},{1,5},{2,6},{3,7},{4,0},{5,1},{6,2},{7,3},{8,12},{9,13},{10,... | collective-permute-start | bytes 2359304 | tf_op jit(solution)/shard_map/ppermute | solution.py:299
  45.4 103.1 %collective-permute-start.20 = (bf16[64,6144]{1,0:T(8,128)(2,1)S(1)}, bf16[64,6144]{1,0:T(8,128)(2,1)S(1)}, u32[]{:S(2)}, u32[]{:S(2)}) collective-permute-start(bf16[64,6144]{1,0:T(8,128)(2,1)S(1)} %fusion.12.refs_6_.refs_14_), channel_id=1, source_target_pairs={{0,1},{1,0},{2,3},{3,2},{4,5},{5,4},{6,7},{7,6},{8,9},{9,8},{10,11... | collective-permute-start | bytes 2359304 | tf_op jit(solution)/shard_map/ppermute | solution.py:299
  95.2 53.9 %collective-permute-start.10 = (bf16[64,6144]{1,0:T(8,128)(2,1)}, bf16[64,6144]{1,0:T(8,128)(2,1)}, u32[]{:S(2)}, u32[]{:S(2)}) collective-permute-start(bf16[64,6144]{1,0:T(8,128)(2,1)} %collective-permute-done.9.refs_7_.refs_15_), channel_id=1, source_target_pairs={{0,8},{1,9},{2,10},{3,11},{4,12},{5,13},{6,14},{7,15},{8,0},{9,1},... | collective-permute-start | bytes 2359304 | tf_op jit(solution)/shard_map/ppermute | solution.py:299
  121.8 17.8 %collective-permute-start.5 = (bf16[34,128]{1,0:T(8,128)(2,1)S(1)}, bf16[34,128]{1,0:T(8,128)(2,1)S(1)}, u32[]{:S(2)}, u32[]{:S(2)}) collective-permute-start(bf16[34,128]{1,0:T(8,128)(2,1)S(1)} %bitcast.234), channel_id=1, source_target_pairs={{0,24},{1,25},{2,26},{3,27},{4,28},{5,29},{6,30},{7,31},{8,16},{9,... | collective-permute-start | bytes 26120 | tf_op jit(solution)/shard_map/ppermute | solution.py:318
  146.5 71.2 %collective-permute-start.13 = (bf16[64,6144]{1,0:T(8,128)(2,1)}, bf16[64,6144]{1,0:T(8,128)(2,1)}, u32[]{:S(2)}, u32[]{:S(2)}) collective-permute-start(bf16[64,6144]{1,0:T(8,128)(2,1)} %collective-permute-done.9.refs_7_.refs_15_), channel_id=1, source_target_pairs={{0,4},{1,5},{2,6},{3,7},{4,0},{5,1},{6,2},{7,3},{8,12},{9,13},{10,... | collective-permute-start | bytes 2359304 | tf_op jit(solution)/shard_map/ppermute | solution.py:299
  148.0 69.6 %collective-permute-start.8 = (bf16[64,6144]{1,0:T(8,128)(2,1)}, bf16[64,6144]{1,0:T(8,128)(2,1)}, u32[]{:S(2)}, u32[]{:S(2)}) collective-permute-start(bf16[64,6144]{1,0:T(8,128)(2,1)} %collective-permute-done.7.refs_4_.refs_12_), channel_id=1, source_target_pairs={{0,4},{1,5},{2,6},{3,7},{4,0},{5,1},{6,2},{7,3},{8,12},{9,13},{10,... | collective-permute-start | bytes 2359304 | tf_op jit(solution)/shard_map/ppermute | solution.py:299
  148.6 69.7 %collective-permute-start.18 = (bf16[64,6144]{1,0:T(8,128)(2,1)}, bf16[64,6144]{1,0:T(8,128)(2,1)}, u32[]{:S(2)}, u32[]{:S(2)}) collective-permute-start(bf16[64,6144]{1,0:T(8,128)(2,1)} %collective-permute-done.7.refs_4_.refs_12_), channel_id=1, source_target_pairs={{0,1},{1,0},{2,3},{3,2},{4,5},{5,4},{6,7},{7,6},{8,9},{9,8},{10,11... | collective-permute-start | bytes 2359304 | tf_op jit(solution)/shard_map/ppermute | solution.py:299
  148.6 69.6 %collective-permute-start.16 = (bf16[64,6144]{1,0:T(8,128)(2,1)}, bf16[64,6144]{1,0:T(8,128)(2,1)}, u32[]{:S(2)}, u32[]{:S(2)}) collective-permute-start(bf16[64,6144]{1,0:T(8,128)(2,1)} %collective-permute-done.12.refs_2_.refs_10_), channel_id=1, source_target_pairs={{0,1},{1,0},{2,3},{3,2},{4,5},{5,4},{6,7},{7,6},{8,9},{9,8},{10,11... | collective-permute-start | bytes 2359304 | tf_op jit(solution)/shard_map/ppermute | solution.py:299
  149.1 82.1 %collective-permute-start.11 = (bf16[64,6144]{1,0:T(8,128)(2,1)}, bf16[64,6144]{1,0:T(8,128)(2,1)}, u32[]{:S(2)}, u32[]{:S(2)}) collective-permute-start(bf16[64,6144]{1,0:T(8,128)(2,1)} %collective-permute-done.10.refs_5_.refs_13_), channel_id=1, source_target_pairs={{0,4},{1,5},{2,6},{3,7},{4,0},{5,1},{6,2},{7,3},{8,12},{9,13},{10,... | collective-permute-start | bytes 2359304 | tf_op jit(solution)/shard_map/ppermute | solution.py:299
  217.6 17.5 %collective-permute-start.21 = (bf16[64,6144]{1,0:T(8,128)(2,1)}, bf16[64,6144]{1,0:T(8,128)(2,1)}, u32[]{:S(2)}, u32[]{:S(2)}) collective-permute-start(bf16[64,6144]{1,0:T(8,128)(2,1)} %collective-permute-done.9.refs_7_.refs_15_), channel_id=1, source_target_pairs={{0,1},{1,0},{2,3},{3,2},{4,5},{5,4},{6,7},{7,6},{8,9},{9,8},{10,11... | collective-permute-start | bytes 2359304 | tf_op jit(solution)/shard_map/ppermute | solution.py:299
  217.6 17.5 %collective-permute-start.19 = (bf16[64,6144]{1,0:T(8,128)(2,1)}, bf16[64,6144]{1,0:T(8,128)(2,1)}, u32[]{:S(2)}, u32[]{:S(2)}) collective-permute-start(bf16[64,6144]{1,0:T(8,128)(2,1)} %collective-permute-done.10.refs_5_.refs_13_), channel_id=1, source_target_pairs={{0,1},{1,0},{2,3},{3,2},{4,5},{5,4},{6,7},{7,6},{8,9},{9,8},{10,11... | collective-permute-start | bytes 2359304 | tf_op jit(solution)/shard_map/ppermute | solution.py:299
  218.1 17.0 %collective-permute-start.14 = (bf16[64,6144]{1,0:T(8,128)(2,1)}, bf16[64,6144]{1,0:T(8,128)(2,1)}, u32[]{:S(2)}, u32[]{:S(2)}) collective-permute-start(bf16[64,6144]{1,0:T(8,128)(2,1)} %collective-permute-done.8.refs_0_.refs_8_), channel_id=1, source_target_pairs={{0,1},{1,0},{2,3},{3,2},{4,5},{5,4},{6,7},{7,6},{8,9},{9,8},{10,11... | collective-permute-start | bytes 2359304 | tf_op jit(solution)/shard_map/ppermute | solution.py:299
  218.2 16.9 %collective-permute-start.17 = (bf16[64,6144]{1,0:T(8,128)(2,1)}, bf16[64,6144]{1,0:T(8,128)(2,1)}, u32[]{:S(2)}, u32[]{:S(2)}) collective-permute-start(bf16[64,6144]{1,0:T(8,128)(2,1)} %collective-permute-done.13.refs_3_.refs_11_), channel_id=1, source_target_pairs={{0,1},{1,0},{2,3},{3,2},{4,5},{5,4},{6,7},{7,6},{8,9},{9,8},{10,11... | collective-permute-start | bytes 2359304 | tf_op jit(solution)/shard_map/ppermute | solution.py:299
  273.2 30.4 %all-to-all-start.1 = ((bf16[8,64,1024]{2,1,0:T(8,128)(2,1)}), bf16[8,64,1024]{2,1,0:T(8,128)(2,1)S(1)}, u32[]{:S(2)}, u32[]{:S(2)}) async-start(bf16[8,64,1024]{2,1,0:T(8,128)(2,1)} %bitcast.36), calls=%async_computation.1 | async-start | bytes 2097152 | tf_op jit(solution)/shard_map/all_to_all | solution.py:888
  355.5 36.5 %collective-permute-start.23 = (bf16[4,64,3072]{2,1,0:T(8,128)(2,1)}, bf16[4,64,3072]{2,1,0:T(8,128)(2,1)}, u32[]{:S(2)}, u32[]{:S(2)}) collective-permute-start(bf16[4,64,3072]{2,1,0:T(8,128)(2,1)} %get-tuple-element.261), channel_id=1, source_target_pairs={{0,4},{1,5},{2,6},{3,7},{4,0},{5,1},{6,2},{7,3},{8,12},{9,13},{10,... | collective-permute-start | bytes 4718600 | tf_op jit(solution)/shard_map/ppermute | solution.py:299
  413.7 46.7 %collective-permute-start.24 = (bf16[8,64,4864]{2,1,0:T(8,128)(2,1)}, bf16[8,64,4864]{2,1,0:T(8,128)(2,1)}, u32[]{:S(2)}, u32[]{:S(2)}) collective-permute-start(bf16[8,64,4864]{2,1,0:T(8,128)(2,1)} %get-tuple-element.127), channel_id=1, source_target_pairs={{0,1},{1,0},{2,3},{3,2},{4,5},{5,4},{6,7},{7,6},{8,9},{9,8},{10,11... | collective-permute-start | bytes 14942216 | tf_op jit(solution)/shard_map/ppermute | solution.py:299
  415.4 218.8 %all-to-all-start.2 = ((bf16[8,64,1024]{2,1,0:T(8,128)(2,1)}), bf16[8,64,1024]{2,1,0:T(8,128)(2,1)}, u32[]{:S(2)}, u32[]{:S(2)}) async-start(bf16[8,64,1024]{2,1,0:T(8,128)(2,1)} %bitcast.189), calls=%async_computation.2 | async-start | bytes 2097152 | tf_op jit(solution)/shard_map/all_to_all | solution.py:888
  420.0 36.9 %collective-permute-start.25 = (bf16[2,64,3072]{2,1,0:T(8,128)(2,1)S(1)}, bf16[2,64,3072]{2,1,0:T(8,128)(2,1)S(1)}, u32[]{:S(2)}, u32[]{:S(2)}) collective-permute-start(bf16[2,64,3072]{2,1,0:T(8,128)(2,1)S(1)} %copy-done.25), channel_id=1, source_target_pairs={{0,8},{1,9},{2,10},{3,11},{4,12},{5,13},{6,14},{7,15},{8,0},{9,1},... | collective-permute-start | bytes 2359304 | tf_op jit(solution)/shard_map/ppermute | solution.py:299
  433.6 53.3 %collective-permute-start.28 = (bf16[8,64,2816]{2,1,0:T(8,128)(2,1)}, bf16[8,64,2816]{2,1,0:T(8,128)(2,1)}, u32[]{:S(2)}, u32[]{:S(2)}) collective-permute-start(bf16[8,64,2816]{2,1,0:T(8,128)(2,1)} %get-tuple-element.130), channel_id=1, source_target_pairs={{0,1},{1,0},{2,3},{3,2},{4,5},{5,4},{6,7},{7,6},{8,9},{9,8},{10,11... | collective-permute-start | bytes 8650760 | tf_op jit(solution)/shard_map/ppermute | solution.py:299
  457.8 35.5 %collective-permute-start.27 = (bf16[64,3072]{1,0:T(8,128)(2,1)}, bf16[64,3072]{1,0:T(8,128)(2,1)}, u32[]{:S(2)}, u32[]{:S(2)}) collective-permute-start(bf16[64,3072]{1,0:T(8,128)(2,1)} %fusion.25), channel_id=1, source_target_pairs={{0,16},{1,17},{2,18},{3,19},{4,20},{5,21},{6,22},{7,23},{8,24},{9,... | collective-permute-start | bytes 1179656 | tf_op jit(solution)/shard_map/ppermute | solution.py:299
  465.8 100.5 %collective-permute-start.26 = (bf16[4,64,4864]{2,1,0:T(8,128)(2,1)}, bf16[4,64,4864]{2,1,0:T(8,128)(2,1)}, u32[]{:S(2)}, u32[]{:S(2)}) collective-permute-start(bf16[4,64,4864]{2,1,0:T(8,128)(2,1)} %get-tuple-element.256), channel_id=1, source_target_pairs={{0,4},{1,5},{2,6},{3,7},{4,0},{5,1},{6,2},{7,3},{8,12},{9,13},{10,... | collective-permute-start | bytes 7471112 | tf_op jit(solution)/shard_map/ppermute | solution.py:299
  492.0 102.4 %collective-permute-start.30 = (bf16[8,32,2816]{2,1,0:T(8,128)(2,1)}, bf16[8,32,2816]{2,1,0:T(8,128)(2,1)}, u32[]{:S(2)}, u32[]{:S(2)}) collective-permute-start(bf16[8,32,2816]{2,1,0:T(8,128)(2,1)} %get-tuple-element.263), channel_id=1, source_target_pairs={{0,2},{1,3},{2,0},{3,1},{4,6},{5,7},{6,4},{7,5},{8,10},{9,11},{10,... | collective-permute-start | bytes 4325384 | tf_op jit(solution)/shard_map/ppermute | solution.py:299
  495.2 115.1 %collective-permute-start.35 = (bf16[64,3072]{1,0:T(8,128)(2,1)}, bf16[64,3072]{1,0:T(8,128)(2,1)}, u32[]{:S(2)}, u32[]{:S(2)}) collective-permute-start(bf16[64,3072]{1,0:T(8,128)(2,1)} %fusion.13), channel_id=1, source_target_pairs={{0,2},{1,3},{2,0},{3,1},{4,6},{5,7},{6,4},{7,5},{8,10},{9,11},{10,... | collective-permute-start | bytes 1179656 | tf_op jit(solution)/shard_map/ppermute | solution.py:299
  522.4 48.2 %collective-permute-start.31 = (bf16[8,64,2048]{2,1,0:T(8,128)(2,1)}, bf16[8,64,2048]{2,1,0:T(8,128)(2,1)}, u32[]{:S(2)}, u32[]{:S(2)}) collective-permute-start(bf16[8,64,2048]{2,1,0:T(8,128)(2,1)} %get-tuple-element.147), channel_id=1, source_target_pairs={{0,1},{1,0},{2,3},{3,2},{4,5},{5,4},{6,7},{7,6},{8,9},{9,8},{10,11... | collective-permute-start | bytes 6291464 | tf_op jit(solution)/shard_map/ppermute | solution.py:299
  540.8 63.0 %collective-permute-start.36 = (bf16[8,64,4096]{2,1,0:T(8,128)(2,1)}, bf16[8,64,4096]{2,1,0:T(8,128)(2,1)}, u32[]{:S(2)}, u32[]{:S(2)}) collective-permute-start(bf16[8,64,4096]{2,1,0:T(8,128)(2,1)} %get-tuple-element.152), channel_id=1, source_target_pairs={{0,1},{1,0},{2,3},{3,2},{4,5},{5,4},{6,7},{7,6},{8,9},{9,8},{10,11... | collective-permute-start | bytes 12582920 | tf_op jit(solution)/shard_map/ppermute | solution.py:299
  570.1 30.2 %collective-permute-start.29 = (bf16[2,64,4864]{2,1,0:T(8,128)(2,1)}, bf16[2,64,4864]{2,1,0:T(8,128)(2,1)}, u32[]{:S(2)}, u32[]{:S(2)}) collective-permute-start(bf16[2,64,4864]{2,1,0:T(8,128)(2,1)} %get-tuple-element.264), channel_id=1, source_target_pairs={{0,8},{1,9},{2,10},{3,11},{4,12},{5,13},{6,14},{7,15},{8,0},{9,1},... | collective-permute-start | bytes 3735560 | tf_op jit(solution)/shard_map/ppermute | solution.py:299
  574.2 39.2 %collective-permute-start.34 = (bf16[4,64,2048]{2,1,0:T(8,128)(2,1)}, bf16[4,64,2048]{2,1,0:T(8,128)(2,1)}, u32[]{:S(2)}, u32[]{:S(2)}) collective-permute-start(bf16[4,64,2048]{2,1,0:T(8,128)(2,1)} %get-tuple-element.269), channel_id=1, source_target_pairs={{0,4},{1,5},{2,6},{3,7},{4,0},{5,1},{6,2},{7,3},{8,12},{9,13},{10,... | collective-permute-start | bytes 3145736 | tf_op jit(solution)/shard_map/ppermute | solution.py:299
  596.3 20.5 %collective-permute-start.33 = (bf16[4,32,2816]{2,1,0:T(8,128)(2,1)S(1)}, bf16[4,32,2816]{2,1,0:T(8,128)(2,1)S(1)}, u32[]{:S(2)}, u32[]{:S(2)}) collective-permute-start(bf16[4,32,2816]{2,1,0:T(8,128)(2,1)S(1)} %get-tuple-element.273), channel_id=1, source_target_pairs={{0,4},{1,5},{2,6},{3,7},{4,0},{5,1},{6,2},{7,3},{8,12},{9,13},{10,... | collective-permute-start | bytes 2162696 | tf_op jit(solution)/shard_map/ppermute | solution.py:299
  602.5 29.5 %collective-permute-start.32 = (bf16[64,4864]{1,0:T(8,128)(2,1)S(1)}, bf16[64,4864]{1,0:T(8,128)(2,1)S(1)}, u32[]{:S(2)}, u32[]{:S(2)}) collective-permute-start(bf16[64,4864]{1,0:T(8,128)(2,1)S(1)} %fusion.14), channel_id=1, source_target_pairs={{0,16},{1,17},{2,18},{3,19},{4,20},{5,21},{6,22},{7,23},{8,24},{9,... | collective-permute-start | bytes 1867784 | tf_op jit(solution)/shard_map/ppermute | solution.py:299
  609.0 91.4 %collective-permute-start.39 = (bf16[8,32,4096]{2,1,0:T(8,128)(2,1)}, bf16[8,32,4096]{2,1,0:T(8,128)(2,1)}, u32[]{:S(2)}, u32[]{:S(2)}) collective-permute-start(bf16[8,32,4096]{2,1,0:T(8,128)(2,1)} %get-tuple-element.259), channel_id=1, source_target_pairs={{0,2},{1,3},{2,0},{3,1},{4,6},{5,7},{6,4},{7,5},{8,10},{9,11},{10,... | collective-permute-start | bytes 6291464 | tf_op jit(solution)/shard_map/ppermute | solution.py:299
  611.5 31.6 %collective-permute-start.58 = (bf16[64,3072]{1,0:T(8,128)(2,1)S(1)}, bf16[64,3072]{1,0:T(8,128)(2,1)}, u32[]{:S(2)}, u32[]{:S(2)}) collective-permute-start(bf16[64,3072]{1,0:T(8,128)(2,1)S(1)} %add_convert_fusion.24), channel_id=1, source_target_pairs={{0,1},{1,0},{2,3},{3,2},{4,5},{5,4},{6,7},{7,6},{8,9},{9,8},{10,11... | collective-permute-start | bytes 1179656 | tf_op jit(solution)/shard_map/ppermute | solution.py:299
  616.0 79.0 %collective-permute-start.40 = (bf16[2,64,2048]{2,1,0:T(8,128)(2,1)}, bf16[2,64,2048]{2,1,0:T(8,128)(2,1)}, u32[]{:S(2)}, u32[]{:S(2)}) collective-permute-start(bf16[2,64,2048]{2,1,0:T(8,128)(2,1)} %get-tuple-element.279), channel_id=1, source_target_pairs={{0,8},{1,9},{2,10},{3,11},{4,12},{5,13},{6,14},{7,15},{8,0},{9,1},... | collective-permute-start | bytes 1572872 | tf_op jit(solution)/shard_map/ppermute | solution.py:299
  617.9 86.4 %collective-permute-start.38 = (bf16[2,32,2816]{2,1,0:T(8,128)(2,1)}, bf16[2,32,2816]{2,1,0:T(8,128)(2,1)}, u32[]{:S(2)}, u32[]{:S(2)}) collective-permute-start(bf16[2,32,2816]{2,1,0:T(8,128)(2,1)} %get-tuple-element.281), channel_id=1, source_target_pairs={{0,8},{1,9},{2,10},{3,11},{4,12},{5,13},{6,14},{7,15},{8,0},{9,1},... | collective-permute-start | bytes 1081352 | tf_op jit(solution)/shard_map/ppermute | solution.py:299
  634.2 76.1 %all-to-all-start.3 = ((bf16[8,64,1024]{2,1,0:T(8,128)(2,1)}), bf16[8,64,1024]{2,1,0:T(8,128)(2,1)}, u32[]{:S(2)}, u32[]{:S(2)}) async-start(bf16[8,64,1024]{2,1,0:T(8,128)(2,1)} %bitcast.58), calls=%async_computation.3 | async-start | bytes 2097152 | tf_op jit(solution)/shard_map/all_to_all | solution.py:888
  641.7 67.1 %collective-permute-start.37 = (bf16[64,4864]{1,0:T(8,128)(2,1)}, bf16[64,4864]{1,0:T(8,128)(2,1)}, u32[]{:S(2)}, u32[]{:S(2)}) collective-permute-start(bf16[64,4864]{1,0:T(8,128)(2,1)} %fusion.10), channel_id=1, source_target_pairs={{0,2},{1,3},{2,0},{3,1},{4,6},{5,7},{6,4},{7,5},{8,10},{9,11},{10,... | collective-permute-start | bytes 1867784 | tf_op jit(solution)/shard_map/ppermute | solution.py:299
  643.1 29.1 %collective-permute-start.42 = (f32[8,4624]{1,0:T(8,128)S(1)}, f32[8,4624]{1,0:T(8,128)S(1)}, u32[]{:S(2)}, u32[]{:S(2)}) collective-permute-start(f32[8,4624]{1,0:T(8,128)S(1)} %add.467), channel_id=1, source_target_pairs={{0,2},{1,3},{2,0},{3,1},{4,6},{5,7},{6,4},{7,5},{8,10},{9,11},{10,... | collective-permute-start | bytes 443912 | tf_op jit(solution)/shard_map/ppermute | solution.py:325
  696.7 16.6 %collective-permute-start.46 = (bf16[64,2048]{1,0:T(8,128)(2,1)}, bf16[64,2048]{1,0:T(8,128)(2,1)}, u32[]{:S(2)}, u32[]{:S(2)}) collective-permute-start(bf16[64,2048]{1,0:T(8,128)(2,1)} %fusion.27), channel_id=1, source_target_pairs={{0,16},{1,17},{2,18},{3,19},{4,20},{5,21},{6,22},{7,23},{8,24},{9,... | collective-permute-start | bytes 786440 | tf_op jit(solution)/shard_map/ppermute | solution.py:299
  705.9 18.0 %collective-permute-start.48 = (bf16[32,2816]{1,0:T(8,128)(2,1)}, bf16[32,2816]{1,0:T(8,128)(2,1)}, u32[]{:S(2)}, u32[]{:S(2)}) collective-permute-start(bf16[32,2816]{1,0:T(8,128)(2,1)} %fusion.33), channel_id=1, source_target_pairs={{0,16},{1,17},{2,18},{3,19},{4,20},{5,21},{6,22},{7,23},{8,24},{9,... | collective-permute-start | bytes 540680 | tf_op jit(solution)/shard_map/ppermute | solution.py:299
  726.4 20.0 %collective-permute-start.50 = (bf16[64,2048]{1,0:T(8,128)(2,1)S(1)}, bf16[64,2048]{1,0:T(8,128)(2,1)S(1)}, u32[]{:S(2)}, u32[]{:S(2)}) collective-permute-start(bf16[64,2048]{1,0:T(8,128)(2,1)S(1)} %add_convert_fusion.29), channel_id=1, source_target_pairs={{0,1},{1,0},{2,3},{3,2},{4,5},{5,4},{6,7},{7,6},{8,9},{9,8},{10,11... | collective-permute-start | bytes 786440 | tf_op jit(solution)/shard_map/ppermute | solution.py:299
  (79 other events, 1526.9 us)
Sparse Core Ops, SparseCore 0:
  17.8 228.0 all-gather.1

commit v2 on v1

--- a/solution.py
+++ b/solution.py
@@ -87,7 +87,7 @@
 
 
 def mixer_forward_kernel(
-    pq, pk, pv, og, col, row, wq, wk, wv, gain, gated_ref, inverse_ref, pseudo_ref
+    pq, pk, pv, og, col, row, wq, wk, wv, gain, gated_ref, turned_ref, inverse_ref, pseudo_ref
 ):
     position = col[0, :, 3:4]
     query, key, value = (
@@ -117,9 +117,9 @@
         heads_out = mm(attend, pseudo)
         scale = lax.rsqrt(jnp.mean(heads_out * heads_out, axis=1, keepdims=True) + norm_eps)
         gate = og[rows]
-        gated_ref[rows] = (
-            heads_out * scale * gain[...] * (gate * jax.nn.sigmoid(gate))
-        ).astype(bf16)
+        gated = heads_out * scale * gain[...] * (gate * jax.nn.sigmoid(gate))
+        gated_ref[rows] = gated.astype(bf16)
+        turned_ref[:, rows] = gated.T.astype(bf16)
 
 
 def silu_back(pre, sig):
@@ -235,9 +235,15 @@
         mixer_forward_kernel,
         grid=(count,),
         in_specs=start + rest,
-        out_specs=[columns(DV, 0), per_head(ROWS, MB_TOK), per_head(ROWS, DV)],
+        out_specs=[
+            columns(DV, 0),
+            pl.BlockSpec((DV, ROWS), lambda head: (head, 0)),
+            per_head(ROWS, MB_TOK),
+            per_head(ROWS, DV),
+        ],
         out_shape=[
             jax.ShapeDtypeStruct((ROWS, count * DV), bf16),
+            jax.ShapeDtypeStruct((count * DV, ROWS), bf16),
             jax.ShapeDtypeStruct((count, ROWS, MB_TOK), bf16),
             jax.ShapeDtypeStruct((count, ROWS, DV), bf16),
         ],
@@ -299,33 +305,24 @@
         return lax.ppermute(value, ("fsdp", "dp"), [(here, here ^ flip) for here in range(32)])
 
     def units(self):
-        own, other = [], []
-        for dz, dx in BLOCKS:
-            base = ((self.z ^ dz) * 2 + (self.x ^ dx)) * 2
-            own.append(base + self.core)
-            other.append(base + 1 - self.core)
-        return jnp.stack(own + other).astype(jnp.int32)
+        dz, dx = (jnp.asarray([at[i] for at in BLOCKS], jnp.int32) for i in (0, 1))
+        base = ((self.z ^ dz) * 2 + (self.x ^ dx)) * 2
+        return jnp.concatenate([base + self.core, base + 1 - self.core])
+
+    def mine(self, half):
+        rows = half.shape[0] // 2
+        return lax.dynamic_slice_in_dim(half, self.y * rows, rows, 0)
+
+    def join(self, mine, other):
+        first = self.y == 0
+        return jnp.concatenate(
+            [jnp.where(first, mine, other), jnp.where(first, other, mine)], axis=0
+        )
 
     def half(self, shard):
         rows = shard.shape[0] // 2
         return lax.dynamic_slice_in_dim(shard, self.core * rows, rows, 0)
 
-    def gather_small(self, row):
-        fsdp = self.z * 2 + self.x
-        rows = [row]
-        for step in range(1, 8):
-            pairs = [(i, (i // 4 ^ step) * 4 + i % 4) for i in range(32)]
-            rows.append(lax.ppermute(row, ("fsdp", "dp"), pairs))
-        place = jnp.arange(8, dtype=jnp.int32)
-        picks = (place[:, None] ^ place[None, :]) == fsdp
-        return exact(picks.astype(bf16), jnp.stack(rows).reshape(8, -1)).astype(bf16)
-
-    def sum_small(self, value):
-        for step in (1, 2, 4, 8, 16):
-            value = value + lax.ppermute(value, ("fsdp", "dp"), [(i, i ^ step) for i in range(32)])
-        return value
-
-
 def after(value, *others):
     return lax.optimization_barrier((value,) + others)[0]
 
@@ -334,12 +331,22 @@
     return sum(term.astype(f32) for term in terms).astype(bf16)
 
 
-def gather_blocks(plane, half):
-    got = {(0, 0): half, (1, 0): plane.move(half, dz=1), (2, 0): plane.move(half, dz=2)}
-    got[3, 0] = plane.move(got[2, 0], dz=1)
-    for dz in range(4):
-        got[dz, 1] = plane.move(got[dz, 0], dx=1)
-    return [got[at] for at in BLOCKS] + [plane.move(got[at], dc=1) for at in BLOCKS]
+class Gather:
+    def __init__(self, plane, held):
+        self.plane = plane
+        self.got = {(0, 0): held}
+        self.from_core = {}
+
+    def pass_to(self, new, old, **step):
+        self.got[new] = self.plane.move(self.got[old], **step)
+
+    def share(self, *blocks):
+        for at in blocks:
+            self.from_core[at] = self.plane.move(self.got[at], dc=1)
+
+    def wait(self, blocks, *others):
+        for at in blocks:
+            self.got[at] = after(self.got[at], *others)
 
 
 class Reduce:
@@ -412,7 +419,7 @@
 
 def cost(us):
     return pl.CostEstimate(
-        flops=int(us * 1.0e9), transcendentals=0, bytes_accessed=int(us * 3.0e6)
+        flops=int(us * 1.0e7), transcendentals=0, bytes_accessed=int(us * 3.0e4)
     )
 
 
@@ -598,12 +605,13 @@
 def late_specs(depth, wide):
     fixed = dict(pipeline_mode=pl.Buffered(1))
     gate = 5 * depth // FTILE
+    up = gate + wide // FTILE
     return [
         pl.BlockSpec((32 * PART, 3 * depth), lambda n: (0, 0), **fixed),
         pl.BlockSpec((32 * PART, depth), lambda n: (0, 3), **fixed),
         pl.BlockSpec((32 * PART, depth), lambda n: (0, 4), **fixed),
         pl.BlockSpec((32 * PART, FTILE), lambda n: (0, gate + n)),
-        pl.BlockSpec((32 * PART, FTILE), lambda n: (0, gate + wide // FTILE + n)),
+        pl.BlockSpec((32 * PART, FTILE), lambda n: (0, up + n)),
     ]
 
 
@@ -621,7 +629,7 @@
 
 def ffn_forward_kernel(
     gated, more, x, gain, down, out_first, out_second, w_gate, w_up,
-    residual, ffn_low, gate_act, up_act, hidden, result, w_out, w_down, total,
+    residual, ffn_turned, gate_act, up_act, hidden_turned, result, w_out, w_down, total, ffn_low,
 ):
     step = pl.program_id(0)
 
@@ -635,14 +643,17 @@
         residual[...] = value
         total[...] = value
         scale = lax.rsqrt(jnp.mean(value * value, axis=1, keepdims=True) + norm_eps)
-        ffn_low[...] = (value * scale * gain[...]).astype(bf16)
+        normed = value * scale * gain[...]
+        ffn_low[...] = normed.astype(bf16)
+        ffn_turned[...] = normed.T.astype(bf16)
 
     gate = jnp.dot(ffn_low[...], w_gate[...], preferred_element_type=f32)
     up = jnp.dot(ffn_low[...], w_up[...], preferred_element_type=f32)
     gate_act[...] = gate.astype(bf16)
     up_act[...] = up.astype(bf16)
-    low = (gate * jax.nn.sigmoid(gate) * up).astype(bf16)
-    hidden[...] = low
+    hidden = gate * jax.nn.sigmoid(gate) * up
+    hidden_turned[...] = hidden.T.astype(bf16)
+    low = hidden.astype(bf16)
     total[...] += jnp.dot(
         low, w_down[pl.ds(pl.multiple_of(step * FTILE, FTILE), FTILE), :],
         preferred_element_type=f32,
@@ -666,19 +677,27 @@
             num_scalar_prefetch=0,
             grid=(wide // FTILE,),
             in_specs=[still(gated), still(more), still(x), still(gain)] + late_specs(depth, wide),
-            out_specs=[whole, whole, tile, tile, tile, whole],
+            out_specs=[
+                whole,
+                pl.BlockSpec((depth, rows), lambda n: (0, 0)),
+                tile,
+                tile,
+                pl.BlockSpec((FTILE, rows), lambda n: (n, 0)),
+                whole,
+            ],
             scratch_shapes=[
                 pltpu.VMEM((tall, depth), bf16),
                 pltpu.VMEM((wide, depth), bf16),
                 pltpu.VMEM((rows, depth), f32),
+                pltpu.VMEM((rows, depth), bf16),
             ],
         ),
         out_shape=[
             jax.ShapeDtypeStruct((rows, depth), f32),
-            jax.ShapeDtypeStruct((rows, depth), bf16),
+            jax.ShapeDtypeStruct((depth, rows), bf16),
             jax.ShapeDtypeStruct((rows, wide), bf16),
             jax.ShapeDtypeStruct((rows, wide), bf16),
-            jax.ShapeDtypeStruct((rows, wide), bf16),
+            jax.ShapeDtypeStruct((wide, rows), bf16),
             jax.ShapeDtypeStruct((rows, depth), bf16),
         ],
         name="ffn_forward",
@@ -899,37 +918,73 @@
     def gram(left, right):
         return exact(left, right, TN).astype(bf16)
 
-    small = (gain_mix, gain_ffn, w_gates, conv_weight)
+    small = (gain_mix, gain_ffn, w_gates, conv_weight.T)
     packed = jnp.concatenate([item.reshape(-1) for item in small])
-    if plane:
-        packed = plane.gather_small(packed.reshape(-1, 128))
-    else:
-        packed = lax.all_gather(packed, "fsdp", axis=0, tiled=False)
-    packed = packed.reshape(parts, -1)
-    full, start = [], 0
-    for item in small:
-        piece = packed[:, start : start + item.size]
-        full.append(piece.reshape((parts * item.shape[0],) + item.shape[1:]))
-        start += item.size
-    full_gain_mix, full_gain_ffn = full[0].astype(f32), full[1].astype(f32)
-    full_gates, taps = full[2], full[3].astype(f32).T
-
-    local_x = select_rows(arrange, exchange(select_rows(send, tokens[0])))
-
+    extra = -(-packed.size // (8 * width)) * 8
+    packed = jnp.pad(packed, (0, extra * width - packed.size)).reshape(1, extra, width)
+    rows_x = select_rows(send, tokens[0])
+    recv_x = lax.all_to_all(
+        jnp.concatenate(
+            [
+                rows_x.reshape(parts, MICRO * share, width),
+                jnp.broadcast_to(packed, (parts, extra, width)),
+            ],
+            axis=1,
+        ),
+        "fsdp",
+        split_axis=0,
+        concat_axis=0,
+        tiled=True,
+    )
     w_mix = jnp.concatenate([w_qkv, w_outgate], axis=1)
     late = (w_down, w_out, w_gate, w_up)
     if plane:
         units = plane.units()
-        late_full = lax.all_gather(late_quarter(*late), ("fsdp", "dp"), axis=0, tiled=True)
-        mix_blocks = gather_blocks(plane, plane.half(w_mix))
         widths = (3 * width, 2 * width, w_gate.shape[1], w_up.shape[1])
+        mix = Gather(plane, plane.half(w_mix))
+        mix.pass_to((1, 0), (0, 0), dz=1)
+        far = plane.move(plane.mine(mix.got[0, 0]), dz=2)
+        mix.pass_to((0, 1), (0, 0), dx=1)
+        mix.share((0, 0))
+        quarter = after(late_quarter(*late), mix.got[0, 0])
+        recv_x = after(recv_x, far, mix.got[0, 1], mix.got[1, 0], quarter)
+        far = after(far, recv_x)
+        mix.wait([(0, 1), (1, 0)], recv_x)
+        far_y = plane.move(far, dy=1)
+        corner = plane.move(far, dz=1)
+        mix.pass_to((1, 1), (1, 0), dx=1)
+        mix.share((0, 1), (1, 0))
+        late_full = lax.all_gather(
+            after(quarter, recv_x), ("fsdp", "dp"), axis=0, tiled=True
+        )
+        recv_x = after(recv_x, mix.from_core[0, 1], mix.from_core[1, 0])
     else:
         full_mix = gather_full(w_mix)
         full_down, full_out, full_gate, full_up = (gather_full(item) for item in late)
-
+    packed = recv_x[:, MICRO * share :].reshape(parts, -1)
+    full, start = [], 0
+    for item in small:
+        piece = packed[:, start : start + item.size]
+        full.append(piece.reshape((parts,) + item.shape))
+        start += item.size
+    full_gain_mix, full_gain_ffn = (item.reshape(-1).astype(f32) for item in full[:2])
+    full_gates = full[2].reshape(width, -1)
+    taps = jnp.swapaxes(full[3], 0, 1).reshape(TAPS, -1).astype(f32)
+
+    place = arrange + arrange // (MICRO * share) * extra
+    local_x = select_rows(place, recv_x.reshape(-1, width))
     inputs_f = local_x.astype(f32)
     normed, mix_back = jax.vjp(rms_scale, inputs_f, full_gain_mix)
     normed_low = normed.astype(bf16)
+    if plane:
+        far_y = after(far_y, normed_low)
+        corner = after(corner, normed_low)
+        mix.wait([(1, 1)], normed_low)
+        mix.got[2, 0] = plane.join(far, far_y)
+        mix.pass_to((2, 1), (2, 0), dx=1)
+        corner_y = plane.move(corner, dy=1)
+        mix.share((1, 1), (2, 0))
+        normed_low = after(normed_low, mix.from_core[1, 1], mix.from_core[2, 0])
     gate_in = exact(normed_low, full_gates)
     (total, strength), gates_back = jax.vjp(gate_tables, gate_in, a_log, dt_bias)
     spread = lambda item: jnp.broadcast_to(item.astype(f32)[:, None], (ROWS, H))
@@ -940,6 +995,15 @@
     row = jnp.transpose(table, (2, 0, 1))
     gain = out_norm_gain[None, :]
     if plane:
+        corner_y = after(corner_y, col, row)
+        mix.got[3, 0] = plane.join(corner, corner_y)
+        mix.pass_to((3, 1), (3, 0), dx=1)
+        mix.share((3, 0))
+        mix.wait([(2, 1)], mix.from_core[3, 0])
+        mix.share((2, 1))
+        mix.wait([(3, 1)], mix.from_core[2, 1])
+        mix.share((3, 1))
+        mix_blocks = [mix.got[at] for at in BLOCKS] + [mix.from_core[at] for at in BLOCKS]
         projected = project(units, normed_low, mix_blocks, 512)
     else:
         projected = exact(normed_low, full_mix)
@@ -948,36 +1012,39 @@
     mixed = [mixer_forward(projected, col, row, taps, gain, firsts[0], count)]
     mixed.append(mixer_forward(projected, col, row, taps, gain, firsts[1], count))
     given_cot = after(cotangent[0], mixed[0][0])
-    local_cot = select_rows(arrange, exchange(select_rows(send, given_cot)))
+    recv_cot = exchange(select_rows(send, given_cot))
     if plane:
-        residual, ffn_low, gate_act, up_act, hidden_low, result = ffn_forward(
+        residual, ffn_turned, gate_act, up_act, hidden_turned, result = ffn_forward(
             mixed[0][0], mixed[1][0], local_x, full_gain_ffn[None, :], late_full
         )
+        local_cot = select_rows(arrange, after(recv_cot, result))
         down = Reduce(
-            plane, gram_blocks(units, hidden_low.T, [local_cot], 1024, widths[0])
+            plane, gram_blocks(units, hidden_turned, [local_cot], 1024, widths[0])
         )
         rows_out = select_rows(arrange, after(result, down.send), TN)
         recv_out = exchange(rows_out)
         sent = down.start(rows_out)
         gate_low, up_low, grad_residual, mix_low, grad_gated, grad_gain_ffn = ffn_backward(
-            after(local_cot, sent), residual, full_gain_ffn[None, :], gate_act, up_act, late_full
-        )
-        sent = down.turn(grad_gated)
-        gated_t = jnp.concatenate([part[0].T for part in mixed], axis=0)
+            after(local_cot, sent), residual, full_gain_ffn[None, :], gate_act, up_act,
+            late_full,
+        )
+        sent = down.turn(grad_gated, recv_out)
+        gated_t = jnp.concatenate([part[1] for part in mixed], axis=0)
         wide = widths[1] + widths[2]
         sums = gram_blocks(units, gated_t, [after(mix_low, sent)], 1024, wide)
-        sums = gram_blocks(units, ffn_low.T, [gate_low], FTILE, wide, widths[1], sums)
+        sums = gram_blocks(units, ffn_turned, [gate_low], FTILE, wide, widths[1], sums)
         out_gate_sums = Reduce(plane, sums)
         up = Reduce(
             plane,
             gram_blocks(
-                units, ffn_low.T, [after(up_low, out_gate_sums.send)], FTILE, widths[3]
+                units, ffn_turned, [after(up_low, out_gate_sums.send)], FTILE, widths[3]
             ),
             split=True,
         )
-        sent = down.along(up.send)
-        sent = out_gate_sums.start(sent)
+        sent = out_gate_sums.start(up.send)
+        sent = up.start(sent)
     else:
+        local_cot = select_rows(arrange, recv_cot)
         gated_low = jnp.concatenate([part[0] for part in mixed], axis=1)
         residual = inputs_f + exact(gated_low, full_out)
         ffn_normed, ffn_back = jax.vjp(rms_scale, residual, full_gain_ffn)
@@ -1007,11 +1074,10 @@
     for part, first in zip(mixed, firsts):
         grad = after(grad_gated, sent) if plane else grad_gated
         backs.append(
-            mixer_backward(projected, grad, col, row, taps, gain, part[1], part[2], first)
+            mixer_backward(projected, grad, col, row, taps, gain, part[2], part[3], first)
         )
         if plane and not first:
-            sent = up.start(backs[0][0])
-            sent = down.across(sent)
+            sent = down.along(backs[0][0])
     rights = [back[i] for i in range(4) for back in backs]
     dtap_q, dtap_k, dtap_v = (
         jnp.concatenate([back[i] for back in backs], axis=1) for i in (4, 5, 6)
@@ -1019,22 +1085,29 @@
     dgain, dcol, drow = (jnp.concatenate([back[i] for back in backs]) for i in (7, 8, 9))
     if plane:
         left = normed_low.T
+        sent = out_gate_sums.turn(backs[1][0])
+        sent = up.beside(sent)
+        rights[4] = after(rights[4], sent)
+        vo = Reduce(plane, gram_blocks(units, left, rights[4:], 512, 2 * H * DV), split=True)
+        rights[0] = after(rights[0], vo.send)
         qk = Reduce(plane, gram_blocks(units, left, rights[:4], 512, 2 * H * DK))
-        rights[4] = after(rights[4], qk.send)
-        vo = Reduce(plane, gram_blocks(units, left, rights[4:], 512, 2 * H * DV), split=True)
-        sent = out_gate_sums.turn(vo.send)
+        sent = vo.start(qk.send)
+        sent = out_gate_sums.along(sent)
         sent = qk.start(sent)
+        sent = up.turn(sent)
         rights[0] = after(rights[0], sent)
         grad_normed = back_project(units, rights, mix_blocks, width, 512)
-        sent = up.beside(grad_normed)
-        sent = out_gate_sums.along(sent)
-        sent = vo.start(sent)
-        sent = down.close(sent)
+        sent = qk.turn(grad_normed)
+        sent = up.along(sent)
+        sent = down.across(sent)
+        sent = out_gate_sums.across(sent)
+        sent = vo.beside(sent)
     else:
         low = jnp.concatenate(rights, axis=1)
         grad_mix = reduce_grad(gram(normed_low, low))
         grad_normed = exact(low, full_mix, NT)
-    grad_conv = jnp.concatenate([dtap_q, dtap_k, dtap_v], axis=1).T
+    grad_conv = jnp.concatenate([dtap_q, dtap_k, dtap_v], axis=1).reshape(TAPS, parts, -1)
+    grad_conv = jnp.swapaxes(grad_conv, 0, 1)
     grad_out_gain = jnp.sum(dgain[:, 0], axis=0)
     grad_strength = drow[:, 0].T
     grad_total = dcol[:, :, 0].T - strength * grad_strength
@@ -1047,9 +1120,9 @@
     if plane:
         rows_in = select_rows(arrange, after(grad_inputs, sent), TN)
         recv_in = exchange(rows_in)
-        sent = qk.turn(rows_in)
-        sent = up.turn(sent)
-        sent = out_gate_sums.across(sent)
+        sent = qk.along(rows_in)
+        sent = up.across(sent)
+        sent = down.close(sent)
         output = select_rows(send, after(recv_out, sent), TN)[None]
     else:
         input_grad = give_back(grad_inputs)
@@ -1062,20 +1135,24 @@
         axis=1,
     )
     if plane:
-        sums = plane.sum_small(after(sums, sent))
-        sent = qk.along(sums)
-        sent = vo.beside(sent)
-        sent = up.along(sent)
+        def add_small(sums, step, *others):
+            pairs = [(i, i ^ step) for i in range(32)]
+            return sums + lax.ppermute(after(sums, *others), ("fsdp", "dp"), pairs)
+
+        sums = add_small(sums, 1, sent)
         sent = out_gate_sums.close(sent)
+        sent = vo.turn(sent, sums)
+        sums = add_small(sums, 4, sent)
+        sent = qk.across(sent)
+        sent = up.close(sent)
+        sent = vo.along(sent, sums)
+        sums = add_small(sums, 2, sent)
+        sent = qk.close(sent)
+        sent = vo.across(sent, sums)
+        sums = add_small(sums, 8, sent)
         input_grad = select_rows(send, after(recv_in, sent), TN)[None]
-        sent = qk.across(input_grad)
-        sent = vo.turn(sent)
-        sent = up.across(sent)
-        sent = qk.close(sent)
-        sent = vo.along(sent)
-        sent = up.close(sent)
-        sent = vo.across(sent)
-        vo.close(sent)
+        sent = vo.close(sent, sums)
+        sums = add_small(sums, 16, sent)
         out_gate_halves = out_gate_sums.halves()
         cut = widths[1]
 
@@ -1100,7 +1177,7 @@
         grad_qkv, grad_outgate = grad_mix[:, : w_qkv.shape[1]], grad_mix[:, w_qkv.shape[1] :]
     sums = lax.dynamic_index_in_dim(sums, own, 0, keepdims=False)
     ready, start = [], 0
-    for item in (gain_mix, gain_ffn, w_gates, conv_weight) + alone:
+    for item in small + alone:
         ready.append(sums[start : start + item.size].reshape(item.shape))
         start += item.size
     return (
@@ -1110,7 +1187,7 @@
         grad_qkv,
         ready[2],
         grad_outgate,
-        ready[3],
+        ready[3].T,
         ready[4],
         ready[5],
         ready[6],

time: 773 us -> 674 us (0.87)
  waiting for transfers between devices: 288 us -> 208 us
  local copies, waits for them, and re-layouts: 56.8 us -> 28.7 us
    ppermute x12 -> x5, waiting for transfers between devices: 90.1 us -> 14.3 us  [add_small(): return sums + lax.ppermute(after(sums, *others), ('fsdp', 'dp'), pairs)]
    all_gather x1, waiting for transfers between devices: 0.01 us -> 29.5 us  [local(): lax.all_gather(after(quarter, recv_x), ('fsdp', 'dp'), axis=0, tiled=True)]
    ppermute x47 -> x49, waiting for transfers between devices: 190 us -> 164 us  [move(): lax.ppermute(value, ('fsdp', 'dp'), [(here, here ^ flip) for here in rang...]
    ppermute x12 -> x5, starting transfers between devices: 19.8 us -> 5.09 us  [add_small(): return sums + lax.ppermute(after(sums, *others), ('fsdp', 'dp'), pairs)]
    ppermute x47 -> x49, starting transfers between devices: 36.5 us -> 50.3 us  [move(): lax.ppermute(value, ('fsdp', 'dp'), [(here, here ^ flip) for here in rang...]
    unnamed x163 -> x169, local copies, waits for them, and re-layouts: 18.7 us -> 14.3 us
    all_to_all x4 -> x3, starting transfers between devices: 19.6 us -> 15.7 us  [exchange(): lax.all_to_all(rows.reshape(parts, MICRO * share, width), 'fsdp', split_a...]
    dot_general x12 -> x11, matrix products: 22.1 us -> 21 us  [exact(): return lax.dot_general(left, right, dims, preferred_element_type=f32)]
  transfers between devices with their start and end apart: 64 -> 59, of which waited for: 19 -> 19; matrix products, arithmetic and copies ran while one was open for 17% -> 16% of each run, Pallas kernels for 23% -> 29%
where the time goes in v2:
time: 674 us; the launch traced here: 662 us
  Pallas kernels  230 us (34%)
  waiting for transfers between devices  208 us (31%)
  starting transfers between devices  78.5 us (12%)
  other arithmetic  77.8 us (12%)
  local copies, waits for them, and re-layouts  28.7 us (4%)
  matrix products  21.3 us (3%)
  between operations  17.9 us (3%)
    ppermute x49, waiting for transfers between devices, move(): lax.ppermute(value, ('fsdp', 'dp'), [(here, here ^ flip) for here in rang...  164 us
    pallas_call x6, Pallas kernels, gram_blocks(): pl.pallas_call(partial(gram_kernel, tuple(firsts), rows), grid_spec=pltpu...  59.2 us
    convert_element_type x25, other arithmetic, summed(): return sum((term.astype(f32) for term in terms)).astype(bf16)  52.6 us
    ppermute x49, starting transfers between devices, move(): lax.ppermute(value, ('fsdp', 'dp'), [(here, here ^ flip) for here in rang...  50.3 us
    pallas_call x2, Pallas kernels, mixer_backward(): pl.pallas_call(mixer_backward_kernel, grid=(count,), in_specs=start + [co...  39.1 us
    pallas_call x2, Pallas kernels, mixer_forward(): pl.pallas_call(mixer_forward_kernel, grid=(count,), in_specs=start + rest...  38.5 us
    pallas_call x1, Pallas kernels, ffn_backward(): pl.pallas_call(ffn_backward_kernel, grid_spec=pltpu.PrefetchScalarGridSpe...  31.2 us
    all_gather x1, waiting for transfers between devices, local(): lax.all_gather(after(quarter, recv_x), ('fsdp', 'dp'), axis=0, tiled=True)  29.5 us
  transfers between devices with their start and end apart: 59, of which 19 were waited for; matrix products, arithmetic and copies ran while one was open for 16% of the time, Pallas kernels for 29%

profile of v2, /device:TPU:0, one launch (start us, length us, event | category | flops | bytes accessed | tf_op | source)
XLA Modules:
  0.0 661.6 jit_solution(12309195598955783929)
XLA Ops:
  17.2 7.4 %all-to-all-start = ((bf16[8,72,1024]{2,1,0:T(8,128)(2,1)}), bf16[8,72,1024]{2,1,0:T(8,128)(2,1)}, u32[]{:S(2)}, u32[]{:S(2)}) async-start(bf16[8,72,1024]{2,1,0:T(8,128)(2,1)} %pad_maximum_fusion.2), calls=%async_computation | async-start | bytes 2359296 | tf_op jit(solution)/shard_map/all_to_all | solution.py:926
  41.5 28.0 %collective-permute-done = bf16[32,6144]{1,0:T(8,128)(2,1)S(1)} collective-permute-done((bf16[32,6144]{1,0:T(8,128)(2,1)}, bf16[32,6144]{1,0:T(8,128)(2,1)S(1)}, u32[]{:S(2)}, u32[]{:S(2)}) %collective-permute-start) | collective-permute-done | bytes 393248 | tf_op jit(solution)/shard_map/ppermute | solution.py:305
  83.3 14.3 %collective-permute-done.5.refs_0_.refs_8_ = bf16[64,6144]{1,0:T(8,128)(2,1)} collective-permute-done((bf16[64,6144]{1,0:T(8,128)(2,1)}, bf16[64,6144]{1,0:T(8,128)(2,1)}, u32[]{:S(2)}, u32[]{:S(2)}) %collective-permute-start.5) | collective-permute-done | bytes 786464 | tf_op jit(solution)/shard_map/ppermute | solution.py:305
  108.5 10.3 %collective-permute-done.10 = bf16[32,6144]{1,0:T(8,128)(2,1)S(1)} collective-permute-done((bf16[32,6144]{1,0:T(8,128)(2,1)}, bf16[32,6144]{1,0:T(8,128)(2,1)S(1)}, u32[]{:S(2)}, u32[]{:S(2)}) %collective-permute-start.10) | collective-permute-done | bytes 393248 | tf_op jit(solution)/shard_map/ppermute | solution.py:305
  120.1 13.7 %collective-permute-done.12.refs_3_.refs_11_ = bf16[64,6144]{1,0:T(8,128)(2,1)} collective-permute-done((bf16[64,6144]{1,0:T(8,128)(2,1)}, bf16[64,6144]{1,0:T(8,128)(2,1)}, u32[]{:S(2)}, u32[]{:S(2)}) %collective-permute-start.12) | collective-permute-done | bytes 786464 | tf_op jit(solution)/shard_map/ppermute | solution.py:305
  134.3 22.8 %collective-permute-done.11.refs_1_.refs_9_ = bf16[64,6144]{1,0:T(8,128)(2,1)} collective-permute-done((bf16[64,6144]{1,0:T(8,128)(2,1)S(1)}, bf16[64,6144]{1,0:T(8,128)(2,1)}, u32[]{:S(2)}, u32[]{:S(2)}) %collective-permute-start.11) | collective-permute-done | bytes 786464 | tf_op jit(solution)/shard_map/ppermute | solution.py:305
  161.8 18.1 %project.1.pq.pk.pv.og = f32[512,6144]{1,0:T(8,128)} custom-call(s32[16]{0:T(128)} %pad_add_fusion.units, bf16[512,1024]{1,0:T(8,128)(2,1)} %copy-done.2, bf16[64,6144]{1,0:T(8,128)(2,1)} %collective-permute-done.5.refs_0_.refs_8_, bf16[64,6144]{1,0:T(8,128)(2,1)} %collective-permute-done.11.refs_1_.refs_9_, ...), custom_call_target="tpu_custom_call" | custom-call | flops 170000000 | bytes 510000 | tf_op jit(solution)/shard_map/project/pallas_call | solution.py:444
  179.9 19.3 %mixer_forward.2 = (bf16[512,1024]{1,0:T(8,128)(2,1)}, bf16[1024,512]{1,0:T(8,128)(2,1)}, bf16[4,512,256]{2,1,0:T(8,128)(2,1)}, bf16[4,512,256]{2,1,0:T(8,128)(2,1)}) custom-call(f32[512,6144]{1,0:T(8,128)} %project.1.pq.pk.pv.og, f32[512,6144]{1,0:T(8,128)} %project.1.pq.pk.pv.og, f32[512,6144]{1,0:T(8,128)} %project.1.pq.pk.pv.og, ...), custom_call_target="tpu_custom_call" | custom-call | flops 176000000 | bytes 528000 | tf_op jit(solution)/shard_map/mixer_forward/pallas_call | solution.py:234
  200.9 4.9 all-to-all-start.1
  205.8 19.3 %mixer_forward.3 = (bf16[512,1024]{1,0:T(8,128)(2,1)}, bf16[1024,512]{1,0:T(8,128)(2,1)}, bf16[4,512,256]{2,1,0:T(8,128)(2,1)}, bf16[4,512,256]{2,1,0:T(8,128)(2,1)}) custom-call(f32[512,6144]{1,0:T(8,128)} %project.1.pq.pk.pv.og, f32[512,6144]{1,0:T(8,128)} %project.1.pq.pk.pv.og, f32[512,6144]{1,0:T(8,128)} %project.1.pq.pk.pv.og, ...), custom_call_target="tpu_custom_call" | custom-call | flops 176000000 | bytes 528000 | tf_op jit(solution)/shard_map/mixer_forward/pallas_call | solution.py:234
  225.1 29.5 %all-gather.2.cloned.1.call-done.down.out_first.out_second.w_gate.w_up = bf16[1024,10752]{1,0:T(8,128)(2,1)} async-done(((bf16[32,10752]{1,0:T(8,128)(2,1)}), bf16[1024,10752]{1,0:T(8,128)(2,1)}) %all-gather.2.cloned.1.call-update) | async-done | bytes 22020112 | tf_op jit(solution)/shard_map/all_gather | solution.py:957
  254.6 24.5 %ffn_forward.1 = (f32[512,1024]{1,0:T(8,128)}, bf16[1024,512]{1,0:T(8,128)(2,1)}, bf16[512,2816]{1,0:T(8,128)(2,1)}, bf16[512,2816]{1,0:T(8,128)(2,1)}, bf16[281...) custom-call(bf16[512,1024]{1,0:T(8,128)(2,1)} %get-tuple-element.140.gated, bf16[512,1024]{1,0:T(8,128)(2,1)} %get-tuple-element.141.more, ...), custom_call_target="tpu_custom_call" | custom-call | flops 270000000 | bytes 810000 | tf_op jit(solution)/shard_map/ffn_forward/pallas_call | solution.py:674
  280.8 9.4 %gram_blocks.6 = (bf16[8,64,3072]{2,1,0:T(8,128)(2,1)}, bf16[8,64,3072]{2,1,0:T(8,128)(2,1)}) custom-call(s32[16]{0:T(128)} %pad_add_fusion.units, bf16[2816,512]{1,0:T(8,128)(2,1)} %get-tuple-element.144.left_ref, bf16[512,1024]{1,0:T(8,128)(2,1)} %convolution_convert_fusion.4.refs_0_.cot), custom_call_target="tpu_custom_call" | custom-call | flops 99433928 | bytes 298301 | tf_op jit(solution)/shard_map/gram_blocks/pallas_call | solution.py:559
  292.2 4.0 all-to-all-start.2
  296.2 5.3 add_convert_fusion.4
  305.0 31.2 %ffn_backward.1 = (bf16[512,2816]{1,0:T(8,128)(2,1)}, bf16[512,2816]{1,0:T(8,128)(2,1)}, f32[512,1024]{1,0:T(8,128)}, bf16[512,1024]{1,0:T(8,128)(2,1)}, f32[512,2048]{1,0:T(8,128)}, /*index=5*/f32[1,1024]{1,0:T(1,128)}) custom-call(bf16[512,1024]{1,0:T(8,128)(2,1)} %convolution_convert_fusion.4.refs_0_.cot, f32[512,1024]{1,0:T(8,128)} %get-tuple-element.152.residual, ...), custom_call_target="tpu_custom_call" | custom-call | flops 350000000 | bytes 1050000 | tf_op jit(solution)/shard_map/ffn_backward/pallas_call | solution.py:754
  336.3 8.7 %collective-permute-done.18 = bf16[4,64,3072]{2,1,0:T(8,128)(2,1)} collective-permute-done((bf16[4,64,3072]{2,1,0:T(8,128)(2,1)}, bf16[4,64,3072]{2,1,0:T(8,128)(2,1)}, u32[]{:S(2)}, u32[]{:S(2)}) %collective-permute-start.18) | collective-permute-done | bytes 1572896 | tf_op jit(solution)/shard_map/ppermute | solution.py:305
  345.0 3.1 add_convert_fusion.14
  348.1 7.2 %gram_blocks.7 = (bf16[8,64,4864]{2,1,0:T(8,128)(2,1)}, bf16[8,64,4864]{2,1,0:T(8,128)(2,1)}) custom-call(s32[16]{0:T(128)} %pad_add_fusion.units, bf16[2048,512]{1,0:T(8,128)(2,1)} %pad_maximum_fusion.left_ref, bf16[512,1024]{1,0:T(8,128)(2,1)} %get-tuple-element.163.refs_0_), custom_call_target="tpu_custom_call" | custom-call | flops 72315584 | bytes 216946 | tf_op jit(solution)/shard_map/gram_blocks/pallas_call | solution.py:559
  355.3 11.6 %gram_blocks.8 = (bf16[8,64,4864]{2,1,0:T(8,128)(2,1)}, bf16[8,64,4864]{2,1,0:T(8,128)(2,1)}) custom-call(s32[16]{0:T(128)} %pad_add_fusion.units, bf16[1024,512]{1,0:T(8,128)(2,1)} %get-tuple-element.157.left_ref, bf16[512,2816]{1,0:T(8,128)(2,1)} %get-tuple-element.159.refs_0_, ...), custom_call_target="tpu_custom_call", output_to_operand_aliasing={{0}: (3, {}), {1}: (4, {})} | custom-call | flops 99433928 | bytes 298301 | tf_op jit(solution)/shard_map/gram_blocks/pallas_call | solution.py:559
  366.9 11.6 %gram_blocks.9 = (bf16[8,64,2816]{2,1,0:T(8,128)(2,1)}, bf16[8,64,2816]{2,1,0:T(8,128)(2,1)}) custom-call(s32[16]{0:T(128)} %pad_add_fusion.units, bf16[1024,512]{1,0:T(8,128)(2,1)} %get-tuple-element.157.left_ref, bf16[512,2816]{1,0:T(8,128)(2,1)} %get-tuple-element.167.refs_0_), custom_call_target="tpu_custom_call" | custom-call | flops 99433928 | bytes 298301 | tf_op jit(solution)/shard_map/gram_blocks/pallas_call | solution.py:559
  379.0 5.5 add_convert_fusion
  387.1 5.0 add_convert_fusion.6
  393.6 19.7 %mixer_backward.2 = (bf16[512,512]{1,0:T(8,128)(2,1)}, bf16[512,512]{1,0:T(8,128)(2,1)}, bf16[512,1024]{1,0:T(8,128)(2,1)}, bf16[512,1024]{1,0:T(8,128)(2,1)}, f...) custom-call(f32[512,6144]{1,0:T(8,128)} %project.1.pq.pk.pv.og, ...), custom_call_target="tpu_custom_call" | custom-call | flops 184000000 | bytes 552000 | tf_op jit(solution)/shard_map/mixer_backward/pallas_call | solution.py:258
  415.3 19.4 %mixer_backward.3 = (bf16[512,512]{1,0:T(8,128)(2,1)}, bf16[512,512]{1,0:T(8,128)(2,1)}, bf16[512,1024]{1,0:T(8,128)(2,1)}, bf16[512,1024]{1,0:T(8,128)(2,1)}, f...) custom-call(f32[512,6144]{1,0:T(8,128)} %project.1.pq.pk.pv.og, ...), custom_call_target="tpu_custom_call" | custom-call | flops 184000000 | bytes 552000 | tf_op jit(solution)/shard_map/mixer_backward/pallas_call | solution.py:258
  434.7 6.1 collective-permute-done.24
  440.8 3.8 add_convert_fusion.8
  444.6 2.8 add_convert_fusion.16
  447.4 12.1 %gram_blocks.10 = (bf16[8,64,4096]{2,1,0:T(8,128)(2,1)}, bf16[8,64,4096]{2,1,0:T(8,128)(2,1)}) custom-call(s32[16]{0:T(128)} %pad_add_fusion.units, bf16[1024,512]{1,0:T(8,128)(2,1)} %copy.90.left_ref, bf16[512,1024]{1,0:T(8,128)(2,1)} %get-tuple-element.185.refs_0_.refs_4_, bf16[512,1024]{1,0:T(8,128)(2,1)} %get-tuple-element.186.refs_1_.refs_5_, ...), custom_call_target="tpu_custom_call" | custom-call | flops 144631168 | bytes 433893 | tf_op jit(solution)/shard_map/gram_blocks/pallas_call | solution.py:559
  462.8 3.7 collective-permute-start.27
  467.0 7.4 %gram_blocks.11 = (bf16[8,64,2048]{2,1,0:T(8,128)(2,1)}, bf16[8,64,2048]{2,1,0:T(8,128)(2,1)}) custom-call(s32[16]{0:T(128)} %pad_add_fusion.units, bf16[1024,512]{1,0:T(8,128)(2,1)} %copy.90.left_ref, bf16[512,512]{1,0:T(8,128)(2,1)} %get-tuple-element.200.refs_0_, bf16[512,512]{1,0:T(8,128)(2,1)} %get-tuple-element.181.refs_1_, ...), custom_call_target="tpu_custom_call" | custom-call | flops 72315584 | bytes 216946 | tf_op jit(solution)/shard_map/gram_blocks/pallas_call | solution.py:559
  475.8 6.6 add_convert_fusion.2
  482.3 18.5 %collective-permute-done.27 = bf16[2,64,4864]{2,1,0:T(8,128)(2,1)} collective-permute-done((bf16[2,64,4864]{2,1,0:T(8,128)(2,1)}, bf16[2,64,4864]{2,1,0:T(8,128)(2,1)}, u32[]{:S(2)}, u32[]{:S(2)}) %collective-permute-start.27) | collective-permute-done | bytes 1245216 | tf_op jit(solution)/shard_map/ppermute | solution.py:305
  502.9 3.8 add_convert_fusion.12
  509.6 4.0 collective-permute-start.35
  513.7 19.1 %back_project.1 = f32[512,1024]{1,0:T(8,128)} custom-call(s32[16]{0:T(128)} %pad_add_fusion.units, bf16[512,512]{1,0:T(8,128)(2,1)} %get-tuple-element.200.refs_0_, bf16[512,512]{1,0:T(8,128)(2,1)} %get-tuple-element.181.refs_1_, bf16[512,512]{1,0:T(8,128)(2,1)} %get-tuple-element.191.refs_2_, bf16[512,512]{1,0:T(8,128)(2,1)} %get-tuple-element.192.refs_3_, ...), custom_call_target="tpu_custom_call" | custom-call | flops 180000000 | bytes 540000 | tf_op jit(solution)/shard_map/back_project/pallas_call | solution.py:505
  545.5 11.4 %collective-permute-done.34 = bf16[8,32,4096]{2,1,0:T(8,128)(2,1)} collective-permute-done((bf16[8,32,4096]{2,1,0:T(8,128)(2,1)}, bf16[8,32,4096]{2,1,0:T(8,128)(2,1)}, u32[]{:S(2)}, u32[]{:S(2)}) %collective-permute-start.34) | collective-permute-done | bytes 2097184 | tf_op jit(solution)/shard_map/ppermute | solution.py:305
  557.0 3.3 add_convert_fusion.10
  563.9 4.1 collective-permute-start.41
  570.8 7.9 %collective-permute-done.37 = bf16[64,4864]{1,0:T(8,128)(2,1)S(1)} collective-permute-done((bf16[64,4864]{1,0:T(8,128)(2,1)S(1)}, bf16[64,4864]{1,0:T(8,128)(2,1)S(1)}, u32[]{:S(2)}, u32[]{:S(2)}) %collective-permute-start.37) | collective-permute-done | bytes 622624 | tf_op jit(solution)/shard_map/ppermute | solution.py:305
  578.8 6.8 %all-to-all-start.3 = ((bf16[8,64,1024]{2,1,0:T(8,128)(2,1)}), bf16[8,64,1024]{2,1,0:T(8,128)(2,1)}, u32[]{:S(2)}, u32[]{:S(2)}) async-start(bf16[8,64,1024]{2,1,0:T(8,128)(2,1)} %bitcast.165), calls=%async_computation.3 | async-start | bytes 2097152 | tf_op jit(solution)/shard_map/all_to_all | solution.py:907
  585.7 3.0 fusion.8
  605.3 12.1 %collective-permute-done.39 = bf16[2,32,4096]{2,1,0:T(8,128)(2,1)S(1)} collective-permute-done((bf16[2,32,4096]{2,1,0:T(8,128)(2,1)S(1)}, bf16[2,32,4096]{2,1,0:T(8,128)(2,1)S(1)}, u32[]{:S(2)}, u32[]{:S(2)}) %collective-permute-start.39) | collective-permute-done | bytes 524320 | tf_op jit(solution)/shard_map/ppermute | solution.py:305
  620.5 3.9 collective-permute-done.45
  624.4 7.5 %collective-permute-done.43 = bf16[32,4096]{1,0:T(8,128)(2,1)S(1)} collective-permute-done((bf16[32,4096]{1,0:T(8,128)(2,1)S(1)}, bf16[32,4096]{1,0:T(8,128)(2,1)S(1)}, u32[]{:S(2)}, u32[]{:S(2)}) %collective-permute-start.43) | collective-permute-done | bytes 262176 | tf_op jit(solution)/shard_map/ppermute | solution.py:305
  633.8 5.0 collective-permute-done.46
  640.8 3.0 fusion.9
  643.9 4.1 collective-permute-done.48
  (399 shorter events, 130.0 us)
Async XLA Ops:
  17.2 54.1 %all-to-all-start = ((bf16[8,72,1024]{2,1,0:T(8,128)(2,1)}), bf16[8,72,1024]{2,1,0:T(8,128)(2,1)}, u32[]{:S(2)}, u32[]{:S(2)}) async-start(bf16[8,72,1024]{2,1,0:T(8,128)(2,1)} %pad_maximum_fusion.2), calls=%async_computation | async-start | bytes 2359296 | tf_op jit(solution)/shard_map/all_to_all | solution.py:926
  24.6 230.0 %all-gather.2.cloned.1.call-start = ((), (), s32[]{:S(2)}) async-start(), calls=%async_computation.4 | async-start | bytes 22708224 | tf_op jit(solution)/shard_map/all_gather | solution.py:957
  26.1 43.4 %collective-permute-start.1 = (bf16[64,6144]{1,0:T(8,128)(2,1)S(1)}, bf16[64,6144]{1,0:T(8,128)(2,1)}, u32[]{:S(2)}, u32[]{:S(2)}) collective-permute-start(bf16[64,6144]{1,0:T(8,128)(2,1)S(1)} %constant_dynamic-slice_fusion.refs_6_.refs_14_), channel_id=1, source_target_pairs={{0,4},{1,5},{2,6},{3,7},{4,0},{5,1},{6,2},{7,3},{8,12},{9,13},{10,... | collective-permute-start | bytes 2359304 | tf_op jit(solution)/shard_map/ppermute | solution.py:305
  28.2 43.2 %collective-permute-start.2 = (bf16[64,6144]{1,0:T(8,128)(2,1)S(1)}, bf16[64,6144]{1,0:T(8,128)(2,1)}, u32[]{:S(2)}, u32[]{:S(2)}) collective-permute-start(bf16[64,6144]{1,0:T(8,128)(2,1)S(1)} %constant_dynamic-slice_fusion.refs_6_.refs_14_), channel_id=1, source_target_pairs={{0,8},{1,9},{2,10},{3,11},{4,12},{5,13},{6,14},{7,15},{8,0},{9,1},... | collective-permute-start | bytes 2359304 | tf_op jit(solution)/shard_map/ppermute | solution.py:305
  30.5 39.0 %collective-permute-start = (bf16[32,6144]{1,0:T(8,128)(2,1)}, bf16[32,6144]{1,0:T(8,128)(2,1)S(1)}, u32[]{:S(2)}, u32[]{:S(2)}) collective-permute-start(bf16[32,6144]{1,0:T(8,128)(2,1)} %constant_dynamic-slice_fusion.1), channel_id=1, source_target_pairs={{0,16},{1,17},{2,18},{3,19},{4,20},{5,21},{6,22},{7,23},{8,24},{9,... | collective-permute-start | bytes 1179656 | tf_op jit(solution)/shard_map/ppermute | solution.py:305
  72.8 24.8 %collective-permute-start.5 = (bf16[64,6144]{1,0:T(8,128)(2,1)}, bf16[64,6144]{1,0:T(8,128)(2,1)}, u32[]{:S(2)}, u32[]{:S(2)}) collective-permute-start(bf16[64,6144]{1,0:T(8,128)(2,1)} %collective-permute-done.2.refs_4_.refs_12_), channel_id=1, source_target_pairs={{0,4},{1,5},{2,6},{3,7},{4,0},{5,1},{6,2},{7,3},{8,12},{9,13},{10,... | collective-permute-start | bytes 2359304 | tf_op jit(solution)/shard_map/ppermute | solution.py:305
  74.3 23.3 %collective-permute-start.7 = (bf16[32,6144]{1,0:T(8,128)(2,1)S(1)}, bf16[32,6144]{1,0:T(8,128)(2,1)S(1)}, u32[]{:S(2)}, u32[]{:S(2)}) collective-permute-start(bf16[32,6144]{1,0:T(8,128)(2,1)S(1)} %collective-permute-done), channel_id=1, source_target_pairs={{0,2},{1,3},{2,0},{3,1},{4,6},{5,7},{6,4},{7,5},{8,10},{9,11},{10,... | collective-permute-start | bytes 1179656 | tf_op jit(solution)/shard_map/ppermute | solution.py:305
  75.8 26.5 %collective-permute-start.9 = (bf16[32,6144]{1,0:T(8,128)(2,1)S(1)}, bf16[32,6144]{1,0:T(8,128)(2,1)}, u32[]{:S(2)}, u32[]{:S(2)}) collective-permute-start(bf16[32,6144]{1,0:T(8,128)(2,1)S(1)} %collective-permute-done), channel_id=1, source_target_pairs={{0,8},{1,9},{2,10},{3,11},{4,12},{5,13},{6,14},{7,15},{8,0},{9,1},... | collective-permute-start | bytes 1179656 | tf_op jit(solution)/shard_map/ppermute | solution.py:305
  97.6 7.8 %collective-permute-start.6 = (bf16[64,6144]{1,0:T(8,128)(2,1)}, bf16[64,6144]{1,0:T(8,128)(2,1)}, u32[]{:S(2)}, u32[]{:S(2)}) collective-permute-start(bf16[64,6144]{1,0:T(8,128)(2,1)} %collective-permute-done.5.refs_0_.refs_8_), channel_id=1, source_target_pairs={{0,1},{1,0},{2,3},{3,2},{4,5},{5,4},{6,7},{7,6},{8,9},{9,8},{10,11... | collective-permute-start | bytes 2359304 | tf_op jit(solution)/shard_map/ppermute | solution.py:305
  100.8 33.0 %collective-permute-start.12 = (bf16[64,6144]{1,0:T(8,128)(2,1)}, bf16[64,6144]{1,0:T(8,128)(2,1)}, u32[]{:S(2)}, u32[]{:S(2)}) collective-permute-start(bf16[64,6144]{1,0:T(8,128)(2,1)} %pad_maximum_fusion.3.refs_7_.refs_15_), channel_id=1, source_target_pairs={{0,4},{1,5},{2,6},{3,7},{4,0},{5,1},{6,2},{7,3},{8,12},{9,13},{10,... | collective-permute-start | bytes 2359304 | tf_op jit(solution)/shard_map/ppermute | solution.py:305
  102.3 16.5 %collective-permute-start.10 = (bf16[32,6144]{1,0:T(8,128)(2,1)}, bf16[32,6144]{1,0:T(8,128)(2,1)S(1)}, u32[]{:S(2)}, u32[]{:S(2)}) collective-permute-start(bf16[32,6144]{1,0:T(8,128)(2,1)} %collective-permute-done.9), channel_id=1, source_target_pairs={{0,2},{1,3},{2,0},{3,1},{4,6},{5,7},{6,4},{7,5},{8,10},{9,11},{10,... | collective-permute-start | bytes 1179656 | tf_op jit(solution)/shard_map/ppermute | solution.py:305
  119.9 13.9 %collective-permute-start.13 = (bf16[64,6144]{1,0:T(8,128)(2,1)S(1)}, bf16[64,6144]{1,0:T(8,128)(2,1)S(1)}, u32[]{:S(2)}, u32[]{:S(2)}) collective-permute-start(bf16[64,6144]{1,0:T(8,128)(2,1)S(1)} %pad_maximum_fusion.4.refs_5_.refs_13_), channel_id=1, source_target_pairs={{0,1},{1,0},{2,3},{3,2},{4,5},{5,4},{6,7},{7,6},{8,9},{9,8},{10,11... | collective-permute-start | bytes 2359304 | tf_op jit(solution)/shard_map/ppermute | solution.py:305
  120.0 37.1 %collective-permute-start.11 = (bf16[64,6144]{1,0:T(8,128)(2,1)S(1)}, bf16[64,6144]{1,0:T(8,128)(2,1)}, u32[]{:S(2)}, u32[]{:S(2)}) collective-permute-start(bf16[64,6144]{1,0:T(8,128)(2,1)S(1)} %pad_maximum_fusion.4.refs_5_.refs_13_), channel_id=1, source_target_pairs={{0,4},{1,5},{2,6},{3,7},{4,0},{5,1},{6,2},{7,3},{8,12},{9,13},{10,... | collective-permute-start | bytes 2359304 | tf_op jit(solution)/shard_map/ppermute | solution.py:305
  133.8 23.3 %collective-permute-start.14 = (bf16[64,6144]{1,0:T(8,128)(2,1)}, bf16[64,6144]{1,0:T(8,128)(2,1)}, u32[]{:S(2)}, u32[]{:S(2)}) collective-permute-start(bf16[64,6144]{1,0:T(8,128)(2,1)} %collective-permute-done.12.refs_3_.refs_11_), channel_id=1, source_target_pairs={{0,1},{1,0},{2,3},{3,2},{4,5},{5,4},{6,7},{7,6},{8,9},{9,8},{10,11... | collective-permute-start | bytes 2359304 | tf_op jit(solution)/shard_map/ppermute | solution.py:305
  133.8 27.9 %collective-permute-start.16 = (bf16[64,6144]{1,0:T(8,128)(2,1)S(1)}, bf16[64,6144]{1,0:T(8,128)(2,1)}, u32[]{:S(2)}, u32[]{:S(2)}) collective-permute-start(bf16[64,6144]{1,0:T(8,128)(2,1)S(1)} %constant_dynamic-slice_fusion.refs_6_.refs_14_), channel_id=1, source_target_pairs={{0,1},{1,0},{2,3},{3,2},{4,5},{5,4},{6,7},{7,6},{8,9},{9,8},{10,11... | collective-permute-start | bytes 2359304 | tf_op jit(solution)/shard_map/ppermute | solution.py:305
  200.9 78.1 %all-to-all-start.1 = ((bf16[8,64,1024]{2,1,0:T(8,128)(2,1)}), bf16[8,64,1024]{2,1,0:T(8,128)(2,1)S(1)}, u32[]{:S(2)}, u32[]{:S(2)}) async-start(bf16[8,64,1024]{2,1,0:T(8,128)(2,1)} %bitcast.20), calls=%async_computation.1 | async-start | bytes 2097152 | tf_op jit(solution)/shard_map/all_to_all | solution.py:907
  292.2 44.0 %all-to-all-start.2 = ((bf16[8,64,1024]{2,1,0:T(8,128)(2,1)}), bf16[8,64,1024]{2,1,0:T(8,128)(2,1)S(1)}, u32[]{:S(2)}, u32[]{:S(2)}) async-start(bf16[8,64,1024]{2,1,0:T(8,128)(2,1)} %bitcast.22), calls=%async_computation.2 | async-start | bytes 2097152 | tf_op jit(solution)/shard_map/all_to_all | solution.py:907
  301.6 43.5 %collective-permute-start.18 = (bf16[4,64,3072]{2,1,0:T(8,128)(2,1)}, bf16[4,64,3072]{2,1,0:T(8,128)(2,1)}, u32[]{:S(2)}, u32[]{:S(2)}) collective-permute-start(bf16[4,64,3072]{2,1,0:T(8,128)(2,1)} %get-tuple-element.304), channel_id=1, source_target_pairs={{0,4},{1,5},{2,6},{3,7},{4,0},{5,1},{6,2},{7,3},{8,12},{9,13},{10,... | collective-permute-start | bytes 4718600 | tf_op jit(solution)/shard_map/ppermute | solution.py:305
  366.9 12.1 %collective-permute-start.21 = (bf16[8,64,4864]{2,1,0:T(8,128)(2,1)}, bf16[8,64,4864]{2,1,0:T(8,128)(2,1)}, u32[]{:S(2)}, u32[]{:S(2)}) collective-permute-start(bf16[8,64,4864]{2,1,0:T(8,128)(2,1)} %get-tuple-element.166), channel_id=1, source_target_pairs={{0,1},{1,0},{2,3},{3,2},{4,5},{5,4},{6,7},{7,6},{8,9},{9,8},{10,11... | collective-permute-start | bytes 14942216 | tf_op jit(solution)/shard_map/ppermute | solution.py:305
  378.5 8.6 %collective-permute-start.20 = (bf16[8,64,2816]{2,1,0:T(8,128)(2,1)}, bf16[8,64,2816]{2,1,0:T(8,128)(2,1)}, u32[]{:S(2)}, u32[]{:S(2)}) collective-permute-start(bf16[8,64,2816]{2,1,0:T(8,128)(2,1)} %get-tuple-element.169), channel_id=1, source_target_pairs={{0,1},{1,0},{2,3},{3,2},{4,5},{5,4},{6,7},{7,6},{8,9},{9,8},{10,11... | collective-permute-start | bytes 8650760 | tf_op jit(solution)/shard_map/ppermute | solution.py:305
  384.5 56.3 %collective-permute-start.24 = (bf16[4,64,4864]{2,1,0:T(8,128)(2,1)}, bf16[4,64,4864]{2,1,0:T(8,128)(2,1)}, u32[]{:S(2)}, u32[]{:S(2)}) collective-permute-start(bf16[4,64,4864]{2,1,0:T(8,128)(2,1)} %get-tuple-element.301), channel_id=1, source_target_pairs={{0,4},{1,5},{2,6},{3,7},{4,0},{5,1},{6,2},{7,3},{8,12},{9,13},{10,... | collective-permute-start | bytes 7471112 | tf_op jit(solution)/shard_map/ppermute | solution.py:305
  384.5 28.9 %collective-permute-start.19 = (bf16[2,64,3072]{2,1,0:T(8,128)(2,1)}, bf16[2,64,3072]{2,1,0:T(8,128)(2,1)}, u32[]{:S(2)}, u32[]{:S(2)}) collective-permute-start(bf16[2,64,3072]{2,1,0:T(8,128)(2,1)} %get-tuple-element.314), channel_id=1, source_target_pairs={{0,8},{1,9},{2,10},{3,11},{4,12},{5,13},{6,14},{7,15},{8,0},{9,1},... | collective-permute-start | bytes 2359304 | tf_op jit(solution)/shard_map/ppermute | solution.py:305
  392.1 52.6 %collective-permute-start.23 = (bf16[8,32,2816]{2,1,0:T(8,128)(2,1)}, bf16[8,32,2816]{2,1,0:T(8,128)(2,1)}, u32[]{:S(2)}, u32[]{:S(2)}) collective-permute-start(bf16[8,32,2816]{2,1,0:T(8,128)(2,1)} %get-tuple-element.307), channel_id=1, source_target_pairs={{0,2},{1,3},{2,0},{3,1},{4,6},{5,7},{6,4},{7,5},{8,10},{9,11},{10,... | collective-permute-start | bytes 4325384 | tf_op jit(solution)/shard_map/ppermute | solution.py:305
  459.6 16.1 %collective-permute-start.28 = (bf16[8,64,4096]{2,1,0:T(8,128)(2,1)}, bf16[8,64,4096]{2,1,0:T(8,128)(2,1)}, u32[]{:S(2)}, u32[]{:S(2)}) collective-permute-start(bf16[8,64,4096]{2,1,0:T(8,128)(2,1)} %get-tuple-element.189), channel_id=1, source_target_pairs={{0,1},{1,0},{2,3},{3,2},{4,5},{5,4},{6,7},{7,6},{8,9},{9,8},{10,11... | collective-permute-start | bytes 12582920 | tf_op jit(solution)/shard_map/ppermute | solution.py:305
  459.7 80.9 %collective-permute-start.22 = (bf16[64,3072]{1,0:T(8,128)(2,1)}, bf16[64,3072]{1,0:T(8,128)(2,1)}, u32[]{:S(2)}, u32[]{:S(2)}) collective-permute-start(bf16[64,3072]{1,0:T(8,128)(2,1)} %fusion.24), channel_id=1, source_target_pairs={{0,16},{1,17},{2,18},{3,19},{4,20},{5,21},{6,22},{7,23},{8,24},{9,... | collective-permute-start | bytes 1179656 | tf_op jit(solution)/shard_map/ppermute | solution.py:305
  462.8 38.0 %collective-permute-start.27 = (bf16[2,64,4864]{2,1,0:T(8,128)(2,1)}, bf16[2,64,4864]{2,1,0:T(8,128)(2,1)}, u32[]{:S(2)}, u32[]{:S(2)}) collective-permute-start(bf16[2,64,4864]{2,1,0:T(8,128)(2,1)} %get-tuple-element.309), channel_id=1, source_target_pairs={{0,8},{1,9},{2,10},{3,11},{4,12},{5,13},{6,14},{7,15},{8,0},{9,1},... | collective-permute-start | bytes 3735560 | tf_op jit(solution)/shard_map/ppermute | solution.py:305
  474.4 28.5 %collective-permute-start.26 = (bf16[8,64,2048]{2,1,0:T(8,128)(2,1)}, bf16[8,64,2048]{2,1,0:T(8,128)(2,1)}, u32[]{:S(2)}, u32[]{:S(2)}) collective-permute-start(bf16[8,64,2048]{2,1,0:T(8,128)(2,1)} %get-tuple-element.194), channel_id=1, source_target_pairs={{0,1},{1,0},{2,3},{3,2},{4,5},{5,4},{6,7},{7,6},{8,9},{9,8},{10,11... | collective-permute-start | bytes 6291464 | tf_op jit(solution)/shard_map/ppermute | solution.py:305
  475.5 31.5 %collective-permute-start.25 = (bf16[4,32,2816]{2,1,0:T(8,128)(2,1)}, bf16[4,32,2816]{2,1,0:T(8,128)(2,1)S(1)}, u32[]{:S(2)}, u32[]{:S(2)}) collective-permute-start(bf16[4,32,2816]{2,1,0:T(8,128)(2,1)} %get-tuple-element.316), channel_id=1, source_target_pairs={{0,4},{1,5},{2,6},{3,7},{4,0},{5,1},{6,2},{7,3},{8,12},{9,13},{10,... | collective-permute-start | bytes 2162696 | tf_op jit(solution)/shard_map/ppermute | solution.py:305
  506.7 29.6 %collective-permute-start.30 = (bf16[4,64,2048]{2,1,0:T(8,128)(2,1)}, bf16[4,64,2048]{2,1,0:T(8,128)(2,1)}, u32[]{:S(2)}, u32[]{:S(2)}) collective-permute-start(bf16[4,64,2048]{2,1,0:T(8,128)(2,1)} %get-tuple-element.313), channel_id=1, source_target_pairs={{0,4},{1,5},{2,6},{3,7},{4,0},{5,1},{6,2},{7,3},{8,12},{9,13},{10,... | collective-permute-start | bytes 3145736 | tf_op jit(solution)/shard_map/ppermute | solution.py:305
  508.0 30.7 %collective-permute-start.29 = (bf16[2,32,2816]{2,1,0:T(8,128)(2,1)}, bf16[2,32,2816]{2,1,0:T(8,128)(2,1)}, u32[]{:S(2)}, u32[]{:S(2)}) collective-permute-start(bf16[2,32,2816]{2,1,0:T(8,128)(2,1)} %get-tuple-element.324), channel_id=1, source_target_pairs={{0,8},{1,9},{2,10},{3,11},{4,12},{5,13},{6,14},{7,15},{8,0},{9,1},... | collective-permute-start | bytes 1081352 | tf_op jit(solution)/shard_map/ppermute | solution.py:305
  508.0 48.9 %collective-permute-start.34 = (bf16[8,32,4096]{2,1,0:T(8,128)(2,1)}, bf16[8,32,4096]{2,1,0:T(8,128)(2,1)}, u32[]{:S(2)}, u32[]{:S(2)}) collective-permute-start(bf16[8,32,4096]{2,1,0:T(8,128)(2,1)} %get-tuple-element.303), channel_id=1, source_target_pairs={{0,2},{1,3},{2,0},{3,1},{4,6},{5,7},{6,4},{7,5},{8,10},{9,11},{10,... | collective-permute-start | bytes 6291464 | tf_op jit(solution)/shard_map/ppermute | solution.py:305
  509.6 32.8 %collective-permute-start.35 = (bf16[64,4864]{1,0:T(8,128)(2,1)}, bf16[64,4864]{1,0:T(8,128)(2,1)}, u32[]{:S(2)}, u32[]{:S(2)}) collective-permute-start(bf16[64,4864]{1,0:T(8,128)(2,1)} %fusion.14), channel_id=1, source_target_pairs={{0,16},{1,17},{2,18},{3,19},{4,20},{5,21},{6,22},{7,23},{8,24},{9,... | collective-permute-start | bytes 1867784 | tf_op jit(solution)/shard_map/ppermute | solution.py:305
  538.6 25.2 %collective-permute-start.33 = (bf16[2,64,2048]{2,1,0:T(8,128)(2,1)S(1)}, bf16[2,64,2048]{2,1,0:T(8,128)(2,1)S(1)}, u32[]{:S(2)}, u32[]{:S(2)}) collective-permute-start(bf16[2,64,2048]{2,1,0:T(8,128)(2,1)S(1)} %get-tuple-element.323), channel_id=1, source_target_pairs={{0,8},{1,9},{2,10},{3,11},{4,12},{5,13},{6,14},{7,15},{8,0},{9,1},... | collective-permute-start | bytes 1572872 | tf_op jit(solution)/shard_map/ppermute | solution.py:305
  539.8 28.2 %collective-permute-start.32 = (bf16[32,2816]{1,0:T(8,128)(2,1)S(1)}, bf16[32,2816]{1,0:T(8,128)(2,1)S(1)}, u32[]{:S(2)}, u32[]{:S(2)}) collective-permute-start(bf16[32,2816]{1,0:T(8,128)(2,1)S(1)} %fusion.32), channel_id=1, source_target_pairs={{0,16},{1,17},{2,18},{3,19},{4,20},{5,21},{6,22},{7,23},{8,24},{9,... | collective-permute-start | bytes 540680 | tf_op jit(solution)/shard_map/ppermute | solution.py:305
  541.9 28.7 %collective-permute-start.31 = (bf16[64,3072]{1,0:T(8,128)(2,1)S(1)}, bf16[64,3072]{1,0:T(8,128)(2,1)S(1)}, u32[]{:S(2)}, u32[]{:S(2)}) collective-permute-start(bf16[64,3072]{1,0:T(8,128)(2,1)S(1)} %fusion.12), channel_id=1, source_target_pairs={{0,2},{1,3},{2,0},{3,1},{4,6},{5,7},{6,4},{7,5},{8,10},{9,11},{10,... | collective-permute-start | bytes 1179656 | tf_op jit(solution)/shard_map/ppermute | solution.py:305
  543.9 34.7 %collective-permute-start.37 = (bf16[64,4864]{1,0:T(8,128)(2,1)S(1)}, bf16[64,4864]{1,0:T(8,128)(2,1)S(1)}, u32[]{:S(2)}, u32[]{:S(2)}) collective-permute-start(bf16[64,4864]{1,0:T(8,128)(2,1)S(1)} %fusion.10), channel_id=1, source_target_pairs={{0,2},{1,3},{2,0},{3,1},{4,6},{5,7},{6,4},{7,5},{8,10},{9,11},{10,... | collective-permute-start | bytes 1867784 | tf_op jit(solution)/shard_map/ppermute | solution.py:305
  560.3 32.8 %collective-permute-start.36 = (bf16[4,32,4096]{2,1,0:T(8,128)(2,1)}, bf16[4,32,4096]{2,1,0:T(8,128)(2,1)S(1)}, u32[]{:S(2)}, u32[]{:S(2)}) collective-permute-start(bf16[4,32,4096]{2,1,0:T(8,128)(2,1)} %get-tuple-element.311), channel_id=1, source_target_pairs={{0,4},{1,5},{2,6},{3,7},{4,0},{5,1},{6,2},{7,3},{8,12},{9,13},{10,... | collective-permute-start | bytes 3145736 | tf_op jit(solution)/shard_map/ppermute | solution.py:305
  563.9 29.4 %collective-permute-start.41 = (bf16[64,2048]{1,0:T(8,128)(2,1)S(1)}, bf16[64,2048]{1,0:T(8,128)(2,1)}, u32[]{:S(2)}, u32[]{:S(2)}) collective-permute-start(bf16[64,2048]{1,0:T(8,128)(2,1)S(1)} %fusion.26), channel_id=1, source_target_pairs={{0,16},{1,17},{2,18},{3,19},{4,20},{5,21},{6,22},{7,23},{8,24},{9,... | collective-permute-start | bytes 786440 | tf_op jit(solution)/shard_map/ppermute | solution.py:305
  569.0 26.3 %collective-permute-start.40 = (bf16[32,2816]{1,0:T(8,128)(2,1)S(1)}, bf16[32,2816]{1,0:T(8,128)(2,1)}, u32[]{:S(2)}, u32[]{:S(2)}) collective-permute-start(bf16[32,2816]{1,0:T(8,128)(2,1)S(1)} %fusion.25), channel_id=1, source_target_pairs={{0,2},{1,3},{2,0},{3,1},{4,6},{5,7},{6,4},{7,5},{8,10},{9,11},{10,... | collective-permute-start | bytes 540680 | tf_op jit(solution)/shard_map/ppermute | solution.py:305
  570.7 18.5 %collective-permute-start.53 = (bf16[64,3072]{1,0:T(8,128)(2,1)S(1)}, bf16[64,3072]{1,0:T(8,128)(2,1)}, u32[]{:S(2)}, u32[]{:S(2)}) collective-permute-start(bf16[64,3072]{1,0:T(8,128)(2,1)S(1)} %add_convert_fusion.24), channel_id=1, source_target_pairs={{0,1},{1,0},{2,3},{3,2},{4,5},{5,4},{6,7},{7,6},{8,9},{9,8},{10,11... | collective-permute-start | bytes 1179656 | tf_op jit(solution)/shard_map/ppermute | solution.py:305
  578.8 54.9 %all-to-all-start.3 = ((bf16[8,64,1024]{2,1,0:T(8,128)(2,1)}), bf16[8,64,1024]{2,1,0:T(8,128)(2,1)}, u32[]{:S(2)}, u32[]{:S(2)}) async-start(bf16[8,64,1024]{2,1,0:T(8,128)(2,1)} %bitcast.165), calls=%async_computation.3 | async-start | bytes 2097152 | tf_op jit(solution)/shard_map/all_to_all | solution.py:907
  596.3 7.6 %collective-permute-start.42 = (f32[8,4624]{1,0:T(8,128)S(1)}, f32[8,4624]{1,0:T(8,128)S(1)}, u32[]{:S(2)}, u32[]{:S(2)}) collective-permute-start(f32[8,4624]{1,0:T(8,128)S(1)} %add.412), channel_id=1, source_target_pairs={{0,4},{1,5},{2,6},{3,7},{4,0},{5,1},{6,2},{7,3},{8,12},{9,13},{10,... | collective-permute-start | bytes 443912 | tf_op jit(solution)/shard_map/ppermute | solution.py:1140
  599.6 17.8 %collective-permute-start.39 = (bf16[2,32,4096]{2,1,0:T(8,128)(2,1)S(1)}, bf16[2,32,4096]{2,1,0:T(8,128)(2,1)S(1)}, u32[]{:S(2)}, u32[]{:S(2)}) collective-permute-start(bf16[2,32,4096]{2,1,0:T(8,128)(2,1)S(1)} %get-tuple-element.320), channel_id=1, source_target_pairs={{0,8},{1,9},{2,10},{3,11},{4,12},{5,13},{6,14},{7,15},{8,0},{9,1},... | collective-permute-start | bytes 1572872 | tf_op jit(solution)/shard_map/ppermute | solution.py:305
  601.0 17.8 %collective-permute-start.44 = (bf16[64,2048]{1,0:T(8,128)(2,1)S(1)}, bf16[64,2048]{1,0:T(8,128)(2,1)S(1)}, u32[]{:S(2)}, u32[]{:S(2)}) collective-permute-start(bf16[64,2048]{1,0:T(8,128)(2,1)S(1)} %fusion.16), channel_id=1, source_target_pairs={{0,2},{1,3},{2,0},{3,1},{4,6},{5,7},{6,4},{7,5},{8,10},{9,11},{10,... | collective-permute-start | bytes 786440 | tf_op jit(solution)/shard_map/ppermute | solution.py:305
  617.4 14.5 %collective-permute-start.43 = (bf16[32,4096]{1,0:T(8,128)(2,1)S(1)}, bf16[32,4096]{1,0:T(8,128)(2,1)S(1)}, u32[]{:S(2)}, u32[]{:S(2)}) collective-permute-start(bf16[32,4096]{1,0:T(8,128)(2,1)S(1)} %fusion.27), channel_id=1, source_target_pairs={{0,16},{1,17},{2,18},{3,19},{4,20},{5,21},{6,22},{7,23},{8,24},{9,... | collective-permute-start | bytes 786440 | tf_op jit(solution)/shard_map/ppermute | solution.py:305
  620.4 13.2 %collective-permute-start.49 = (bf16[64,2048]{1,0:T(8,128)(2,1)S(1)}, bf16[64,2048]{1,0:T(8,128)(2,1)S(1)}, u32[]{:S(2)}, u32[]{:S(2)}) collective-permute-start(bf16[64,2048]{1,0:T(8,128)(2,1)S(1)} %add_convert_fusion.28), channel_id=1, source_target_pairs={{0,1},{1,0},{2,3},{3,2},{4,5},{5,4},{6,7},{7,6},{8,9},{9,8},{10,11... | collective-permute-start | bytes 786440 | tf_op jit(solution)/shard_map/ppermute | solution.py:305
  632.0 7.3 %collective-permute-start.47 = (bf16[32,4096]{1,0:T(8,128)(2,1)S(1)}, bf16[32,4096]{1,0:T(8,128)(2,1)S(1)}, u32[]{:S(2)}, u32[]{:S(2)}) collective-permute-start(bf16[32,4096]{1,0:T(8,128)(2,1)S(1)} %fusion.15), channel_id=1, source_target_pairs={{0,2},{1,3},{2,0},{3,1},{4,6},{5,7},{6,4},{7,5},{8,10},{9,11},{10,... | collective-permute-start | bytes 786440 | tf_op jit(solution)/shard_map/ppermute | solution.py:305
  639.5 8.5 %collective-permute-start.48 = (f32[8,4624]{1,0:T(8,128)S(1)}, f32[8,4624]{1,0:T(8,128)S(1)}, u32[]{:S(2)}, u32[]{:S(2)}) collective-permute-start(f32[8,4624]{1,0:T(8,128)S(1)} %add.425), channel_id=1, source_target_pairs={{0,16},{1,17},{2,18},{3,19},{4,20},{5,21},{6,22},{7,23},{8,24},{9,... | collective-permute-start | bytes 443912 | tf_op jit(solution)/shard_map/ppermute | solution.py:1140
  (80 other events, 1017.4 us)
Sparse Core Ops, SparseCore 0:
  71.5 183.0 all-gather.1
